TPU v7x, 512 devices: a whole 4x8x8 slice. The times are simulated.
512 devices in a mesh: ctx: 32 (over z_lo, x, core), tp: 16 (over z_hi, y).
Axes of the slice: x: 4, y: 8, z: 8 (z_hi: 2, z_lo: 4; z = z_hi * 4 + z_lo), core: 2. Of those that a mesh axis runs over, the one named last changes fastest.
Arguments:
- queries: bfloat16 [8192, 8192], P('ctx', 'tp'), may hold values from -100 to 100
- key_rows: bfloat16 [8192, 1024], P('ctx'), may hold values from -5 to 5
- value_rows: bfloat16 [8192, 1024], P('ctx'), may hold values from -6 to 6
- documents: int32 [8192], P('ctx'), may hold values from 0 to 3, never falling along the last dimension, each value on 1 to 6144 neighbouring positions
- out_weight: bfloat16 [8192, 8192], P('tp', 'ctx'), may hold values from -0.75 to 0.75
Outputs:
- attention_out: bfloat16 [8192, 8192], P(('ctx', 'tp'))
Inputs may be any that keep to these rules, and one draw needn't show every extreme that they name: `documents`: document numbers never fall along the window; each document holds 1 to 6144 tokens and one holds exactly 6144.
All inputs are finite; a program needn't handle non-finite values.
Results may differ from a plain program's by a relative error of at most 0.015.
Values may be sent and summed in bfloat16 or wider, within the bound.
No kernel may reach another device: no remote copies, remote signals or barrier semaphores. Data moves between devices by JAX's collectives and lax.ppermute only.
A program may use at most 128 MiB of HBM per device.

v0:
```python
import functools
import math

import jax
import jax.numpy as jnp
from jax import lax
from jax.experimental import pallas as pl
from jax.experimental.pallas import tpu as pltpu
from jax.sharding import Mesh, PartitionSpec as P

HEADS = 64
KV_HEADS = 8
HD = 128
ZL, X, CORE, ZH, Y = 4, 4, 2, 2, 8
AXES = ("zl", "x", "core", "zh", "y")
CTX = ("zl", "x", "core")
TP = ("zh", "y")
PAD = 8
NEG = -1e30
SCALE2 = math.log2(math.e) / math.sqrt(HD)


def attend_kernel(heads, sources, first, last, where_ref, q_ref, docs_ref, *refs):
    n = len(sources)
    pieces = refs[: 2 * n]
    refs = refs[2 * n :]
    if not first:
        m_in, acc_in = refs[:2]
        refs = refs[2:]
    if last:
        out_ref, m_ref, acc_ref = refs
    else:
        m_ref, acc_ref = refs
    rows = q_ref.shape[0]
    my_z, my_x, my_core = where_ref[0], where_ref[1], where_ref[2]
    my_block = my_z * X + my_x
    if first:
        m_ref[...] = jnp.full_like(m_ref, NEG)
        acc_ref[...] = jnp.zeros_like(acc_ref)
    else:
        m_ref[...] = m_in[...]
        acc_ref[...] = acc_in[...]
    q_docs = docs_ref[...]
    q_first, q_last = jnp.min(q_docs), jnp.max(q_docs)
    ones = jnp.ones((rows, HD), jnp.bfloat16)

    for at, (offset, z_from, z_count) in enumerate(sources):
        own, other = pieces[2 * at], pieces[2 * at + 1]
        their_x = lax.rem(my_x + offset, X)

        def block(z, carry, own=own, other=other, their_x=their_x, z_from=z_from):
            their_block = (z_from + z) * X + their_x
            docs_own = own[z, rows : rows + PAD, :].astype(jnp.float32)
            docs_other = other[z, rows : rows + PAD, :].astype(jnp.float32)
            k_first = jnp.min(jnp.minimum(docs_own, docs_other))
            k_last = jnp.max(jnp.maximum(docs_own, docs_other))
            needed = (their_block <= my_block) & (k_last >= q_first)
            whole = needed & (their_block < my_block) & (k_first >= q_last)

            def update(masked):
                if masked:
                    row = lax.broadcasted_iota(jnp.int32, (rows, rows), 0)
                    lane = lax.broadcasted_iota(jnp.int32, (rows, rows), 1)
                    q_pos = my_block * (2 * rows) + my_core * rows + row
                    k_pos = their_block * (2 * rows) + lane
                    allowed = []
                    for side, docs in ((my_core, docs_own), (1 - my_core, docs_other)):
                        same = jnp.broadcast_to(docs[:1], (rows, rows)) == jnp.concatenate(
                            [q_docs] * (rows // HD), axis=1
                        )
                        allowed.append(same & (k_pos + side * rows <= q_pos))
                values = [
                    jnp.concatenate([ref[z, :rows, HD:], ones], axis=1) for ref in (own, other)
                ]
                for h in range(heads):
                    q = q_ref[:, h * HD : (h + 1) * HD]
                    scores = [
                        lax.dot_general(
                            q,
                            ref[z, :rows, :HD],
                            (((1,), (1,)), ((), ())),
                            preferred_element_type=jnp.float32,
                        )
                        for ref in (own, other)
                    ]
                    if masked:
                        scores = [jnp.where(a, s, NEG) for a, s in zip(allowed, scores)]
                    old = m_ref[h]
                    top = jnp.max(jnp.maximum(scores[0], scores[1]), axis=1, keepdims=True)
                    new = jnp.maximum(old, top)
                    wide = jnp.concatenate([new] * (rows // HD), axis=1)
                    total = None
                    for side in range(2):
                        weights = jnp.exp2((scores[side] - wide) * SCALE2)
                        if masked:
                            weights = jnp.where(allowed[side], weights, 0.0)
                        term = jnp.dot(
                            weights.astype(jnp.bfloat16),
                            values[side],
                            preferred_element_type=jnp.float32,
                        )
                        total = term if total is None else total + term
                    keep = jnp.exp2((old - new) * SCALE2)
                    m_ref[h] = new
                    acc_ref[h] = acc_ref[h] * jnp.concatenate([keep, keep], axis=1) + total

            @pl.when(whole)
            def _():
                update(False)

            @pl.when(needed & jnp.logical_not(whole))
            def _():
                update(True)

            return carry

        lax.fori_loop(0, z_count, block, 0)

    if last:
        for h in range(heads):
            done = (acc_ref[h, :, :HD] / acc_ref[h, :, HD:]).astype(jnp.bfloat16)
            out_ref[:, h * HD : (h + 1) * HD] = done


def attend(where, q, docs, pieces, sources, state, last):
    rows, width = q.shape
    heads = width // HD
    first = state is None
    states = (
        jax.ShapeDtypeStruct((heads, rows, HD), jnp.float32),
        jax.ShapeDtypeStruct((heads, rows, 2 * HD), jnp.float32),
    )
    vmem = pl.BlockSpec(memory_space=pltpu.VMEM)
    inputs = [q, docs, *pieces] + ([] if first else list(state))
    blocks = sum(s[2] for s in sources)
    return pl.pallas_call(
        functools.partial(attend_kernel, heads, sources, first, last),
        out_shape=jax.ShapeDtypeStruct((rows, width), jnp.bfloat16) if last else states,
        in_specs=[pl.BlockSpec(memory_space=pltpu.SMEM)] + [vmem] * len(inputs),
        out_specs=vmem if last else (vmem, vmem),
        scratch_shapes=[pltpu.VMEM(s.shape, s.dtype) for s in states] if last else [],
        compiler_params=pltpu.CompilerParams(vmem_limit_bytes=40 << 20),
        cost_estimate=pl.CostEstimate(
            flops=blocks * heads * rows * 2 * rows * HD * 6,
            bytes_accessed=blocks * rows * HD * 8,
            transcendentals=blocks * heads * rows * 2 * rows,
        ),
    )(where, *inputs)


def around(value, axis, size, step):
    return lax.ppermute(value, axis, [(i, (i + step) % size) for i in range(size)])


def ring_over_y(attended):
    half = attended.shape[0] // 2
    pieces = [(0, attended)]
    left = right = attended
    for step in range(1, Y // 2):
        left = around(left, "y", Y, 1)
        right = around(right, "y", Y, -1)
        pieces += [(-step, left), (step, right)]
    far = (around(left[:half], "y", Y, 1), around(right[half:], "y", Y, -1))
    return pieces + [(Y // 2, far)]


def project_kernel(offsets, y_ref, *refs):
    pieces, (weight_ref, out_ref, held_ref, acc_ref, sems) = refs[: Y + 1], refs[Y + 1 :]
    half = acc_ref.shape[1] // 2
    width = acc_ref.shape[2]
    part = out_ref.shape[1]

    def copy(at, z):
        their_y = lax.rem(y_ref[0] + (offsets[at] + Y), Y)
        return pltpu.make_async_copy(
            weight_ref.at[z, their_y], held_ref.at[at, z], sems.at[at, z]
        )

    for at in range(Y):
        for z in range(ZL):
            copy(at, z).start()
    for at in range(Y):
        for z in range(ZL):
            copy(at, z).wait()
            if at < Y - 1:
                term = jnp.dot(
                    pieces[at][...], held_ref[at, z], preferred_element_type=jnp.float32
                )
                acc_ref[z] = term if at == 0 else acc_ref[z] + term
                continue
            for side in range(2):
                rows = slice(side * half, (side + 1) * half)
                term = jnp.dot(
                    pieces[at + side][...], held_ref[at, z], preferred_element_type=jnp.float32
                )
                done = (acc_ref[z, rows] + term).astype(jnp.bfloat16)
                out_ref[
                    side * half // part : (side + 1) * half // part,
                    :,
                    z * width : (z + 1) * width,
                ] = done.reshape(half // part, part, width)


def project(y, pieces, weight):
    rows, depth = pieces[0][1].shape
    width = weight.shape[2]
    weight = weight.reshape(ZL, X * CORE, depth, width)
    offsets = tuple(offset for offset, _ in pieces)
    blocks = [block for _, block in pieces[:-1]] + list(pieces[-1][1])
    whole = pl.BlockSpec(memory_space=pltpu.VMEM)
    out = (ZH * Y, rows // (ZH * Y), ZL * width)
    return pl.pallas_call(
        functools.partial(project_kernel, offsets),
        out_shape=jax.ShapeDtypeStruct(out, jnp.bfloat16),
        in_specs=[pl.BlockSpec(memory_space=pltpu.SMEM)]
        + [whole] * len(blocks)
        + [pl.BlockSpec(memory_space=pltpu.HBM)],
        out_specs=whole,
        scratch_shapes=[
            pltpu.VMEM((Y, ZL, depth, width), jnp.bfloat16),
            pltpu.VMEM((ZL, rows, width), jnp.float32),
            pltpu.SemaphoreType.DMA((Y, ZL)),
        ],
        compiler_params=pltpu.CompilerParams(vmem_limit_bytes=24 << 20),
        cost_estimate=pl.CostEstimate(
            flops=2 * Y * rows * depth * ZL * width,
            bytes_accessed=2 * (Y * depth * ZL * width + Y * rows * depth),
            transcendentals=0,
        ),
    )(y, *blocks, weight)


def collect_kernel(came_ref, out_ref):
    width = came_ref.shape[2] // ZL
    for y in range(Y):
        for z in range(ZL):
            columns = slice(z * width, (z + 1) * width)
            both = came_ref[y, :, columns].astype(jnp.float32) + came_ref[
                Y + y, :, columns
            ].astype(jnp.float32)
            block = z * X * CORE + y
            out_ref[:, block * width : (block + 1) * width] = both.astype(jnp.bfloat16)


def collect(came):
    vmem = pl.BlockSpec(memory_space=pltpu.VMEM)
    return pl.pallas_call(
        collect_kernel,
        out_shape=jax.ShapeDtypeStruct((came.shape[1], Y * came.shape[2]), jnp.bfloat16),
        in_specs=[vmem],
        out_specs=vmem,
    )(came)


def compute(queries, key_rows, value_rows, documents, out_weight):
    rows = queries.shape[0]
    heads_here = queries.shape[1] // HD
    swap = [(a * Y + b, b * Y + a) for a in range(X * CORE) for b in range(Y)]
    swapped = lax.ppermute(out_weight, ("x", "core", "y"), swap)
    weight = lax.all_gather(swapped, CTX, axis=0)

    kv = lax.axis_index(TP) * heads_here // (HEADS // KV_HEADS)
    own_keys = lax.dynamic_slice_in_dim(key_rows, kv * HD, HD, 1)
    own_values = lax.dynamic_slice_in_dim(value_rows, kv * HD, HD, 1)
    doc_rows = jnp.broadcast_to(documents.astype(jnp.bfloat16)[None, :], (PAD, rows))
    packed = jnp.concatenate(
        [jnp.concatenate([own_keys, own_values], axis=1), doc_rows], axis=0
    )
    where = jnp.stack([lax.axis_index(a) for a in CTX]).astype(jnp.int32)
    docs = jnp.broadcast_to(documents.astype(jnp.float32)[:, None], (rows, HD))

    mine = lax.all_gather(packed, "zl", axis=0)
    left = around(mine, "x", X, 1)
    right = around(mine, "x", X, -1)
    mine_other = around(mine, "core", CORE, 1)
    far_a = around(left[: ZL // 2], "x", X, 1)
    far_b = around(right[ZL // 2 :], "x", X, -1)
    left_other = around(left, "core", CORE, 1)
    right_other = around(right, "core", CORE, 1)
    far = jnp.concatenate([far_a, far_b], axis=0)
    far_other = around(far, "core", CORE, 1)

    state = attend(where, queries, docs, [mine, mine_other], [(0, 0, ZL)], None, False)
    state = attend(
        where,
        queries,
        docs,
        [left, left_other, right, right_other],
        [(X - 1, 0, ZL), (1, 0, ZL)],
        state,
        False,
    )
    attended = attend(where, queries, docs, [far, far_other], [(2, 0, ZL)], state, True)
    pieces = ring_over_y(attended)
    y = lax.axis_index("y").astype(jnp.int32).reshape(1)
    terms = project(y, pieces, weight)
    came = lax.all_to_all(terms, TP, split_axis=0, concat_axis=0, tiled=True)
    return collect(came)


def solution(mesh):
    fine = Mesh(mesh.devices.reshape(ZL, X, CORE, ZH, Y), AXES)
    in_specs = (P(CTX, TP), P(CTX, None), P(CTX, None), P(CTX), P(TP, CTX))
    return jax.shard_map(
        compute, mesh=fine, in_specs=in_specs, out_specs=P(CTX + TP, None), check_vma=False
    )
```

profile of v0, /device:TPU:200, one launch (start us, length us, event | category | flops | bytes accessed | tf_op | source)
XLA Modules:
  0.0 214.6 jit_solution(3009235141735393108)
XLA Ops:
  8.5 6.0 %collective-permute-done.16 = bf16[512,256]{1,0:T(8,128)(2,1)S(1)} collective-permute-done((bf16[512,256]{1,0:T(8,128)(2,1)}, bf16[512,256]{1,0:T(8,128)(2,1)S(1)}, u32[]{:S(2)}, u32[]{:S(2)}) %collective-permute-start.16) | collective-permute-done | bytes 262176 | tf_op jit(solution)/shard_map/ppermute | solution.py:259
  16.9 15.0 %all-gather = bf16[1056,256]{1,0:T(8,128)(2,1)S(1)} all-gather(bf16[264,256]{1,0:T(8,128)(2,1)S(1)} %pad_maximum_fusion), channel_id=2, replica_groups=mesh['zl'=4,'x'=4,'core'=2,'zh'=2,'y'=8] {'zl'}, dimensions={0}, use_global_device_ids=true | all-gather | bytes 675840 | tf_op jit(solution)/shard_map/all_gather | solution.py:272
  31.9 18.6 %collective-permute-start = (bf16[4,264,256]{2,1,0:T(8,128)(2,1)S(1)}, bf16[4,264,256]{2,1,0:T(8,128)(2,1)S(1)}, u32[]{:S(2)}, u32[]{:S(2)}) collective-permute-start(bf16[4,264,256]{2,1,0:T(8,128)(2,1)S(1)} %bitcast.7), channel_id=1, source_target_pairs={{0,32},{32,64},{64,96},{96,0},{1,33},{33,65},{65,97},{97,1},{2,34}... | collective-permute-start | bytes 1622024 | tf_op jit(solution)/shard_map/ppermute | solution.py:152
  52.4 20.4 %collective-permute-done.refs_0_ = bf16[4,264,256]{2,1,0:T(8,128)(2,1)S(1)} collective-permute-done((bf16[4,264,256]{2,1,0:T(8,128)(2,1)S(1)}, bf16[4,264,256]{2,1,0:T(8,128)(2,1)S(1)}, u32[]{:S(2)}, u32[]{:S(2)}) %collective-permute-start) | collective-permute-done | bytes 540704 | tf_op jit(solution)/shard_map/ppermute | solution.py:152
  73.5 4.4 %collective-permute-start.1 = (bf16[2,264,256]{2,1,0:T(8,128)(2,1)}, bf16[2,264,256]{2,1,0:T(8,128)(2,1)S(1)}, u32[]{:S(2)}, u32[]{:S(2)}) collective-permute-start(bf16[2,264,256]{2,1,0:T(8,128)(2,1)} %slice.16), channel_id=1, source_target_pairs={{0,32},{32,64},{64,96},{96,0},{1,33},{33,65},{65,97},{97,1},{2,34}... | collective-permute-start | bytes 811016 | tf_op jit(solution)/shard_map/ppermute | solution.py:152
  80.6 4.8 %collective-permute-start.3 = (bf16[2,264,256]{2,1,0:T(8,128)(2,1)}, bf16[2,264,256]{2,1,0:T(8,128)(2,1)}, u32[]{:S(2)}, u32[]{:S(2)}) collective-permute-start(bf16[2,264,256]{2,1,0:T(8,128)(2,1)} %slice.17), channel_id=1, source_target_pairs={{0,96},{32,0},{64,32},{96,64},{1,97},{33,1},{65,33},{97,65},{2,98}... | collective-permute-start | bytes 811016 | tf_op jit(solution)/shard_map/ppermute | solution.py:152
  87.3 2.4 %collective-permute-start.6 = (bf16[4,264,256]{2,1,0:T(8,128)(2,1)S(1)}, bf16[4,264,256]{2,1,0:T(8,128)(2,1)S(1)}, u32[]{:S(2)}, u32[]{:S(2)}) collective-permute-start(bf16[4,264,256]{2,1,0:T(8,128)(2,1)S(1)} %collective-permute-done.2.refs_2_), channel_id=1, source_target_pairs={{0,16},{16,0},{1,17},{17,1},{2,18},{18,2},{3,19},{19,3},{4,20},{20... | collective-permute-start | bytes 1622024 | tf_op jit(solution)/shard_map/ppermute | solution.py:152
  89.7 7.7 %collective-permute-done.3 = bf16[2,264,256]{2,1,0:T(8,128)(2,1)} collective-permute-done((bf16[2,264,256]{2,1,0:T(8,128)(2,1)}, bf16[2,264,256]{2,1,0:T(8,128)(2,1)}, u32[]{:S(2)}, u32[]{:S(2)}) %collective-permute-start.3) | collective-permute-done | bytes 270368 | tf_op jit(solution)/shard_map/ppermute | solution.py:152
  101.5 5.7 %shard_map.55 = (f32[4,256,128]{2,1,0:T(8,128)S(1)}, f32[4,256,256]{2,1,0:T(8,128)S(1)}) custom-call(s32[3]{0:T(128)S(1)} %pad_add_fusion.where_ref, bf16[256,512]{1,0:T(8,128)(2,1)S(1)} %copy-done.1, f32[256,128]{1,0:T(8,128)S(1)} %broadcast_in_dim.4.docs_ref, bf16[4,264,256]{2,1,0:T(8,128)(2,1)S(1)} %bitcast.10, ...), custom_call_target="tpu_custom_call" | custom-call | flops 1610612736 | bytes 1048576 | tf_op jit(solution)/shard_map/pallas_call | solution.py:136
  107.2 8.0 %shard_map.56 = (f32[4,256,128]{2,1,0:T(8,128)S(1)}, f32[4,256,256]{2,1,0:T(8,128)S(1)}) custom-call(s32[3]{0:T(128)S(1)} %pad_add_fusion.where_ref, bf16[256,512]{1,0:T(8,128)(2,1)S(1)} %copy-done.1, f32[256,128]{1,0:T(8,128)S(1)} %broadcast_in_dim.4.docs_ref, bf16[4,264,256]{2,1,0:T(8,128)(2,1)S(1)} %collective-permute-done.refs_0_, ...), custom_call_target="tpu_custom_call" | custom-call | flops 3221225472 | bytes 2097152 | tf_op jit(solution)/shard_map/pallas_call | solution.py:136
  115.3 4.3 %shard_map.57.refs_0_ = bf16[256,512]{1,0:T(8,128)(2,1)S(1)} custom-call(s32[3]{0:T(128)S(1)} %pad_add_fusion.where_ref, bf16[256,512]{1,0:T(8,128)(2,1)S(1)} %copy-done.1, f32[256,128]{1,0:T(8,128)S(1)} %broadcast_in_dim.4.docs_ref, bf16[4,264,256]{2,1,0:T(8,128)(2,1)S(1)} %constant_dynamic-update-slice_fusion.refs_0_, ...), custom_call_target="tpu_custom_call" | custom-call | flops 1610612736 | bytes 1048576 | tf_op jit(solution)/shard_map/pallas_call | solution.py:136
  119.6 2.5 %collective-permute-start.8 = (bf16[256,512]{1,0:T(8,128)(2,1)S(1)}, bf16[256,512]{1,0:T(8,128)(2,1)S(1)}, u32[]{:S(2)}, u32[]{:S(2)}) collective-permute-start(bf16[256,512]{1,0:T(8,128)(2,1)S(1)} %shard_map.57.refs_0_), channel_id=1, source_target_pairs={{0,1},{1,2},{2,3},{3,4},{4,5},{5,6},{6,7},{7,0},{8,9},{9,10},{10,1... | collective-permute-start | bytes 786440 | tf_op jit(solution)/shard_map/ppermute | solution.py:152
  122.1 3.6 %collective-permute-start.9 = (bf16[256,512]{1,0:T(8,128)(2,1)S(1)}, bf16[256,512]{1,0:T(8,128)(2,1)S(1)}, u32[]{:S(2)}, u32[]{:S(2)}) collective-permute-start(bf16[256,512]{1,0:T(8,128)(2,1)S(1)} %shard_map.57.refs_0_), channel_id=1, source_target_pairs={{0,7},{1,0},{2,1},{3,2},{4,3},{5,4},{6,5},{7,6},{8,15},{9,8},{10,9... | collective-permute-start | bytes 786440 | tf_op jit(solution)/shard_map/ppermute | solution.py:152
  125.7 3.6 %collective-permute-done.8.refs_1_ = bf16[256,512]{1,0:T(8,128)(2,1)S(1)} collective-permute-done((bf16[256,512]{1,0:T(8,128)(2,1)S(1)}, bf16[256,512]{1,0:T(8,128)(2,1)S(1)}, u32[]{:S(2)}, u32[]{:S(2)}) %collective-permute-start.8) | collective-permute-done | bytes 262176 | tf_op jit(solution)/shard_map/ppermute | solution.py:152
  129.3 2.5 %collective-permute-start.10 = (bf16[256,512]{1,0:T(8,128)(2,1)S(1)}, bf16[256,512]{1,0:T(8,128)(2,1)S(1)}, u32[]{:S(2)}, u32[]{:S(2)}) collective-permute-start(bf16[256,512]{1,0:T(8,128)(2,1)S(1)} %collective-permute-done.8.refs_1_), channel_id=1, source_target_pairs={{0,1},{1,2},{2,3},{3,4},{4,5},{5,6},{6,7},{7,0},{8,9},{9,10},{10,1... | collective-permute-start | bytes 786440 | tf_op jit(solution)/shard_map/ppermute | solution.py:152
  132.3 4.4 %collective-permute-start.11 = (bf16[256,512]{1,0:T(8,128)(2,1)S(1)}, bf16[256,512]{1,0:T(8,128)(2,1)S(1)}, u32[]{:S(2)}, u32[]{:S(2)}) collective-permute-start(bf16[256,512]{1,0:T(8,128)(2,1)S(1)} %collective-permute-done.9.refs_2_), channel_id=1, source_target_pairs={{0,7},{1,0},{2,1},{3,2},{4,3},{5,4},{6,5},{7,6},{8,15},{9,8},{10,9... | collective-permute-start | bytes 786440 | tf_op jit(solution)/shard_map/ppermute | solution.py:152
  136.7 4.4 %collective-permute-done.10.refs_3_ = bf16[256,512]{1,0:T(8,128)(2,1)S(1)} collective-permute-done((bf16[256,512]{1,0:T(8,128)(2,1)S(1)}, bf16[256,512]{1,0:T(8,128)(2,1)S(1)}, u32[]{:S(2)}, u32[]{:S(2)}) %collective-permute-start.10) | collective-permute-done | bytes 262176 | tf_op jit(solution)/shard_map/ppermute | solution.py:152
  143.6 4.9 %collective-permute-start.13 = (bf16[256,512]{1,0:T(8,128)(2,1)S(1)}, bf16[256,512]{1,0:T(8,128)(2,1)S(1)}, u32[]{:S(2)}, u32[]{:S(2)}) collective-permute-start(bf16[256,512]{1,0:T(8,128)(2,1)S(1)} %collective-permute-done.11.refs_4_), channel_id=1, source_target_pairs={{0,7},{1,0},{2,1},{3,2},{4,3},{5,4},{6,5},{7,6},{8,15},{9,8},{10,9... | collective-permute-start | bytes 786440 | tf_op jit(solution)/shard_map/ppermute | solution.py:152
  148.6 4.8 %collective-permute-done.12.refs_5_ = bf16[256,512]{1,0:T(8,128)(2,1)S(1)} collective-permute-done((bf16[256,512]{1,0:T(8,128)(2,1)S(1)}, bf16[256,512]{1,0:T(8,128)(2,1)S(1)}, u32[]{:S(2)}, u32[]{:S(2)}) %collective-permute-start.12) | collective-permute-done | bytes 262176 | tf_op jit(solution)/shard_map/ppermute | solution.py:152
  156.4 3.9 %collective-permute-start.15 = (bf16[128,512]{1,0:T(8,128)(2,1)S(1)}, bf16[128,512]{1,0:T(8,128)(2,1)S(1)}, u32[]{:S(2)}, u32[]{:S(2)}) collective-permute-start(bf16[128,512]{1,0:T(8,128)(2,1)S(1)} %slice.19), channel_id=1, source_target_pairs={{0,7},{1,0},{2,1},{3,2},{4,3},{5,4},{6,5},{7,6},{8,15},{9,8},{10,9... | collective-permute-start | bytes 393224 | tf_op jit(solution)/shard_map/ppermute | solution.py:152
  161.3 3.3 %collective-permute-done.15.refs_8_ = bf16[128,512]{1,0:T(8,128)(2,1)S(1)} collective-permute-done((bf16[128,512]{1,0:T(8,128)(2,1)S(1)}, bf16[128,512]{1,0:T(8,128)(2,1)S(1)}, u32[]{:S(2)}, u32[]{:S(2)}) %collective-permute-start.15) | collective-permute-done | bytes 131104 | tf_op jit(solution)/shard_map/ppermute | solution.py:152
  164.6 3.4 %copy-done = bf16[16384,256]{1,0:T(8,128)(2,1)S(1)} copy-done((bf16[16384,256]{1,0:T(8,128)(2,1)S(1)}, bf16[16384,256]{1,0:T(8,128)(2,1)}, u32[]{:S(2)}) %copy-start) | copy-done | bytes 8388632
  168.0 7.0 %shard_map.58 = bf16[16,16,1024]{2,1,0:T(8,128)(2,1)S(1)} custom-call(s32[1]{0:T(128)} %bitcast.y_ref, bf16[256,512]{1,0:T(8,128)(2,1)S(1)} %shard_map.57.refs_0_, bf16[256,512]{1,0:T(8,128)(2,1)S(1)} %collective-permute-done.8.refs_1_, bf16[256,512]{1,0:T(8,128)(2,1)S(1)} %collective-permute-done.9.refs_2_, ...), custom_call_target="tpu_custom_call" | custom-call | flops 2147483648 | bytes 10485760 | tf_op jit(solution)/shard_map/pallas_call | solution.py:212
  175.0 31.0 %all_to_all.5.came_ref = bf16[16,16,1024]{2,1,0:T(8,128)(2,1)} all-to-all(bf16[16,16,1024]{2,1,0:T(8,128)(2,1)S(1)} %shard_map.58), channel_id=1, replica_groups=mesh['zl'=4,'x'=4,'core'=2,'zh'=2,'y'=8] {'zh','y'}, dimensions={0} | all-to-all | bytes 1048576 | tf_op jit(solution)/shard_map/all_to_all | solution.py:297
  (38 shorter events, 24.4 us)
Async XLA Ops:
  6.5 158.1 %all-gather.4.cloned.1.call-start = ((), (), s32[]{:S(2)}) async-start(), calls=%async_computation.1 | async-start | bytes 8650752 | tf_op jit(solution)/shard_map/all_gather | solution.py:260
  6.5 7.9 %collective-permute-start.16 = (bf16[512,256]{1,0:T(8,128)(2,1)}, bf16[512,256]{1,0:T(8,128)(2,1)S(1)}, u32[]{:S(2)}, u32[]{:S(2)}) collective-permute-start(bf16[512,256]{1,0:T(8,128)(2,1)} %param.9), channel_id=1, source_target_pairs={{0,0},{1,16},{2,32},{3,48},{4,64},{5,80},{6,96},{7,112},{16,1},{17... | collective-permute-start | bytes 786440 | tf_op jit(solution)/shard_map/ppermute | solution.py:259
  14.4 0.7 copy-start.2
  31.9 40.9 %collective-permute-start = (bf16[4,264,256]{2,1,0:T(8,128)(2,1)S(1)}, bf16[4,264,256]{2,1,0:T(8,128)(2,1)S(1)}, u32[]{:S(2)}, u32[]{:S(2)}) collective-permute-start(bf16[4,264,256]{2,1,0:T(8,128)(2,1)S(1)} %bitcast.7), channel_id=1, source_target_pairs={{0,32},{32,64},{64,96},{96,0},{1,33},{33,65},{65,97},{97,1},{2,34}... | collective-permute-start | bytes 1622024 | tf_op jit(solution)/shard_map/ppermute | solution.py:152
  50.4 29.4 %collective-permute-start.2 = (bf16[4,264,256]{2,1,0:T(8,128)(2,1)S(1)}, bf16[4,264,256]{2,1,0:T(8,128)(2,1)S(1)}, u32[]{:S(2)}, u32[]{:S(2)}) collective-permute-start(bf16[4,264,256]{2,1,0:T(8,128)(2,1)S(1)} %bitcast.8), channel_id=1, source_target_pairs={{0,96},{32,0},{64,32},{96,64},{1,97},{33,1},{65,33},{97,65},{2,98}... | collective-permute-start | bytes 1622024 | tf_op jit(solution)/shard_map/ppermute | solution.py:152
  73.5 16.2 %collective-permute-start.1 = (bf16[2,264,256]{2,1,0:T(8,128)(2,1)}, bf16[2,264,256]{2,1,0:T(8,128)(2,1)S(1)}, u32[]{:S(2)}, u32[]{:S(2)}) collective-permute-start(bf16[2,264,256]{2,1,0:T(8,128)(2,1)} %slice.16), channel_id=1, source_target_pairs={{0,32},{32,64},{64,96},{96,0},{1,33},{33,65},{65,97},{97,1},{2,34}... | collective-permute-start | bytes 811016 | tf_op jit(solution)/shard_map/ppermute | solution.py:152
  77.9 22.6 %collective-permute-start.7 = (bf16[4,264,256]{2,1,0:T(8,128)(2,1)S(1)}, bf16[4,264,256]{2,1,0:T(8,128)(2,1)S(1)}, u32[]{:S(2)}, u32[]{:S(2)}) collective-permute-start(bf16[4,264,256]{2,1,0:T(8,128)(2,1)S(1)} %bitcast.9), channel_id=1, source_target_pairs={{0,16},{16,0},{1,17},{17,1},{2,18},{18,2},{3,19},{19,3},{4,20},{20... | collective-permute-start | bytes 1622024 | tf_op jit(solution)/shard_map/ppermute | solution.py:152
  80.6 16.9 %collective-permute-start.3 = (bf16[2,264,256]{2,1,0:T(8,128)(2,1)}, bf16[2,264,256]{2,1,0:T(8,128)(2,1)}, u32[]{:S(2)}, u32[]{:S(2)}) collective-permute-start(bf16[2,264,256]{2,1,0:T(8,128)(2,1)} %slice.17), channel_id=1, source_target_pairs={{0,96},{32,0},{64,32},{96,64},{1,97},{33,1},{65,33},{97,65},{2,98}... | collective-permute-start | bytes 811016 | tf_op jit(solution)/shard_map/ppermute | solution.py:152
  85.3 21.9 %collective-permute-start.5 = (bf16[4,264,256]{2,1,0:T(8,128)(2,1)S(1)}, bf16[4,264,256]{2,1,0:T(8,128)(2,1)S(1)}, u32[]{:S(2)}, u32[]{:S(2)}) collective-permute-start(bf16[4,264,256]{2,1,0:T(8,128)(2,1)S(1)} %collective-permute-done.refs_0_), channel_id=1, source_target_pairs={{0,16},{16,0},{1,17},{17,1},{2,18},{18,2},{3,19},{19,3},{4,20},{20... | collective-permute-start | bytes 1622024 | tf_op jit(solution)/shard_map/ppermute | solution.py:152
  87.3 20.0 %collective-permute-start.6 = (bf16[4,264,256]{2,1,0:T(8,128)(2,1)S(1)}, bf16[4,264,256]{2,1,0:T(8,128)(2,1)S(1)}, u32[]{:S(2)}, u32[]{:S(2)}) collective-permute-start(bf16[4,264,256]{2,1,0:T(8,128)(2,1)S(1)} %collective-permute-done.2.refs_2_), channel_id=1, source_target_pairs={{0,16},{16,0},{1,17},{17,1},{2,18},{18,2},{3,19},{19,3},{4,20},{20... | collective-permute-start | bytes 1622024 | tf_op jit(solution)/shard_map/ppermute | solution.py:152
  98.4 16.8 %collective-permute-start.4 = (bf16[4,264,256]{2,1,0:T(8,128)(2,1)S(1)}, bf16[4,264,256]{2,1,0:T(8,128)(2,1)S(1)}, u32[]{:S(2)}, u32[]{:S(2)}) collective-permute-start(bf16[4,264,256]{2,1,0:T(8,128)(2,1)S(1)} %constant_dynamic-update-slice_fusion.refs_0_), channel_id=1, source_target_pairs={{0,16},{16,0},{1,17},{17,1},{2,18},{18,2},{3,19},{19,3},{4,20},{20... | collective-permute-start | bytes 1622024 | tf_op jit(solution)/shard_map/ppermute | solution.py:152
  100.5 1.0 copy-start.1
  119.6 9.7 %collective-permute-start.8 = (bf16[256,512]{1,0:T(8,128)(2,1)S(1)}, bf16[256,512]{1,0:T(8,128)(2,1)S(1)}, u32[]{:S(2)}, u32[]{:S(2)}) collective-permute-start(bf16[256,512]{1,0:T(8,128)(2,1)S(1)} %shard_map.57.refs_0_), channel_id=1, source_target_pairs={{0,1},{1,2},{2,3},{3,4},{4,5},{5,6},{6,7},{7,0},{8,9},{9,10},{10,1... | collective-permute-start | bytes 786440 | tf_op jit(solution)/shard_map/ppermute | solution.py:152
  122.1 10.2 %collective-permute-start.9 = (bf16[256,512]{1,0:T(8,128)(2,1)S(1)}, bf16[256,512]{1,0:T(8,128)(2,1)S(1)}, u32[]{:S(2)}, u32[]{:S(2)}) collective-permute-start(bf16[256,512]{1,0:T(8,128)(2,1)S(1)} %shard_map.57.refs_0_), channel_id=1, source_target_pairs={{0,7},{1,0},{2,1},{3,2},{4,3},{5,4},{6,5},{7,6},{8,15},{9,8},{10,9... | collective-permute-start | bytes 786440 | tf_op jit(solution)/shard_map/ppermute | solution.py:152
  129.3 11.9 %collective-permute-start.10 = (bf16[256,512]{1,0:T(8,128)(2,1)S(1)}, bf16[256,512]{1,0:T(8,128)(2,1)S(1)}, u32[]{:S(2)}, u32[]{:S(2)}) collective-permute-start(bf16[256,512]{1,0:T(8,128)(2,1)S(1)} %collective-permute-done.8.refs_1_), channel_id=1, source_target_pairs={{0,1},{1,2},{2,3},{3,4},{4,5},{5,6},{6,7},{7,0},{8,9},{9,10},{10,1... | collective-permute-start | bytes 786440 | tf_op jit(solution)/shard_map/ppermute | solution.py:152
  132.3 11.3 %collective-permute-start.11 = (bf16[256,512]{1,0:T(8,128)(2,1)S(1)}, bf16[256,512]{1,0:T(8,128)(2,1)S(1)}, u32[]{:S(2)}, u32[]{:S(2)}) collective-permute-start(bf16[256,512]{1,0:T(8,128)(2,1)S(1)} %collective-permute-done.9.refs_2_), channel_id=1, source_target_pairs={{0,7},{1,0},{2,1},{3,2},{4,3},{5,4},{6,5},{7,6},{8,15},{9,8},{10,9... | collective-permute-start | bytes 786440 | tf_op jit(solution)/shard_map/ppermute | solution.py:152
  141.1 12.2 %collective-permute-start.12 = (bf16[256,512]{1,0:T(8,128)(2,1)S(1)}, bf16[256,512]{1,0:T(8,128)(2,1)S(1)}, u32[]{:S(2)}, u32[]{:S(2)}) collective-permute-start(bf16[256,512]{1,0:T(8,128)(2,1)S(1)} %collective-permute-done.10.refs_3_), channel_id=1, source_target_pairs={{0,1},{1,2},{2,3},{3,4},{4,5},{5,6},{6,7},{7,0},{8,9},{9,10},{10,1... | collective-permute-start | bytes 786440 | tf_op jit(solution)/shard_map/ppermute | solution.py:152
  143.6 12.8 %collective-permute-start.13 = (bf16[256,512]{1,0:T(8,128)(2,1)S(1)}, bf16[256,512]{1,0:T(8,128)(2,1)S(1)}, u32[]{:S(2)}, u32[]{:S(2)}) collective-permute-start(bf16[256,512]{1,0:T(8,128)(2,1)S(1)} %collective-permute-done.11.refs_4_), channel_id=1, source_target_pairs={{0,7},{1,0},{2,1},{3,2},{4,3},{5,4},{6,5},{7,6},{8,15},{9,8},{10,9... | collective-permute-start | bytes 786440 | tf_op jit(solution)/shard_map/ppermute | solution.py:152
  153.3 8.0 %collective-permute-start.14 = (bf16[128,512]{1,0:T(8,128)(2,1)S(1)}, bf16[128,512]{1,0:T(8,128)(2,1)S(1)}, u32[]{:S(2)}, u32[]{:S(2)}) collective-permute-start(bf16[128,512]{1,0:T(8,128)(2,1)S(1)} %slice.18), channel_id=1, source_target_pairs={{0,1},{1,2},{2,3},{3,4},{4,5},{5,6},{6,7},{7,0},{8,9},{9,10},{10,1... | collective-permute-start | bytes 393224 | tf_op jit(solution)/shard_map/ppermute | solution.py:152
  156.4 8.2 %collective-permute-start.15 = (bf16[128,512]{1,0:T(8,128)(2,1)S(1)}, bf16[128,512]{1,0:T(8,128)(2,1)S(1)}, u32[]{:S(2)}, u32[]{:S(2)}) collective-permute-start(bf16[128,512]{1,0:T(8,128)(2,1)S(1)} %slice.19), channel_id=1, source_target_pairs={{0,7},{1,0},{2,1},{3,2},{4,3},{5,4},{6,5},{7,6},{8,15},{9,8},{10,9... | collective-permute-start | bytes 393224 | tf_op jit(solution)/shard_map/ppermute | solution.py:152
  164.6 3.4 %copy-start = (bf16[16384,256]{1,0:T(8,128)(2,1)S(1)}, bf16[16384,256]{1,0:T(8,128)(2,1)}, u32[]{:S(2)}) copy-start(bf16[16384,256]{1,0:T(8,128)(2,1)} %all-gather.4.cloned.1.call-done) | copy-start | bytes 25165828
Sparse Core Ops, SparseCore 0:
  15.3 100.5 all-gather.3
where the time goes:
time: 215 us
  starting transfers between devices  65.4 us (30%)
  waiting for transfers between devices  53.3 us (25%)
  blocking collectives  46 us (21%)
  Pallas kernels  26.8 us (12%)
  between operations  13.7 us (6%)
  local copies, waits for them, and re-layouts  8.5 us (4%)
    ppermute x16, starting transfers between devices, around(): lax.ppermute(value, axis, [(i, (i + step) % size) for i in range(size)])  63.5 us
    ppermute x16, waiting for transfers between devices, around(): lax.ppermute(value, axis, [(i, (i + step) % size) for i in range(size)])  47.4 us
    all_to_all x1, blocking collectives, compute(): came = lax.all_to_all(terms, TP, split_axis=0, concat_axis=0, tiled=True)  31 us
    pallas_call x3, Pallas kernels, attend(): pl.pallas_call(functools.partial(attend_kernel, heads, sources, first, la...  18.1 us
    all_gather x1, blocking collectives, compute(): mine = lax.all_gather(packed, 'zl', axis=0)  15 us
    pallas_call x1, Pallas kernels, project(): pl.pallas_call(functools.partial(project_kernel, offsets), out_shape=jax....  6.97 us
    ppermute x1, waiting for transfers between devices, compute(): swapped = lax.ppermute(out_weight, ('x', 'core', 'y'), swap)  5.97 us
    unnamed x7, local copies, waits for them, and re-layouts  5.05 us
  transfers between devices with their start and end apart: 18, of which 11 were waited for; matrix products, arithmetic and copies ran while one was open for 2% of the time, Pallas kernels for 8%

commit v1 on v0

--- a/solution.py
+++ b/solution.py
@@ -16,11 +16,12 @@
 CTX = ("zl", "x", "core")
 TP = ("zh", "y")
 PAD = 8
+GROUP = 1
 NEG = -1e30
 SCALE2 = math.log2(math.e) / math.sqrt(HD)
 
 
-def attend_kernel(heads, sources, first, last, where_ref, q_ref, docs_ref, *refs):
+def attend_kernel(group, sources, first, last, where_ref, q_ref, docs_ref, *refs):
     n = len(sources)
     pieces = refs[: 2 * n]
     refs = refs[2 * n :]
@@ -28,10 +29,11 @@
         m_in, acc_in = refs[:2]
         refs = refs[2:]
     if last:
-        out_ref, m_ref, acc_ref = refs
+        out_ref, m_ref, acc_ref, stack_ref = refs
     else:
-        m_ref, acc_ref = refs
+        m_ref, acc_ref, stack_ref = refs
     rows = q_ref.shape[0]
+    heads = q_ref.shape[1] // HD
     my_z, my_x, my_core = where_ref[0], where_ref[1], where_ref[2]
     my_block = my_z * X + my_x
     if first:
@@ -40,16 +42,19 @@
     else:
         m_ref[...] = m_in[...]
         acc_ref[...] = acc_in[...]
+    for h in range(heads):
+        stack_ref[h * rows : (h + 1) * rows, :] = q_ref[:, h * HD : (h + 1) * HD]
     q_docs = docs_ref[...]
     q_first, q_last = jnp.min(q_docs), jnp.max(q_docs)
     ones = jnp.ones((rows, HD), jnp.bfloat16)
-
-    for at, (offset, z_from, z_count) in enumerate(sources):
+    wide = rows // HD
+
+    for at, offset in enumerate(sources):
         own, other = pieces[2 * at], pieces[2 * at + 1]
         their_x = lax.rem(my_x + offset, X)
 
-        def block(z, carry, own=own, other=other, their_x=their_x, z_from=z_from):
-            their_block = (z_from + z) * X + their_x
+        def block(z, carry, own=own, other=other, their_x=their_x):
+            their_block = z * X + their_x
             docs_own = own[z, rows : rows + PAD, :].astype(jnp.float32)
             docs_other = other[z, rows : rows + PAD, :].astype(jnp.float32)
             k_first = jnp.min(jnp.minimum(docs_own, docs_other))
@@ -66,32 +71,33 @@
                     allowed = []
                     for side, docs in ((my_core, docs_own), (1 - my_core, docs_other)):
                         same = jnp.broadcast_to(docs[:1], (rows, rows)) == jnp.concatenate(
-                            [q_docs] * (rows // HD), axis=1
+                            [q_docs] * wide, axis=1
                         )
-                        allowed.append(same & (k_pos + side * rows <= q_pos))
+                        one = same & (k_pos + side * rows <= q_pos)
+                        one = jnp.where(one, 1.0, 0.0)
+                        allowed.append(jnp.concatenate([one] * group, axis=0) > 0.5)
+                keys = [ref[z, :rows, :HD] for ref in (own, other)]
                 values = [
                     jnp.concatenate([ref[z, :rows, HD:], ones], axis=1) for ref in (own, other)
                 ]
-                for h in range(heads):
-                    q = q_ref[:, h * HD : (h + 1) * HD]
+                for g in range(heads // group):
+                    these = slice(g * group * rows, (g + 1) * group * rows)
+                    q = stack_ref[these, :]
                     scores = [
                         lax.dot_general(
-                            q,
-                            ref[z, :rows, :HD],
-                            (((1,), (1,)), ((), ())),
-                            preferred_element_type=jnp.float32,
+                            q, k, (((1,), (1,)), ((), ())), preferred_element_type=jnp.float32
                         )
-                        for ref in (own, other)
+                        for k in keys
                     ]
                     if masked:
                         scores = [jnp.where(a, s, NEG) for a, s in zip(allowed, scores)]
-                    old = m_ref[h]
+                    old = m_ref[these, :]
                     top = jnp.max(jnp.maximum(scores[0], scores[1]), axis=1, keepdims=True)
                     new = jnp.maximum(old, top)
-                    wide = jnp.concatenate([new] * (rows // HD), axis=1)
+                    broad = jnp.concatenate([new] * wide, axis=1)
                     total = None
                     for side in range(2):
-                        weights = jnp.exp2((scores[side] - wide) * SCALE2)
+                        weights = jnp.exp2((scores[side] - broad) * SCALE2)
                         if masked:
                             weights = jnp.where(allowed[side], weights, 0.0)
                         term = jnp.dot(
@@ -101,8 +107,10 @@
                         )
                         total = term if total is None else total + term
                     keep = jnp.exp2((old - new) * SCALE2)
-                    m_ref[h] = new
-                    acc_ref[h] = acc_ref[h] * jnp.concatenate([keep, keep], axis=1) + total
+                    m_ref[these, :] = new
+                    acc_ref[these, :] = (
+                        acc_ref[these, :] * jnp.concatenate([keep, keep], axis=1) + total
+                    )
 
             @pl.when(whole)
             def _():
@@ -114,31 +122,34 @@
 
             return carry
 
-        lax.fori_loop(0, z_count, block, 0)
+        lax.fori_loop(0, ZL, block, 0)
 
     if last:
         for h in range(heads):
-            done = (acc_ref[h, :, :HD] / acc_ref[h, :, HD:]).astype(jnp.bfloat16)
-            out_ref[:, h * HD : (h + 1) * HD] = done
-
-
-def attend(where, q, docs, pieces, sources, state, last):
+            these = slice(h * rows, (h + 1) * rows)
+            out_ref[:, h * HD : (h + 1) * HD] = (
+                acc_ref[these, :HD] / acc_ref[these, HD:]
+            ).astype(jnp.bfloat16)
+
+
+def attend(where, q, docs, pieces, sources, state, last, group=GROUP):
     rows, width = q.shape
     heads = width // HD
     first = state is None
     states = (
-        jax.ShapeDtypeStruct((heads, rows, HD), jnp.float32),
-        jax.ShapeDtypeStruct((heads, rows, 2 * HD), jnp.float32),
+        jax.ShapeDtypeStruct((heads * rows, HD), jnp.float32),
+        jax.ShapeDtypeStruct((heads * rows, 2 * HD), jnp.float32),
     )
     vmem = pl.BlockSpec(memory_space=pltpu.VMEM)
     inputs = [q, docs, *pieces] + ([] if first else list(state))
-    blocks = sum(s[2] for s in sources)
+    blocks = ZL * len(sources)
     return pl.pallas_call(
-        functools.partial(attend_kernel, heads, sources, first, last),
+        functools.partial(attend_kernel, group, sources, first, last),
         out_shape=jax.ShapeDtypeStruct((rows, width), jnp.bfloat16) if last else states,
         in_specs=[pl.BlockSpec(memory_space=pltpu.SMEM)] + [vmem] * len(inputs),
         out_specs=vmem if last else (vmem, vmem),
-        scratch_shapes=[pltpu.VMEM(s.shape, s.dtype) for s in states] if last else [],
+        scratch_shapes=([pltpu.VMEM(s.shape, s.dtype) for s in states] if last else [])
+        + [pltpu.VMEM((heads * rows, HD), jnp.bfloat16)],
         compiler_params=pltpu.CompilerParams(vmem_limit_bytes=40 << 20),
         cost_estimate=pl.CostEstimate(
             flops=blocks * heads * rows * 2 * rows * HD * 6,
@@ -280,17 +291,10 @@
     far = jnp.concatenate([far_a, far_b], axis=0)
     far_other = around(far, "core", CORE, 1)
 
-    state = attend(where, queries, docs, [mine, mine_other], [(0, 0, ZL)], None, False)
-    state = attend(
-        where,
-        queries,
-        docs,
-        [left, left_other, right, right_other],
-        [(X - 1, 0, ZL), (1, 0, ZL)],
-        state,
-        False,
-    )
-    attended = attend(where, queries, docs, [far, far_other], [(2, 0, ZL)], state, True)
+    state = attend(where, queries, docs, [mine, mine_other], (0,), None, False)
+    state = attend(where, queries, docs, [left, left_other], (X - 1,), state, False)
+    state = attend(where, queries, docs, [right, right_other], (1,), state, False)
+    attended = attend(where, queries, docs, [far, far_other], (2,), state, True)
     pieces = ring_over_y(attended)
     y = lax.axis_index("y").astype(jnp.int32).reshape(1)
     terms = project(y, pieces, weight)

time: 215 us -> 215 us (level)
    pallas_call x3 -> x4, Pallas kernels: 18.1 us -> 19 us  [attend(): pl.pallas_call(functools.partial(attend_kernel, group, sources, first, la...]
  transfers between devices with their start and end apart: 18 -> 18, of which waited for: 11 -> 11; matrix products, arithmetic and copies ran while one was open for 2% -> 1% of each run, Pallas kernels for 8% -> 9%
where the time goes in v1:
time: 215 us; the launch traced here: 214 us
  starting transfers between devices  63.7 us (30%)
  waiting for transfers between devices  55 us (26%)
  blocking collectives  45.9 us (21%)
  Pallas kernels  27.7 us (13%)
  between operations  13.7 us (6%)
  local copies, waits for them, and re-layouts  6.83 us (3%)
    ppermute x16, starting transfers between devices, around(): lax.ppermute(value, axis, [(i, (i + step) % size) for i in range(size)])  61.8 us
    ppermute x16, waiting for transfers between devices, around(): lax.ppermute(value, axis, [(i, (i + step) % size) for i in range(size)])  49 us
    all_to_all x1, blocking collectives, compute(): came = lax.all_to_all(terms, TP, split_axis=0, concat_axis=0, tiled=True)  30.9 us
    pallas_call x4, Pallas kernels, attend(): pl.pallas_call(functools.partial(attend_kernel, group, sources, first, la...  19 us
    all_gather x1, blocking collectives, compute(): mine = lax.all_gather(packed, 'zl', axis=0)  15 us
    pallas_call x1, Pallas kernels, project(): pl.pallas_call(functools.partial(project_kernel, offsets), out_shape=jax....  6.97 us
    ppermute x1, waiting for transfers between devices, compute(): swapped = lax.ppermute(out_weight, ('x', 'core', 'y'), swap)  5.97 us
    unnamed x7, local copies, waits for them, and re-layouts  5.05 us
  transfers between devices with their start and end apart: 18, of which 11 were waited for; matrix products, arithmetic and copies ran while one was open for 1% of the time, Pallas kernels for 9%

profile of v1, /device:TPU:200, one launch (start us, length us, event | category | flops | bytes accessed | tf_op | source)
XLA Modules:
  0.0 213.8 jit_solution(3529023246059610872)
XLA Ops:
  8.5 6.0 %collective-permute-done.16 = bf16[512,256]{1,0:T(8,128)(2,1)S(1)} collective-permute-done((bf16[512,256]{1,0:T(8,128)(2,1)}, bf16[512,256]{1,0:T(8,128)(2,1)S(1)}, u32[]{:S(2)}, u32[]{:S(2)}) %collective-permute-start.16) | collective-permute-done | bytes 262176 | tf_op jit(solution)/shard_map/ppermute | solution.py:270
  16.9 15.0 %all-gather = bf16[1056,256]{1,0:T(8,128)(2,1)S(1)} all-gather(bf16[264,256]{1,0:T(8,128)(2,1)S(1)} %pad_maximum_fusion), channel_id=2, replica_groups=mesh['zl'=4,'x'=4,'core'=2,'zh'=2,'y'=8] {'zl'}, dimensions={0}, use_global_device_ids=true | all-gather | bytes 675840 | tf_op jit(solution)/shard_map/all_gather | solution.py:283
  31.9 18.6 %collective-permute-start = (bf16[4,264,256]{2,1,0:T(8,128)(2,1)S(1)}, bf16[4,264,256]{2,1,0:T(8,128)(2,1)S(1)}, u32[]{:S(2)}, u32[]{:S(2)}) collective-permute-start(bf16[4,264,256]{2,1,0:T(8,128)(2,1)S(1)} %bitcast.7), channel_id=1, source_target_pairs={{0,32},{32,64},{64,96},{96,0},{1,33},{33,65},{65,97},{97,1},{2,34}... | collective-permute-start | bytes 1622024 | tf_op jit(solution)/shard_map/ppermute | solution.py:163
  52.4 20.7 %collective-permute-done.refs_0_ = bf16[4,264,256]{2,1,0:T(8,128)(2,1)S(1)} collective-permute-done((bf16[4,264,256]{2,1,0:T(8,128)(2,1)S(1)}, bf16[4,264,256]{2,1,0:T(8,128)(2,1)S(1)}, u32[]{:S(2)}, u32[]{:S(2)}) %collective-permute-start) | collective-permute-done | bytes 540704 | tf_op jit(solution)/shard_map/ppermute | solution.py:163
  73.1 4.4 %collective-permute-start.1 = (bf16[2,264,256]{2,1,0:T(8,128)(2,1)S(1)}, bf16[2,264,256]{2,1,0:T(8,128)(2,1)S(1)}, u32[]{:S(2)}, u32[]{:S(2)}) collective-permute-start(bf16[2,264,256]{2,1,0:T(8,128)(2,1)S(1)} %slice.16), channel_id=1, source_target_pairs={{0,32},{32,64},{64,96},{96,0},{1,33},{33,65},{65,97},{97,1},{2,34}... | collective-permute-start | bytes 811016 | tf_op jit(solution)/shard_map/ppermute | solution.py:163
  80.2 4.5 %collective-permute-start.3 = (bf16[2,264,256]{2,1,0:T(8,128)(2,1)}, bf16[2,264,256]{2,1,0:T(8,128)(2,1)S(1)}, u32[]{:S(2)}, u32[]{:S(2)}) collective-permute-start(bf16[2,264,256]{2,1,0:T(8,128)(2,1)} %slice.17), channel_id=1, source_target_pairs={{0,96},{32,0},{64,32},{96,64},{1,97},{33,1},{65,33},{97,65},{2,98}... | collective-permute-start | bytes 811016 | tf_op jit(solution)/shard_map/ppermute | solution.py:163
  89.0 8.0 %collective-permute-done.3 = bf16[2,264,256]{2,1,0:T(8,128)(2,1)S(1)} collective-permute-done((bf16[2,264,256]{2,1,0:T(8,128)(2,1)}, bf16[2,264,256]{2,1,0:T(8,128)(2,1)S(1)}, u32[]{:S(2)}, u32[]{:S(2)}) %collective-permute-start.3) | collective-permute-done | bytes 270368 | tf_op jit(solution)/shard_map/ppermute | solution.py:163
  100.1 5.8 %shard_map.55 = (f32[1024,128]{1,0:T(8,128)S(1)}, f32[1024,256]{1,0:T(8,128)S(1)}) custom-call(s32[3]{0:T(128)S(1)} %pad_add_fusion.where_ref, bf16[256,512]{1,0:T(8,128)(2,1)S(1)} %copy-done.1, f32[256,128]{1,0:T(8,128)S(1)} %broadcast_in_dim.4.docs_ref, bf16[4,264,256]{2,1,0:T(8,128)(2,1)S(1)} %bitcast.10, ...), custom_call_target="tpu_custom_call" | custom-call | flops 1610612736 | bytes 1048576 | tf_op jit(solution)/shard_map/pallas_call | solution.py:146
  105.9 4.4 %shard_map.56 = (f32[1024,128]{1,0:T(8,128)S(1)}, f32[1024,256]{1,0:T(8,128)S(1)}) custom-call(s32[3]{0:T(128)S(1)} %pad_add_fusion.where_ref, bf16[256,512]{1,0:T(8,128)(2,1)S(1)} %copy-done.1, f32[256,128]{1,0:T(8,128)S(1)} %broadcast_in_dim.4.docs_ref, bf16[4,264,256]{2,1,0:T(8,128)(2,1)S(1)} %collective-permute-done.refs_0_, ...), custom_call_target="tpu_custom_call" | custom-call | flops 1610612736 | bytes 1048576 | tf_op jit(solution)/shard_map/pallas_call | solution.py:146
  110.3 4.4 %shard_map.57 = (f32[1024,128]{1,0:T(8,128)S(1)}, f32[1024,256]{1,0:T(8,128)S(1)}) custom-call(s32[3]{0:T(128)S(1)} %pad_add_fusion.where_ref, bf16[256,512]{1,0:T(8,128)(2,1)S(1)} %copy-done.1, f32[256,128]{1,0:T(8,128)S(1)} %broadcast_in_dim.4.docs_ref, bf16[4,264,256]{2,1,0:T(8,128)(2,1)S(1)} %collective-permute-done.2.refs_0_, ...), custom_call_target="tpu_custom_call" | custom-call | flops 1610612736 | bytes 1048576 | tf_op jit(solution)/shard_map/pallas_call | solution.py:146
  114.7 4.4 %shard_map.58.refs_0_ = bf16[256,512]{1,0:T(8,128)(2,1)S(1)} custom-call(s32[3]{0:T(128)S(1)} %pad_add_fusion.where_ref, bf16[256,512]{1,0:T(8,128)(2,1)S(1)} %copy-done.1, f32[256,128]{1,0:T(8,128)S(1)} %broadcast_in_dim.4.docs_ref, bf16[4,264,256]{2,1,0:T(8,128)(2,1)S(1)} %constant_dynamic-update-slice_fusion.refs_0_, ...), custom_call_target="tpu_custom_call" | custom-call | flops 1610612736 | bytes 1048576 | tf_op jit(solution)/shard_map/pallas_call | solution.py:146
  119.2 2.5 %collective-permute-start.8 = (bf16[256,512]{1,0:T(8,128)(2,1)S(1)}, bf16[256,512]{1,0:T(8,128)(2,1)S(1)}, u32[]{:S(2)}, u32[]{:S(2)}) collective-permute-start(bf16[256,512]{1,0:T(8,128)(2,1)S(1)} %shard_map.58.refs_0_), channel_id=1, source_target_pairs={{0,1},{1,2},{2,3},{3,4},{4,5},{5,6},{6,7},{7,0},{8,9},{9,10},{10,1... | collective-permute-start | bytes 786440 | tf_op jit(solution)/shard_map/ppermute | solution.py:163
  121.7 3.3 %collective-permute-start.9 = (bf16[256,512]{1,0:T(8,128)(2,1)S(1)}, bf16[256,512]{1,0:T(8,128)(2,1)S(1)}, u32[]{:S(2)}, u32[]{:S(2)}) collective-permute-start(bf16[256,512]{1,0:T(8,128)(2,1)S(1)} %shard_map.58.refs_0_), channel_id=1, source_target_pairs={{0,7},{1,0},{2,1},{3,2},{4,3},{5,4},{6,5},{7,6},{8,15},{9,8},{10,9... | collective-permute-start | bytes 786440 | tf_op jit(solution)/shard_map/ppermute | solution.py:163
  125.0 3.8 %collective-permute-done.8.refs_1_ = bf16[256,512]{1,0:T(8,128)(2,1)S(1)} collective-permute-done((bf16[256,512]{1,0:T(8,128)(2,1)S(1)}, bf16[256,512]{1,0:T(8,128)(2,1)S(1)}, u32[]{:S(2)}, u32[]{:S(2)}) %collective-permute-start.8) | collective-permute-done | bytes 262176 | tf_op jit(solution)/shard_map/ppermute | solution.py:163
  128.8 2.5 %collective-permute-start.10 = (bf16[256,512]{1,0:T(8,128)(2,1)S(1)}, bf16[256,512]{1,0:T(8,128)(2,1)S(1)}, u32[]{:S(2)}, u32[]{:S(2)}) collective-permute-start(bf16[256,512]{1,0:T(8,128)(2,1)S(1)} %collective-permute-done.8.refs_1_), channel_id=1, source_target_pairs={{0,1},{1,2},{2,3},{3,4},{4,5},{5,6},{6,7},{7,0},{8,9},{9,10},{10,1... | collective-permute-start | bytes 786440 | tf_op jit(solution)/shard_map/ppermute | solution.py:163
  131.7 3.7 %collective-permute-start.11 = (bf16[256,512]{1,0:T(8,128)(2,1)S(1)}, bf16[256,512]{1,0:T(8,128)(2,1)S(1)}, u32[]{:S(2)}, u32[]{:S(2)}) collective-permute-start(bf16[256,512]{1,0:T(8,128)(2,1)S(1)} %collective-permute-done.9.refs_2_), channel_id=1, source_target_pairs={{0,7},{1,0},{2,1},{3,2},{4,3},{5,4},{6,5},{7,6},{8,15},{9,8},{10,9... | collective-permute-start | bytes 786440 | tf_op jit(solution)/shard_map/ppermute | solution.py:163
  135.5 4.4 %collective-permute-done.10.refs_3_ = bf16[256,512]{1,0:T(8,128)(2,1)S(1)} collective-permute-done((bf16[256,512]{1,0:T(8,128)(2,1)S(1)}, bf16[256,512]{1,0:T(8,128)(2,1)S(1)}, u32[]{:S(2)}, u32[]{:S(2)}) %collective-permute-start.10) | collective-permute-done | bytes 262176 | tf_op jit(solution)/shard_map/ppermute | solution.py:163
  142.7 4.5 %collective-permute-start.13 = (bf16[256,512]{1,0:T(8,128)(2,1)S(1)}, bf16[256,512]{1,0:T(8,128)(2,1)S(1)}, u32[]{:S(2)}, u32[]{:S(2)}) collective-permute-start(bf16[256,512]{1,0:T(8,128)(2,1)S(1)} %collective-permute-done.11.refs_4_), channel_id=1, source_target_pairs={{0,7},{1,0},{2,1},{3,2},{4,3},{5,4},{6,5},{7,6},{8,15},{9,8},{10,9... | collective-permute-start | bytes 786440 | tf_op jit(solution)/shard_map/ppermute | solution.py:163
  147.3 4.8 %collective-permute-done.12.refs_5_ = bf16[256,512]{1,0:T(8,128)(2,1)S(1)} collective-permute-done((bf16[256,512]{1,0:T(8,128)(2,1)S(1)}, bf16[256,512]{1,0:T(8,128)(2,1)S(1)}, u32[]{:S(2)}, u32[]{:S(2)}) %collective-permute-start.12) | collective-permute-done | bytes 262176 | tf_op jit(solution)/shard_map/ppermute | solution.py:163
  155.6 3.5 %collective-permute-start.15 = (bf16[128,512]{1,0:T(8,128)(2,1)S(1)}, bf16[128,512]{1,0:T(8,128)(2,1)S(1)}, u32[]{:S(2)}, u32[]{:S(2)}) collective-permute-start(bf16[128,512]{1,0:T(8,128)(2,1)S(1)} %slice.19), channel_id=1, source_target_pairs={{0,7},{1,0},{2,1},{3,2},{4,3},{5,4},{6,5},{7,6},{8,15},{9,8},{10,9... | collective-permute-start | bytes 393224 | tf_op jit(solution)/shard_map/ppermute | solution.py:163
  160.1 3.7 %collective-permute-done.15.refs_8_ = bf16[128,512]{1,0:T(8,128)(2,1)S(1)} collective-permute-done((bf16[128,512]{1,0:T(8,128)(2,1)S(1)}, bf16[128,512]{1,0:T(8,128)(2,1)S(1)}, u32[]{:S(2)}, u32[]{:S(2)}) %collective-permute-start.15) | collective-permute-done | bytes 131104 | tf_op jit(solution)/shard_map/ppermute | solution.py:163
  163.8 3.4 %copy-done = bf16[16384,256]{1,0:T(8,128)(2,1)S(1)} copy-done((bf16[16384,256]{1,0:T(8,128)(2,1)S(1)}, bf16[16384,256]{1,0:T(8,128)(2,1)}, u32[]{:S(2)}) %copy-start) | copy-done | bytes 8388632
  167.2 7.0 %shard_map.59 = bf16[16,16,1024]{2,1,0:T(8,128)(2,1)S(1)} custom-call(s32[1]{0:T(128)} %bitcast.y_ref, bf16[256,512]{1,0:T(8,128)(2,1)S(1)} %shard_map.58.refs_0_, bf16[256,512]{1,0:T(8,128)(2,1)S(1)} %collective-permute-done.8.refs_1_, bf16[256,512]{1,0:T(8,128)(2,1)S(1)} %collective-permute-done.9.refs_2_, ...), custom_call_target="tpu_custom_call" | custom-call | flops 2147483648 | bytes 10485760 | tf_op jit(solution)/shard_map/pallas_call | solution.py:223
  174.2 30.9 %all_to_all.5.came_ref = bf16[16,16,1024]{2,1,0:T(8,128)(2,1)} all-to-all(bf16[16,16,1024]{2,1,0:T(8,128)(2,1)S(1)} %shard_map.59), channel_id=1, replica_groups=mesh['zl'=4,'x'=4,'core'=2,'zh'=2,'y'=8] {'zh','y'}, dimensions={0} | all-to-all | bytes 1048576 | tf_op jit(solution)/shard_map/all_to_all | solution.py:301
  (39 shorter events, 25.9 us)
Async XLA Ops:
  6.5 157.3 %all-gather.4.cloned.1.call-start = ((), (), s32[]{:S(2)}) async-start(), calls=%async_computation.1 | async-start | bytes 8650752 | tf_op jit(solution)/shard_map/all_gather | solution.py:271
  6.5 7.9 %collective-permute-start.16 = (bf16[512,256]{1,0:T(8,128)(2,1)}, bf16[512,256]{1,0:T(8,128)(2,1)S(1)}, u32[]{:S(2)}, u32[]{:S(2)}) collective-permute-start(bf16[512,256]{1,0:T(8,128)(2,1)} %param.9), channel_id=1, source_target_pairs={{0,0},{1,16},{2,32},{3,48},{4,64},{5,80},{6,96},{7,112},{16,1},{17... | collective-permute-start | bytes 786440 | tf_op jit(solution)/shard_map/ppermute | solution.py:270
  14.4 0.7 copy-start.2
  31.9 41.2 %collective-permute-start = (bf16[4,264,256]{2,1,0:T(8,128)(2,1)S(1)}, bf16[4,264,256]{2,1,0:T(8,128)(2,1)S(1)}, u32[]{:S(2)}, u32[]{:S(2)}) collective-permute-start(bf16[4,264,256]{2,1,0:T(8,128)(2,1)S(1)} %bitcast.7), channel_id=1, source_target_pairs={{0,32},{32,64},{64,96},{96,0},{1,33},{33,65},{65,97},{97,1},{2,34}... | collective-permute-start | bytes 1622024 | tf_op jit(solution)/shard_map/ppermute | solution.py:163
  50.4 29.0 %collective-permute-start.2 = (bf16[4,264,256]{2,1,0:T(8,128)(2,1)S(1)}, bf16[4,264,256]{2,1,0:T(8,128)(2,1)S(1)}, u32[]{:S(2)}, u32[]{:S(2)}) collective-permute-start(bf16[4,264,256]{2,1,0:T(8,128)(2,1)S(1)} %bitcast.8), channel_id=1, source_target_pairs={{0,96},{32,0},{64,32},{96,64},{1,97},{33,1},{65,33},{97,65},{2,98}... | collective-permute-start | bytes 1622024 | tf_op jit(solution)/shard_map/ppermute | solution.py:163
  73.1 15.9 %collective-permute-start.1 = (bf16[2,264,256]{2,1,0:T(8,128)(2,1)S(1)}, bf16[2,264,256]{2,1,0:T(8,128)(2,1)S(1)}, u32[]{:S(2)}, u32[]{:S(2)}) collective-permute-start(bf16[2,264,256]{2,1,0:T(8,128)(2,1)S(1)} %slice.16), channel_id=1, source_target_pairs={{0,32},{32,64},{64,96},{96,0},{1,33},{33,65},{65,97},{97,1},{2,34}... | collective-permute-start | bytes 811016 | tf_op jit(solution)/shard_map/ppermute | solution.py:163
  77.5 21.6 %collective-permute-start.7 = (bf16[4,264,256]{2,1,0:T(8,128)(2,1)S(1)}, bf16[4,264,256]{2,1,0:T(8,128)(2,1)S(1)}, u32[]{:S(2)}, u32[]{:S(2)}) collective-permute-start(bf16[4,264,256]{2,1,0:T(8,128)(2,1)S(1)} %bitcast.9), channel_id=1, source_target_pairs={{0,16},{16,0},{1,17},{17,1},{2,18},{18,2},{3,19},{19,3},{4,20},{20... | collective-permute-start | bytes 1622024 | tf_op jit(solution)/shard_map/ppermute | solution.py:163
  80.2 16.9 %collective-permute-start.3 = (bf16[2,264,256]{2,1,0:T(8,128)(2,1)}, bf16[2,264,256]{2,1,0:T(8,128)(2,1)S(1)}, u32[]{:S(2)}, u32[]{:S(2)}) collective-permute-start(bf16[2,264,256]{2,1,0:T(8,128)(2,1)} %slice.17), channel_id=1, source_target_pairs={{0,96},{32,0},{64,32},{96,64},{1,97},{33,1},{65,33},{97,65},{2,98}... | collective-permute-start | bytes 811016 | tf_op jit(solution)/shard_map/ppermute | solution.py:163
  84.6 21.3 %collective-permute-start.6 = (bf16[4,264,256]{2,1,0:T(8,128)(2,1)S(1)}, bf16[4,264,256]{2,1,0:T(8,128)(2,1)S(1)}, u32[]{:S(2)}, u32[]{:S(2)}) collective-permute-start(bf16[4,264,256]{2,1,0:T(8,128)(2,1)S(1)} %collective-permute-done.refs_0_), channel_id=1, source_target_pairs={{0,16},{16,0},{1,17},{17,1},{2,18},{18,2},{3,19},{19,3},{4,20},{20... | collective-permute-start | bytes 1622024 | tf_op jit(solution)/shard_map/ppermute | solution.py:163
  86.6 23.7 %collective-permute-start.5 = (bf16[4,264,256]{2,1,0:T(8,128)(2,1)S(1)}, bf16[4,264,256]{2,1,0:T(8,128)(2,1)S(1)}, u32[]{:S(2)}, u32[]{:S(2)}) collective-permute-start(bf16[4,264,256]{2,1,0:T(8,128)(2,1)S(1)} %collective-permute-done.2.refs_0_), channel_id=1, source_target_pairs={{0,16},{16,0},{1,17},{17,1},{2,18},{18,2},{3,19},{19,3},{4,20},{20... | collective-permute-start | bytes 1622024 | tf_op jit(solution)/shard_map/ppermute | solution.py:163
  97.1 17.7 %collective-permute-start.4 = (bf16[4,264,256]{2,1,0:T(8,128)(2,1)S(1)}, bf16[4,264,256]{2,1,0:T(8,128)(2,1)S(1)}, u32[]{:S(2)}, u32[]{:S(2)}) collective-permute-start(bf16[4,264,256]{2,1,0:T(8,128)(2,1)S(1)} %constant_dynamic-update-slice_fusion.refs_0_), channel_id=1, source_target_pairs={{0,16},{16,0},{1,17},{17,1},{2,18},{18,2},{3,19},{19,3},{4,20},{20... | collective-permute-start | bytes 1622024 | tf_op jit(solution)/shard_map/ppermute | solution.py:163
  99.2 1.0 copy-start.1
  119.2 9.7 %collective-permute-start.8 = (bf16[256,512]{1,0:T(8,128)(2,1)S(1)}, bf16[256,512]{1,0:T(8,128)(2,1)S(1)}, u32[]{:S(2)}, u32[]{:S(2)}) collective-permute-start(bf16[256,512]{1,0:T(8,128)(2,1)S(1)} %shard_map.58.refs_0_), channel_id=1, source_target_pairs={{0,1},{1,2},{2,3},{3,4},{4,5},{5,6},{6,7},{7,0},{8,9},{9,10},{10,1... | collective-permute-start | bytes 786440 | tf_op jit(solution)/shard_map/ppermute | solution.py:163
  121.7 10.0 %collective-permute-start.9 = (bf16[256,512]{1,0:T(8,128)(2,1)S(1)}, bf16[256,512]{1,0:T(8,128)(2,1)S(1)}, u32[]{:S(2)}, u32[]{:S(2)}) collective-permute-start(bf16[256,512]{1,0:T(8,128)(2,1)S(1)} %shard_map.58.refs_0_), channel_id=1, source_target_pairs={{0,7},{1,0},{2,1},{3,2},{4,3},{5,4},{6,5},{7,6},{8,15},{9,8},{10,9... | collective-permute-start | bytes 786440 | tf_op jit(solution)/shard_map/ppermute | solution.py:163
  128.8 11.0 %collective-permute-start.10 = (bf16[256,512]{1,0:T(8,128)(2,1)S(1)}, bf16[256,512]{1,0:T(8,128)(2,1)S(1)}, u32[]{:S(2)}, u32[]{:S(2)}) collective-permute-start(bf16[256,512]{1,0:T(8,128)(2,1)S(1)} %collective-permute-done.8.refs_1_), channel_id=1, source_target_pairs={{0,1},{1,2},{2,3},{3,4},{4,5},{5,6},{6,7},{7,0},{8,9},{9,10},{10,1... | collective-permute-start | bytes 786440 | tf_op jit(solution)/shard_map/ppermute | solution.py:163
  131.7 11.0 %collective-permute-start.11 = (bf16[256,512]{1,0:T(8,128)(2,1)S(1)}, bf16[256,512]{1,0:T(8,128)(2,1)S(1)}, u32[]{:S(2)}, u32[]{:S(2)}) collective-permute-start(bf16[256,512]{1,0:T(8,128)(2,1)S(1)} %collective-permute-done.9.refs_2_), channel_id=1, source_target_pairs={{0,7},{1,0},{2,1},{3,2},{4,3},{5,4},{6,5},{7,6},{8,15},{9,8},{10,9... | collective-permute-start | bytes 786440 | tf_op jit(solution)/shard_map/ppermute | solution.py:163
  139.9 12.2 %collective-permute-start.12 = (bf16[256,512]{1,0:T(8,128)(2,1)S(1)}, bf16[256,512]{1,0:T(8,128)(2,1)S(1)}, u32[]{:S(2)}, u32[]{:S(2)}) collective-permute-start(bf16[256,512]{1,0:T(8,128)(2,1)S(1)} %collective-permute-done.10.refs_3_), channel_id=1, source_target_pairs={{0,1},{1,2},{2,3},{3,4},{4,5},{5,6},{6,7},{7,0},{8,9},{9,10},{10,1... | collective-permute-start | bytes 786440 | tf_op jit(solution)/shard_map/ppermute | solution.py:163
  142.7 12.8 %collective-permute-start.13 = (bf16[256,512]{1,0:T(8,128)(2,1)S(1)}, bf16[256,512]{1,0:T(8,128)(2,1)S(1)}, u32[]{:S(2)}, u32[]{:S(2)}) collective-permute-start(bf16[256,512]{1,0:T(8,128)(2,1)S(1)} %collective-permute-done.11.refs_4_), channel_id=1, source_target_pairs={{0,7},{1,0},{2,1},{3,2},{4,3},{5,4},{6,5},{7,6},{8,15},{9,8},{10,9... | collective-permute-start | bytes 786440 | tf_op jit(solution)/shard_map/ppermute | solution.py:163
  152.1 8.0 %collective-permute-start.14 = (bf16[128,512]{1,0:T(8,128)(2,1)S(1)}, bf16[128,512]{1,0:T(8,128)(2,1)S(1)}, u32[]{:S(2)}, u32[]{:S(2)}) collective-permute-start(bf16[128,512]{1,0:T(8,128)(2,1)S(1)} %slice.18), channel_id=1, source_target_pairs={{0,1},{1,2},{2,3},{3,4},{4,5},{5,6},{6,7},{7,0},{8,9},{9,10},{10,1... | collective-permute-start | bytes 393224 | tf_op jit(solution)/shard_map/ppermute | solution.py:163
  155.6 8.2 %collective-permute-start.15 = (bf16[128,512]{1,0:T(8,128)(2,1)S(1)}, bf16[128,512]{1,0:T(8,128)(2,1)S(1)}, u32[]{:S(2)}, u32[]{:S(2)}) collective-permute-start(bf16[128,512]{1,0:T(8,128)(2,1)S(1)} %slice.19), channel_id=1, source_target_pairs={{0,7},{1,0},{2,1},{3,2},{4,3},{5,4},{6,5},{7,6},{8,15},{9,8},{10,9... | collective-permute-start | bytes 393224 | tf_op jit(solution)/shard_map/ppermute | solution.py:163
  163.8 3.4 %copy-start = (bf16[16384,256]{1,0:T(8,128)(2,1)S(1)}, bf16[16384,256]{1,0:T(8,128)(2,1)}, u32[]{:S(2)}) copy-start(bf16[16384,256]{1,0:T(8,128)(2,1)} %all-gather.4.cloned.1.call-done) | copy-start | bytes 25165828
Sparse Core Ops, SparseCore 0:
  15.3 100.2 all-gather.3

commit v2 on v1

--- a/solution.py
+++ b/solution.py
@@ -168,10 +168,11 @@
     pieces = [(0, attended)]
     left = right = attended
     for step in range(1, Y // 2):
+        if step == Y // 2 - 1:
+            far = (around(left[:half], "y", Y, 2), around(right[half:], "y", Y, -2))
         left = around(left, "y", Y, 1)
         right = around(right, "y", Y, -1)
         pieces += [(-step, left), (step, right)]
-    far = (around(left[:half], "y", Y, 1), around(right[half:], "y", Y, -1))
     return pieces + [(Y // 2, far)]
 
 
@@ -232,7 +233,7 @@
             pltpu.VMEM((ZL, rows, width), jnp.float32),
             pltpu.SemaphoreType.DMA((Y, ZL)),
         ],
-        compiler_params=pltpu.CompilerParams(vmem_limit_bytes=24 << 20),
+        compiler_params=pltpu.CompilerParams(vmem_limit_bytes=51 << 20),
         cost_estimate=pl.CostEstimate(
             flops=2 * Y * rows * depth * ZL * width,
             bytes_accessed=2 * (Y * depth * ZL * width + Y * rows * depth),

time: 215 us -> 210 us (0.977)
  waiting for transfers between devices: 55 us -> 50 us
  local copies, waits for them, and re-layouts: 6.83 us -> 3.44 us
  starting transfers between devices: 63.7 us -> 66.6 us
    ppermute x16, waiting for transfers between devices: 49 us -> 44 us  [around(): lax.ppermute(value, axis, [(i, (i + step) % size) for i in range(size)])]
    unnamed x7 -> x5, local copies, waits for them, and re-layouts: 5.05 us -> 1.67 us
    ppermute x16, starting transfers between devices: 61.8 us -> 64.7 us  [around(): lax.ppermute(value, axis, [(i, (i + step) % size) for i in range(size)])]
  transfers between devices with their start and end apart: 18 -> 18, of which waited for: 11 -> 9; matrix products, arithmetic and copies ran while one was open for 1% -> 1% of each run, Pallas kernels for 9% -> 9%
where the time goes in v2:
time: 210 us; the launch traced here: 209 us
  starting transfers between devices  66.6 us (32%)
  waiting for transfers between devices  50 us (24%)
  blocking collectives  46.9 us (22%)
  Pallas kernels  27.9 us (13%)
  between operations  13.7 us (7%)
  local copies, waits for them, and re-layouts  3.44 us (2%)
    ppermute x16, starting transfers between devices, around(): lax.ppermute(value, axis, [(i, (i + step) % size) for i in range(size)])  64.7 us
    ppermute x16, waiting for transfers between devices, around(): lax.ppermute(value, axis, [(i, (i + step) % size) for i in range(size)])  44 us
    all_to_all x1, blocking collectives, compute(): came = lax.all_to_all(terms, TP, split_axis=0, concat_axis=0, tiled=True)  31.9 us
    pallas_call x4, Pallas kernels, attend(): pl.pallas_call(functools.partial(attend_kernel, group, sources, first, la...  19 us
    all_gather x1, blocking collectives, compute(): mine = lax.all_gather(packed, 'zl', axis=0)  15 us
    pallas_call x1, Pallas kernels, project(): pl.pallas_call(functools.partial(project_kernel, offsets), out_shape=jax....  7.12 us
    ppermute x1, waiting for transfers between devices, compute(): swapped = lax.ppermute(out_weight, ('x', 'core', 'y'), swap)  5.97 us
  transfers between devices with their start and end apart: 18, of which 9 were waited for; matrix products, arithmetic and copies ran while one was open for 1% of the time, Pallas kernels for 9%

profile of v2, /device:TPU:200, one launch (start us, length us, event | category | flops | bytes accessed | tf_op | source)
XLA Modules:
  0.0 209.4 jit_solution(6189286131891442655)
XLA Ops:
  8.5 6.0 %collective-permute-done.16 = bf16[512,256]{1,0:T(8,128)(2,1)S(1)} collective-permute-done((bf16[512,256]{1,0:T(8,128)(2,1)}, bf16[512,256]{1,0:T(8,128)(2,1)S(1)}, u32[]{:S(2)}, u32[]{:S(2)}) %collective-permute-start.16) | collective-permute-done | bytes 262176 | tf_op jit(solution)/shard_map/ppermute | solution.py:271
  16.9 15.0 %all-gather = bf16[1056,256]{1,0:T(8,128)(2,1)S(1)} all-gather(bf16[264,256]{1,0:T(8,128)(2,1)S(1)} %pad_maximum_fusion), channel_id=2, replica_groups=mesh['zl'=4,'x'=4,'core'=2,'zh'=2,'y'=8] {'zl'}, dimensions={0}, use_global_device_ids=true | all-gather | bytes 675840 | tf_op jit(solution)/shard_map/all_gather | solution.py:284
  31.9 18.6 %collective-permute-start = (bf16[4,264,256]{2,1,0:T(8,128)(2,1)S(1)}, bf16[4,264,256]{2,1,0:T(8,128)(2,1)S(1)}, u32[]{:S(2)}, u32[]{:S(2)}) collective-permute-start(bf16[4,264,256]{2,1,0:T(8,128)(2,1)S(1)} %bitcast.6), channel_id=1, source_target_pairs={{0,32},{32,64},{64,96},{96,0},{1,33},{33,65},{65,97},{97,1},{2,34}... | collective-permute-start | bytes 1622024 | tf_op jit(solution)/shard_map/ppermute | solution.py:163
  52.4 20.7 %collective-permute-done.refs_0_ = bf16[4,264,256]{2,1,0:T(8,128)(2,1)S(1)} collective-permute-done((bf16[4,264,256]{2,1,0:T(8,128)(2,1)S(1)}, bf16[4,264,256]{2,1,0:T(8,128)(2,1)S(1)}, u32[]{:S(2)}, u32[]{:S(2)}) %collective-permute-start) | collective-permute-done | bytes 540704 | tf_op jit(solution)/shard_map/ppermute | solution.py:163
  73.1 4.4 %collective-permute-start.1 = (bf16[2,264,256]{2,1,0:T(8,128)(2,1)S(1)}, bf16[2,264,256]{2,1,0:T(8,128)(2,1)S(1)}, u32[]{:S(2)}, u32[]{:S(2)}) collective-permute-start(bf16[2,264,256]{2,1,0:T(8,128)(2,1)S(1)} %slice.16), channel_id=1, source_target_pairs={{0,32},{32,64},{64,96},{96,0},{1,33},{33,65},{65,97},{97,1},{2,34}... | collective-permute-start | bytes 811016 | tf_op jit(solution)/shard_map/ppermute | solution.py:163
  80.2 4.5 %collective-permute-start.3 = (bf16[2,264,256]{2,1,0:T(8,128)(2,1)}, bf16[2,264,256]{2,1,0:T(8,128)(2,1)S(1)}, u32[]{:S(2)}, u32[]{:S(2)}) collective-permute-start(bf16[2,264,256]{2,1,0:T(8,128)(2,1)} %slice.17), channel_id=1, source_target_pairs={{0,96},{32,0},{64,32},{96,64},{1,97},{33,1},{65,33},{97,65},{2,98}... | collective-permute-start | bytes 811016 | tf_op jit(solution)/shard_map/ppermute | solution.py:163
  86.6 2.4 %collective-permute-start.5 = (bf16[4,264,256]{2,1,0:T(8,128)(2,1)S(1)}, bf16[4,264,256]{2,1,0:T(8,128)(2,1)S(1)}, u32[]{:S(2)}, u32[]{:S(2)}) collective-permute-start(bf16[4,264,256]{2,1,0:T(8,128)(2,1)S(1)} %collective-permute-done.2.refs_0_), channel_id=1, source_target_pairs={{0,16},{16,0},{1,17},{17,1},{2,18},{18,2},{3,19},{19,3},{4,20},{20... | collective-permute-start | bytes 1622024 | tf_op jit(solution)/shard_map/ppermute | solution.py:163
  89.0 8.0 %collective-permute-done.3 = bf16[2,264,256]{2,1,0:T(8,128)(2,1)S(1)} collective-permute-done((bf16[2,264,256]{2,1,0:T(8,128)(2,1)}, bf16[2,264,256]{2,1,0:T(8,128)(2,1)S(1)}, u32[]{:S(2)}, u32[]{:S(2)}) %collective-permute-start.3) | collective-permute-done | bytes 270368 | tf_op jit(solution)/shard_map/ppermute | solution.py:163
  100.1 5.8 %shard_map.55 = (f32[1024,128]{1,0:T(8,128)S(1)}, f32[1024,256]{1,0:T(8,128)S(1)}) custom-call(s32[3]{0:T(128)S(1)} %pad_add_fusion.where_ref, bf16[256,512]{1,0:T(8,128)(2,1)S(1)} %copy-done, f32[256,128]{1,0:T(8,128)S(1)} %broadcast_in_dim.4.docs_ref, bf16[4,264,256]{2,1,0:T(8,128)(2,1)S(1)} %bitcast.9, bf16[4,264,256]{2,1,0:T(8,128)(2,1)S(1)} %collective-permute-done.7.refs_1_), custom_call_target="tpu_custom_call" | custom-call | flops 1610612736 | bytes 1048576 | tf_op jit(solution)/shard_map/pallas_call | solution.py:146
  105.9 4.4 %shard_map.56 = (f32[1024,128]{1,0:T(8,128)S(1)}, f32[1024,256]{1,0:T(8,128)S(1)}) custom-call(s32[3]{0:T(128)S(1)} %pad_add_fusion.where_ref, bf16[256,512]{1,0:T(8,128)(2,1)S(1)} %copy-done, f32[256,128]{1,0:T(8,128)S(1)} %broadcast_in_dim.4.docs_ref, bf16[4,264,256]{2,1,0:T(8,128)(2,1)S(1)} %collective-permute-done.refs_0_, ...), custom_call_target="tpu_custom_call" | custom-call | flops 1610612736 | bytes 1048576 | tf_op jit(solution)/shard_map/pallas_call | solution.py:146
  110.3 4.4 %shard_map.57 = (f32[1024,128]{1,0:T(8,128)S(1)}, f32[1024,256]{1,0:T(8,128)S(1)}) custom-call(s32[3]{0:T(128)S(1)} %pad_add_fusion.where_ref, bf16[256,512]{1,0:T(8,128)(2,1)S(1)} %copy-done, f32[256,128]{1,0:T(8,128)S(1)} %broadcast_in_dim.4.docs_ref, bf16[4,264,256]{2,1,0:T(8,128)(2,1)S(1)} %collective-permute-done.2.refs_0_, ...), custom_call_target="tpu_custom_call" | custom-call | flops 1610612736 | bytes 1048576 | tf_op jit(solution)/shard_map/pallas_call | solution.py:146
  114.7 4.4 %shard_map.58.refs_0_ = bf16[256,512]{1,0:T(8,128)(2,1)S(1)} custom-call(s32[3]{0:T(128)S(1)} %pad_add_fusion.where_ref, bf16[256,512]{1,0:T(8,128)(2,1)S(1)} %copy-done, f32[256,128]{1,0:T(8,128)S(1)} %broadcast_in_dim.4.docs_ref, bf16[4,264,256]{2,1,0:T(8,128)(2,1)S(1)} %constant_dynamic-update-slice_fusion.refs_0_, ...), custom_call_target="tpu_custom_call" | custom-call | flops 1610612736 | bytes 1048576 | tf_op jit(solution)/shard_map/pallas_call | solution.py:146
  119.1 2.5 %collective-permute-start.8 = (bf16[256,512]{1,0:T(8,128)(2,1)S(1)}, bf16[256,512]{1,0:T(8,128)(2,1)S(1)}, u32[]{:S(2)}, u32[]{:S(2)}) collective-permute-start(bf16[256,512]{1,0:T(8,128)(2,1)S(1)} %shard_map.58.refs_0_), channel_id=1, source_target_pairs={{0,1},{1,2},{2,3},{3,4},{4,5},{5,6},{6,7},{7,0},{8,9},{9,10},{10,1... | collective-permute-start | bytes 786440 | tf_op jit(solution)/shard_map/ppermute | solution.py:163
  121.7 3.3 %collective-permute-start.9 = (bf16[256,512]{1,0:T(8,128)(2,1)S(1)}, bf16[256,512]{1,0:T(8,128)(2,1)S(1)}, u32[]{:S(2)}, u32[]{:S(2)}) collective-permute-start(bf16[256,512]{1,0:T(8,128)(2,1)S(1)} %shard_map.58.refs_0_), channel_id=1, source_target_pairs={{0,7},{1,0},{2,1},{3,2},{4,3},{5,4},{6,5},{7,6},{8,15},{9,8},{10,9... | collective-permute-start | bytes 786440 | tf_op jit(solution)/shard_map/ppermute | solution.py:163
  125.0 3.8 %collective-permute-done.8.refs_1_ = bf16[256,512]{1,0:T(8,128)(2,1)S(1)} collective-permute-done((bf16[256,512]{1,0:T(8,128)(2,1)S(1)}, bf16[256,512]{1,0:T(8,128)(2,1)S(1)}, u32[]{:S(2)}, u32[]{:S(2)}) %collective-permute-start.8) | collective-permute-done | bytes 262176 | tf_op jit(solution)/shard_map/ppermute | solution.py:163
  128.8 2.5 %collective-permute-start.10 = (bf16[256,512]{1,0:T(8,128)(2,1)S(1)}, bf16[256,512]{1,0:T(8,128)(2,1)S(1)}, u32[]{:S(2)}, u32[]{:S(2)}) collective-permute-start(bf16[256,512]{1,0:T(8,128)(2,1)S(1)} %collective-permute-done.8.refs_1_), channel_id=1, source_target_pairs={{0,1},{1,2},{2,3},{3,4},{4,5},{5,6},{6,7},{7,0},{8,9},{9,10},{10,1... | collective-permute-start | bytes 786440 | tf_op jit(solution)/shard_map/ppermute | solution.py:163
  131.7 3.7 %collective-permute-start.11 = (bf16[256,512]{1,0:T(8,128)(2,1)S(1)}, bf16[256,512]{1,0:T(8,128)(2,1)S(1)}, u32[]{:S(2)}, u32[]{:S(2)}) collective-permute-start(bf16[256,512]{1,0:T(8,128)(2,1)S(1)} %collective-permute-done.9.refs_2_), channel_id=1, source_target_pairs={{0,7},{1,0},{2,1},{3,2},{4,3},{5,4},{6,5},{7,6},{8,15},{9,8},{10,9... | collective-permute-start | bytes 786440 | tf_op jit(solution)/shard_map/ppermute | solution.py:163
  135.4 4.4 %collective-permute-done.10.refs_3_ = bf16[256,512]{1,0:T(8,128)(2,1)S(1)} collective-permute-done((bf16[256,512]{1,0:T(8,128)(2,1)S(1)}, bf16[256,512]{1,0:T(8,128)(2,1)S(1)}, u32[]{:S(2)}, u32[]{:S(2)}) %collective-permute-start.10) | collective-permute-done | bytes 262176 | tf_op jit(solution)/shard_map/ppermute | solution.py:163
  142.7 4.5 %collective-permute-start.13 = (bf16[256,512]{1,0:T(8,128)(2,1)S(1)}, bf16[256,512]{1,0:T(8,128)(2,1)S(1)}, u32[]{:S(2)}, u32[]{:S(2)}) collective-permute-start(bf16[256,512]{1,0:T(8,128)(2,1)S(1)} %collective-permute-done.11.refs_4_), channel_id=1, source_target_pairs={{0,7},{1,0},{2,1},{3,2},{4,3},{5,4},{6,5},{7,6},{8,15},{9,8},{10,9... | collective-permute-start | bytes 786440 | tf_op jit(solution)/shard_map/ppermute | solution.py:163
  147.3 6.3 %collective-permute-start.14 = (bf16[128,512]{1,0:T(8,128)(2,1)S(1)}, bf16[128,512]{1,0:T(8,128)(2,1)S(1)}, u32[]{:S(2)}, u32[]{:S(2)}) collective-permute-start(bf16[128,512]{1,0:T(8,128)(2,1)S(1)} %slice.18), channel_id=1, source_target_pairs={{0,2},{1,3},{2,4},{3,5},{4,6},{5,7},{6,0},{7,1},{8,10},{9,11},{10,... | collective-permute-start | bytes 393224 | tf_op jit(solution)/shard_map/ppermute | solution.py:163
  155.7 2.9 %collective-permute-done.14.refs_7_ = bf16[128,512]{1,0:T(8,128)(2,1)S(1)} collective-permute-done((bf16[128,512]{1,0:T(8,128)(2,1)S(1)}, bf16[128,512]{1,0:T(8,128)(2,1)S(1)}, u32[]{:S(2)}, u32[]{:S(2)}) %collective-permute-start.14) | collective-permute-done | bytes 131104 | tf_op jit(solution)/shard_map/ppermute | solution.py:163
  158.6 3.1 %collective-permute-done.15.refs_8_ = bf16[128,512]{1,0:T(8,128)(2,1)S(1)} collective-permute-done((bf16[128,512]{1,0:T(8,128)(2,1)S(1)}, bf16[128,512]{1,0:T(8,128)(2,1)S(1)}, u32[]{:S(2)}, u32[]{:S(2)}) %collective-permute-start.15) | collective-permute-done | bytes 131104 | tf_op jit(solution)/shard_map/ppermute | solution.py:163
  161.7 7.1 %shard_map.59 = bf16[16,16,1024]{2,1,0:T(8,128)(2,1)S(1)} custom-call(s32[1]{0:T(128)} %bitcast.y_ref, bf16[256,512]{1,0:T(8,128)(2,1)S(1)} %shard_map.58.refs_0_, bf16[256,512]{1,0:T(8,128)(2,1)S(1)} %collective-permute-done.8.refs_1_, bf16[256,512]{1,0:T(8,128)(2,1)S(1)} %collective-permute-done.9.refs_2_, ...), custom_call_target="tpu_custom_call" | custom-call | flops 2147483648 | bytes 10485760 | tf_op jit(solution)/shard_map/pallas_call | solution.py:224
  168.8 31.9 %all_to_all.5.came_ref = bf16[16,16,1024]{2,1,0:T(8,128)(2,1)} all-to-all(bf16[16,16,1024]{2,1,0:T(8,128)(2,1)S(1)} %shard_map.59), channel_id=1, replica_groups=mesh['zl'=4,'x'=4,'core'=2,'zh'=2,'y'=8] {'zh','y'}, dimensions={0} | all-to-all | bytes 1048576 | tf_op jit(solution)/shard_map/all_to_all | solution.py:302
  (37 shorter events, 21.2 us)
Async XLA Ops:
  6.5 155.2 %all-gather.4.cloned.1.call-start = ((), (), s32[]{:S(2)}) async-start(), calls=%async_computation.1 | async-start | bytes 8650752 | tf_op jit(solution)/shard_map/all_gather | solution.py:272
  6.5 7.9 %collective-permute-start.16 = (bf16[512,256]{1,0:T(8,128)(2,1)}, bf16[512,256]{1,0:T(8,128)(2,1)S(1)}, u32[]{:S(2)}, u32[]{:S(2)}) collective-permute-start(bf16[512,256]{1,0:T(8,128)(2,1)} %param.9), channel_id=1, source_target_pairs={{0,0},{1,16},{2,32},{3,48},{4,64},{5,80},{6,96},{7,112},{16,1},{17... | collective-permute-start | bytes 786440 | tf_op jit(solution)/shard_map/ppermute | solution.py:271
  14.4 0.7 copy-start.1
  31.9 41.2 %collective-permute-start = (bf16[4,264,256]{2,1,0:T(8,128)(2,1)S(1)}, bf16[4,264,256]{2,1,0:T(8,128)(2,1)S(1)}, u32[]{:S(2)}, u32[]{:S(2)}) collective-permute-start(bf16[4,264,256]{2,1,0:T(8,128)(2,1)S(1)} %bitcast.6), channel_id=1, source_target_pairs={{0,32},{32,64},{64,96},{96,0},{1,33},{33,65},{65,97},{97,1},{2,34}... | collective-permute-start | bytes 1622024 | tf_op jit(solution)/shard_map/ppermute | solution.py:163
  50.4 29.0 %collective-permute-start.2 = (bf16[4,264,256]{2,1,0:T(8,128)(2,1)S(1)}, bf16[4,264,256]{2,1,0:T(8,128)(2,1)S(1)}, u32[]{:S(2)}, u32[]{:S(2)}) collective-permute-start(bf16[4,264,256]{2,1,0:T(8,128)(2,1)S(1)} %bitcast.7), channel_id=1, source_target_pairs={{0,96},{32,0},{64,32},{96,64},{1,97},{33,1},{65,33},{97,65},{2,98}... | collective-permute-start | bytes 1622024 | tf_op jit(solution)/shard_map/ppermute | solution.py:163
  73.1 15.9 %collective-permute-start.1 = (bf16[2,264,256]{2,1,0:T(8,128)(2,1)S(1)}, bf16[2,264,256]{2,1,0:T(8,128)(2,1)S(1)}, u32[]{:S(2)}, u32[]{:S(2)}) collective-permute-start(bf16[2,264,256]{2,1,0:T(8,128)(2,1)S(1)} %slice.16), channel_id=1, source_target_pairs={{0,32},{32,64},{64,96},{96,0},{1,33},{33,65},{65,97},{97,1},{2,34}... | collective-permute-start | bytes 811016 | tf_op jit(solution)/shard_map/ppermute | solution.py:163
  77.5 21.6 %collective-permute-start.7 = (bf16[4,264,256]{2,1,0:T(8,128)(2,1)S(1)}, bf16[4,264,256]{2,1,0:T(8,128)(2,1)S(1)}, u32[]{:S(2)}, u32[]{:S(2)}) collective-permute-start(bf16[4,264,256]{2,1,0:T(8,128)(2,1)S(1)} %bitcast.8), channel_id=1, source_target_pairs={{0,16},{16,0},{1,17},{17,1},{2,18},{18,2},{3,19},{19,3},{4,20},{20... | collective-permute-start | bytes 1622024 | tf_op jit(solution)/shard_map/ppermute | solution.py:163
  80.2 16.9 %collective-permute-start.3 = (bf16[2,264,256]{2,1,0:T(8,128)(2,1)}, bf16[2,264,256]{2,1,0:T(8,128)(2,1)S(1)}, u32[]{:S(2)}, u32[]{:S(2)}) collective-permute-start(bf16[2,264,256]{2,1,0:T(8,128)(2,1)} %slice.17), channel_id=1, source_target_pairs={{0,96},{32,0},{64,32},{96,64},{1,97},{33,1},{65,33},{97,65},{2,98}... | collective-permute-start | bytes 811016 | tf_op jit(solution)/shard_map/ppermute | solution.py:163
  84.6 21.2 %collective-permute-start.6 = (bf16[4,264,256]{2,1,0:T(8,128)(2,1)S(1)}, bf16[4,264,256]{2,1,0:T(8,128)(2,1)S(1)}, u32[]{:S(2)}, u32[]{:S(2)}) collective-permute-start(bf16[4,264,256]{2,1,0:T(8,128)(2,1)S(1)} %collective-permute-done.refs_0_), channel_id=1, source_target_pairs={{0,16},{16,0},{1,17},{17,1},{2,18},{18,2},{3,19},{19,3},{4,20},{20... | collective-permute-start | bytes 1622024 | tf_op jit(solution)/shard_map/ppermute | solution.py:163
  86.6 23.7 %collective-permute-start.5 = (bf16[4,264,256]{2,1,0:T(8,128)(2,1)S(1)}, bf16[4,264,256]{2,1,0:T(8,128)(2,1)S(1)}, u32[]{:S(2)}, u32[]{:S(2)}) collective-permute-start(bf16[4,264,256]{2,1,0:T(8,128)(2,1)S(1)} %collective-permute-done.2.refs_0_), channel_id=1, source_target_pairs={{0,16},{16,0},{1,17},{17,1},{2,18},{18,2},{3,19},{19,3},{4,20},{20... | collective-permute-start | bytes 1622024 | tf_op jit(solution)/shard_map/ppermute | solution.py:163
  97.0 17.7 %collective-permute-start.4 = (bf16[4,264,256]{2,1,0:T(8,128)(2,1)S(1)}, bf16[4,264,256]{2,1,0:T(8,128)(2,1)S(1)}, u32[]{:S(2)}, u32[]{:S(2)}) collective-permute-start(bf16[4,264,256]{2,1,0:T(8,128)(2,1)S(1)} %constant_dynamic-update-slice_fusion.refs_0_), channel_id=1, source_target_pairs={{0,16},{16,0},{1,17},{17,1},{2,18},{18,2},{3,19},{19,3},{4,20},{20... | collective-permute-start | bytes 1622024 | tf_op jit(solution)/shard_map/ppermute | solution.py:163
  99.2 1.0 copy-start
  119.1 9.7 %collective-permute-start.8 = (bf16[256,512]{1,0:T(8,128)(2,1)S(1)}, bf16[256,512]{1,0:T(8,128)(2,1)S(1)}, u32[]{:S(2)}, u32[]{:S(2)}) collective-permute-start(bf16[256,512]{1,0:T(8,128)(2,1)S(1)} %shard_map.58.refs_0_), channel_id=1, source_target_pairs={{0,1},{1,2},{2,3},{3,4},{4,5},{5,6},{6,7},{7,0},{8,9},{9,10},{10,1... | collective-permute-start | bytes 786440 | tf_op jit(solution)/shard_map/ppermute | solution.py:163
  121.7 10.1 %collective-permute-start.9 = (bf16[256,512]{1,0:T(8,128)(2,1)S(1)}, bf16[256,512]{1,0:T(8,128)(2,1)S(1)}, u32[]{:S(2)}, u32[]{:S(2)}) collective-permute-start(bf16[256,512]{1,0:T(8,128)(2,1)S(1)} %shard_map.58.refs_0_), channel_id=1, source_target_pairs={{0,7},{1,0},{2,1},{3,2},{4,3},{5,4},{6,5},{7,6},{8,15},{9,8},{10,9... | collective-permute-start | bytes 786440 | tf_op jit(solution)/shard_map/ppermute | solution.py:163
  128.8 11.0 %collective-permute-start.10 = (bf16[256,512]{1,0:T(8,128)(2,1)S(1)}, bf16[256,512]{1,0:T(8,128)(2,1)S(1)}, u32[]{:S(2)}, u32[]{:S(2)}) collective-permute-start(bf16[256,512]{1,0:T(8,128)(2,1)S(1)} %collective-permute-done.8.refs_1_), channel_id=1, source_target_pairs={{0,1},{1,2},{2,3},{3,4},{4,5},{5,6},{6,7},{7,0},{8,9},{9,10},{10,1... | collective-permute-start | bytes 786440 | tf_op jit(solution)/shard_map/ppermute | solution.py:163
  131.7 11.0 %collective-permute-start.11 = (bf16[256,512]{1,0:T(8,128)(2,1)S(1)}, bf16[256,512]{1,0:T(8,128)(2,1)S(1)}, u32[]{:S(2)}, u32[]{:S(2)}) collective-permute-start(bf16[256,512]{1,0:T(8,128)(2,1)S(1)} %collective-permute-done.9.refs_2_), channel_id=1, source_target_pairs={{0,7},{1,0},{2,1},{3,2},{4,3},{5,4},{6,5},{7,6},{8,15},{9,8},{10,9... | collective-permute-start | bytes 786440 | tf_op jit(solution)/shard_map/ppermute | solution.py:163
  139.8 21.8 %collective-permute-start.12 = (bf16[256,512]{1,0:T(8,128)(2,1)S(1)}, bf16[256,512]{1,0:T(8,128)(2,1)S(1)}, u32[]{:S(2)}, u32[]{:S(2)}) collective-permute-start(bf16[256,512]{1,0:T(8,128)(2,1)S(1)} %collective-permute-done.10.refs_3_), channel_id=1, source_target_pairs={{0,1},{1,2},{2,3},{3,4},{4,5},{5,6},{6,7},{7,0},{8,9},{9,10},{10,1... | collective-permute-start | bytes 786440 | tf_op jit(solution)/shard_map/ppermute | solution.py:163
  142.7 18.9 %collective-permute-start.13 = (bf16[256,512]{1,0:T(8,128)(2,1)S(1)}, bf16[256,512]{1,0:T(8,128)(2,1)S(1)}, u32[]{:S(2)}, u32[]{:S(2)}) collective-permute-start(bf16[256,512]{1,0:T(8,128)(2,1)S(1)} %collective-permute-done.11.refs_4_), channel_id=1, source_target_pairs={{0,7},{1,0},{2,1},{3,2},{4,3},{5,4},{6,5},{7,6},{8,15},{9,8},{10,9... | collective-permute-start | bytes 786440 | tf_op jit(solution)/shard_map/ppermute | solution.py:163
  147.3 11.3 %collective-permute-start.14 = (bf16[128,512]{1,0:T(8,128)(2,1)S(1)}, bf16[128,512]{1,0:T(8,128)(2,1)S(1)}, u32[]{:S(2)}, u32[]{:S(2)}) collective-permute-start(bf16[128,512]{1,0:T(8,128)(2,1)S(1)} %slice.18), channel_id=1, source_target_pairs={{0,2},{1,3},{2,4},{3,5},{4,6},{5,7},{6,0},{7,1},{8,10},{9,11},{10,... | collective-permute-start | bytes 393224 | tf_op jit(solution)/shard_map/ppermute | solution.py:163
  153.6 8.1 %collective-permute-start.15 = (bf16[128,512]{1,0:T(8,128)(2,1)S(1)}, bf16[128,512]{1,0:T(8,128)(2,1)S(1)}, u32[]{:S(2)}, u32[]{:S(2)}) collective-permute-start(bf16[128,512]{1,0:T(8,128)(2,1)S(1)} %slice.19), channel_id=1, source_target_pairs={{0,6},{1,7},{2,0},{3,1},{4,2},{5,3},{6,4},{7,5},{8,14},{9,15},{10,... | collective-permute-start | bytes 393224 | tf_op jit(solution)/shard_map/ppermute | solution.py:163
Sparse Core Ops, SparseCore 0:
  15.3 100.2 all-gather.3

commit v3 on v2

--- a/solution.py
+++ b/solution.py
@@ -16,12 +16,11 @@
 CTX = ("zl", "x", "core")
 TP = ("zh", "y")
 PAD = 8
-GROUP = 1
 NEG = -1e30
 SCALE2 = math.log2(math.e) / math.sqrt(HD)
 
 
-def attend_kernel(group, sources, first, last, where_ref, q_ref, docs_ref, *refs):
+def attend_kernel(sources, first, last, where_ref, q_ref, docs_ref, *refs):
     n = len(sources)
     pieces = refs[: 2 * n]
     refs = refs[2 * n :]
@@ -29,9 +28,9 @@
         m_in, acc_in = refs[:2]
         refs = refs[2:]
     if last:
-        out_ref, m_ref, acc_ref, stack_ref = refs
+        out_ref, m_ref, acc_ref = refs
     else:
-        m_ref, acc_ref, stack_ref = refs
+        m_ref, acc_ref = refs
     rows = q_ref.shape[0]
     heads = q_ref.shape[1] // HD
     my_z, my_x, my_core = where_ref[0], where_ref[1], where_ref[2]
@@ -42,28 +41,43 @@
     else:
         m_ref[...] = m_in[...]
         acc_ref[...] = acc_in[...]
-    for h in range(heads):
-        stack_ref[h * rows : (h + 1) * rows, :] = q_ref[:, h * HD : (h + 1) * HD]
     q_docs = docs_ref[...]
-    q_first, q_last = jnp.min(q_docs), jnp.max(q_docs)
+    q_first, q_last = jnp.min(q_docs[:PAD]), jnp.max(q_docs[rows - PAD :])
     ones = jnp.ones((rows, HD), jnp.bfloat16)
     wide = rows // HD
 
+    def extent(own, other, z):
+        head, tail = [
+            [ref[z, rows : rows + PAD, lanes].astype(jnp.float32) for ref in (own, other)]
+            for lanes in (slice(0, HD), slice(rows - HD, rows))
+        ]
+        return jnp.min(jnp.minimum(*head)), jnp.max(jnp.maximum(*tail))
+
+    extents = [
+        [extent(pieces[2 * at], pieces[2 * at + 1], z) for z in range(ZL)] for at in range(n)
+    ]
     for at, offset in enumerate(sources):
         own, other = pieces[2 * at], pieces[2 * at + 1]
         their_x = lax.rem(my_x + offset, X)
-
-        def block(z, carry, own=own, other=other, their_x=their_x):
+        firsts = [low for low, _ in extents[at]]
+        lasts = [high for _, high in extents[at]]
+
+        def pick(values, z):
+            value = values[0]
+            for index in range(1, ZL):
+                value = jnp.where(z == index, values[index], value)
+            return value
+
+        def block(z, carry, own=own, other=other, their_x=their_x, firsts=firsts, lasts=lasts):
             their_block = z * X + their_x
-            docs_own = own[z, rows : rows + PAD, :].astype(jnp.float32)
-            docs_other = other[z, rows : rows + PAD, :].astype(jnp.float32)
-            k_first = jnp.min(jnp.minimum(docs_own, docs_other))
-            k_last = jnp.max(jnp.maximum(docs_own, docs_other))
+            k_first, k_last = pick(firsts, z), pick(lasts, z)
             needed = (their_block <= my_block) & (k_last >= q_first)
             whole = needed & (their_block < my_block) & (k_first >= q_last)
 
             def update(masked):
                 if masked:
+                    docs_own = own[z, rows : rows + PAD, :].astype(jnp.float32)
+                    docs_other = other[z, rows : rows + PAD, :].astype(jnp.float32)
                     row = lax.broadcasted_iota(jnp.int32, (rows, rows), 0)
                     lane = lax.broadcasted_iota(jnp.int32, (rows, rows), 1)
                     q_pos = my_block * (2 * rows) + my_core * rows + row
@@ -73,16 +87,14 @@
                         same = jnp.broadcast_to(docs[:1], (rows, rows)) == jnp.concatenate(
                             [q_docs] * wide, axis=1
                         )
-                        one = same & (k_pos + side * rows <= q_pos)
-                        one = jnp.where(one, 1.0, 0.0)
-                        allowed.append(jnp.concatenate([one] * group, axis=0) > 0.5)
+                        allowed.append(same & (k_pos + side * rows <= q_pos))
                 keys = [ref[z, :rows, :HD] for ref in (own, other)]
                 values = [
                     jnp.concatenate([ref[z, :rows, HD:], ones], axis=1) for ref in (own, other)
                 ]
-                for g in range(heads // group):
-                    these = slice(g * group * rows, (g + 1) * group * rows)
-                    q = stack_ref[these, :]
+
+                def score(h):
+                    q = q_ref[:, h * HD : (h + 1) * HD]
                     scores = [
                         lax.dot_general(
                             q, k, (((1,), (1,)), ((), ())), preferred_element_type=jnp.float32
@@ -91,6 +103,14 @@
                     ]
                     if masked:
                         scores = [jnp.where(a, s, NEG) for a, s in zip(allowed, scores)]
+                    return scores
+
+                ahead = score(0)
+                for h in range(heads):
+                    these = slice(h * rows, (h + 1) * rows)
+                    scores = ahead
+                    if h + 1 < heads:
+                        ahead = score(h + 1)
                     old = m_ref[these, :]
                     top = jnp.max(jnp.maximum(scores[0], scores[1]), axis=1, keepdims=True)
                     new = jnp.maximum(old, top)
@@ -132,7 +152,7 @@
             ).astype(jnp.bfloat16)
 
 
-def attend(where, q, docs, pieces, sources, state, last, group=GROUP):
+def attend(where, q, docs, pieces, sources, state, last):
     rows, width = q.shape
     heads = width // HD
     first = state is None
@@ -144,12 +164,11 @@
     inputs = [q, docs, *pieces] + ([] if first else list(state))
     blocks = ZL * len(sources)
     return pl.pallas_call(
-        functools.partial(attend_kernel, group, sources, first, last),
+        functools.partial(attend_kernel, sources, first, last),
         out_shape=jax.ShapeDtypeStruct((rows, width), jnp.bfloat16) if last else states,
         in_specs=[pl.BlockSpec(memory_space=pltpu.SMEM)] + [vmem] * len(inputs),
         out_specs=vmem if last else (vmem, vmem),
-        scratch_shapes=([pltpu.VMEM(s.shape, s.dtype) for s in states] if last else [])
-        + [pltpu.VMEM((heads * rows, HD), jnp.bfloat16)],
+        scratch_shapes=[pltpu.VMEM(s.shape, s.dtype) for s in states] if last else [],
         compiler_params=pltpu.CompilerParams(vmem_limit_bytes=40 << 20),
         cost_estimate=pl.CostEstimate(
             flops=blocks * heads * rows * 2 * rows * HD * 6,

time: 210 us -> 206 us (0.981)
  Pallas kernels: 27.9 us -> 25.1 us
    pallas_call x4, Pallas kernels: 19 us -> 16.2 us  [attend(): pl.pallas_call(functools.partial(attend_kernel, sources, first, last), ou...]
  transfers between devices with their start and end apart: 18 -> 18, of which waited for: 9 -> 9; matrix products, arithmetic and copies ran while one was open for 1% -> 1% of each run, Pallas kernels for 9% -> 8%
where the time goes in v3:
time: 206 us; the launch traced here: 205 us
  starting transfers between devices  65.4 us (32%)
  waiting for transfers between devices  51.2 us (25%)
  blocking collectives  45.7 us (22%)
  Pallas kernels  25.1 us (12%)
  between operations  13.7 us (7%)
  local copies, waits for them, and re-layouts  3.44 us (2%)
    ppermute x16, starting transfers between devices, around(): lax.ppermute(value, axis, [(i, (i + step) % size) for i in range(size)])  63.5 us
    ppermute x16, waiting for transfers between devices, around(): lax.ppermute(value, axis, [(i, (i + step) % size) for i in range(size)])  45.2 us
    all_to_all x1, blocking collectives, compute(): came = lax.all_to_all(terms, TP, split_axis=0, concat_axis=0, tiled=True)  30.7 us
    pallas_call x4, Pallas kernels, attend(): pl.pallas_call(functools.partial(attend_kernel, sources, first, last), ou...  16.2 us
    all_gather x1, blocking collectives, compute(): mine = lax.all_gather(packed, 'zl', axis=0)  15 us
    pallas_call x1, Pallas kernels, project(): pl.pallas_call(functools.partial(project_kernel, offsets), out_shape=jax....  7.12 us
    ppermute x1, waiting for transfers between devices, compute(): swapped = lax.ppermute(out_weight, ('x', 'core', 'y'), swap)  5.97 us
  transfers between devices with their start and end apart: 18, of which 9 were waited for; matrix products, arithmetic and copies ran while one was open for 1% of the time, Pallas kernels for 8%

profile of v3, /device:TPU:200, one launch (start us, length us, event | category | flops | bytes accessed | tf_op | source)
XLA Modules:
  0.0 205.4 jit_solution(584962101899633685)
XLA Ops:
  8.5 6.0 %collective-permute-done.16 = bf16[512,256]{1,0:T(8,128)(2,1)S(1)} collective-permute-done((bf16[512,256]{1,0:T(8,128)(2,1)}, bf16[512,256]{1,0:T(8,128)(2,1)S(1)}, u32[]{:S(2)}, u32[]{:S(2)}) %collective-permute-start.16) | collective-permute-done | bytes 262176 | tf_op jit(solution)/shard_map/ppermute | solution.py:290
  16.9 15.0 %all-gather = bf16[1056,256]{1,0:T(8,128)(2,1)S(1)} all-gather(bf16[264,256]{1,0:T(8,128)(2,1)S(1)} %pad_maximum_fusion), channel_id=2, replica_groups=mesh['zl'=4,'x'=4,'core'=2,'zh'=2,'y'=8] {'zl'}, dimensions={0}, use_global_device_ids=true | all-gather | bytes 675840 | tf_op jit(solution)/shard_map/all_gather | solution.py:303
  31.9 18.6 %collective-permute-start = (bf16[4,264,256]{2,1,0:T(8,128)(2,1)S(1)}, bf16[4,264,256]{2,1,0:T(8,128)(2,1)S(1)}, u32[]{:S(2)}, u32[]{:S(2)}) collective-permute-start(bf16[4,264,256]{2,1,0:T(8,128)(2,1)S(1)} %bitcast.6), channel_id=1, source_target_pairs={{0,32},{32,64},{64,96},{96,0},{1,33},{33,65},{65,97},{97,1},{2,34}... | collective-permute-start | bytes 1622024 | tf_op jit(solution)/shard_map/ppermute | solution.py:182
  52.4 20.7 %collective-permute-done.refs_0_ = bf16[4,264,256]{2,1,0:T(8,128)(2,1)S(1)} collective-permute-done((bf16[4,264,256]{2,1,0:T(8,128)(2,1)S(1)}, bf16[4,264,256]{2,1,0:T(8,128)(2,1)S(1)}, u32[]{:S(2)}, u32[]{:S(2)}) %collective-permute-start) | collective-permute-done | bytes 540704 | tf_op jit(solution)/shard_map/ppermute | solution.py:182
  73.1 4.4 %collective-permute-start.1 = (bf16[2,264,256]{2,1,0:T(8,128)(2,1)S(1)}, bf16[2,264,256]{2,1,0:T(8,128)(2,1)S(1)}, u32[]{:S(2)}, u32[]{:S(2)}) collective-permute-start(bf16[2,264,256]{2,1,0:T(8,128)(2,1)S(1)} %slice.16), channel_id=1, source_target_pairs={{0,32},{32,64},{64,96},{96,0},{1,33},{33,65},{65,97},{97,1},{2,34}... | collective-permute-start | bytes 811016 | tf_op jit(solution)/shard_map/ppermute | solution.py:182
  80.2 4.5 %collective-permute-start.3 = (bf16[2,264,256]{2,1,0:T(8,128)(2,1)}, bf16[2,264,256]{2,1,0:T(8,128)(2,1)S(1)}, u32[]{:S(2)}, u32[]{:S(2)}) collective-permute-start(bf16[2,264,256]{2,1,0:T(8,128)(2,1)} %slice.17), channel_id=1, source_target_pairs={{0,96},{32,0},{64,32},{96,64},{1,97},{33,1},{65,33},{97,65},{2,98}... | collective-permute-start | bytes 811016 | tf_op jit(solution)/shard_map/ppermute | solution.py:182
  89.0 8.0 %collective-permute-done.3 = bf16[2,264,256]{2,1,0:T(8,128)(2,1)S(1)} collective-permute-done((bf16[2,264,256]{2,1,0:T(8,128)(2,1)}, bf16[2,264,256]{2,1,0:T(8,128)(2,1)S(1)}, u32[]{:S(2)}, u32[]{:S(2)}) %collective-permute-start.3) | collective-permute-done | bytes 270368 | tf_op jit(solution)/shard_map/ppermute | solution.py:182
  100.1 4.9 %shard_map.55 = (f32[1024,128]{1,0:T(8,128)S(1)}, f32[1024,256]{1,0:T(8,128)S(1)}) custom-call(s32[3]{0:T(128)S(1)} %pad_add_fusion.where_ref, bf16[256,512]{1,0:T(8,128)(2,1)S(1)} %copy-done, f32[256,128]{1,0:T(8,128)S(1)} %broadcast_in_dim.4.docs_ref, bf16[4,264,256]{2,1,0:T(8,128)(2,1)S(1)} %bitcast.9, bf16[4,264,256]{2,1,0:T(8,128)(2,1)S(1)} %collective-permute-done.7.refs_1_), custom_call_target="tpu_custom_call" | custom-call | flops 1610612736 | bytes 1048576 | tf_op jit(solution)/shard_map/pallas_call | solution.py:166
  105.1 3.7 %shard_map.56 = (f32[1024,128]{1,0:T(8,128)S(1)}, f32[1024,256]{1,0:T(8,128)S(1)}) custom-call(s32[3]{0:T(128)S(1)} %pad_add_fusion.where_ref, bf16[256,512]{1,0:T(8,128)(2,1)S(1)} %copy-done, f32[256,128]{1,0:T(8,128)S(1)} %broadcast_in_dim.4.docs_ref, bf16[4,264,256]{2,1,0:T(8,128)(2,1)S(1)} %collective-permute-done.refs_0_, ...), custom_call_target="tpu_custom_call" | custom-call | flops 1610612736 | bytes 1048576 | tf_op jit(solution)/shard_map/pallas_call | solution.py:166
  108.8 3.8 %shard_map.57 = (f32[1024,128]{1,0:T(8,128)S(1)}, f32[1024,256]{1,0:T(8,128)S(1)}) custom-call(s32[3]{0:T(128)S(1)} %pad_add_fusion.where_ref, bf16[256,512]{1,0:T(8,128)(2,1)S(1)} %copy-done, f32[256,128]{1,0:T(8,128)S(1)} %broadcast_in_dim.4.docs_ref, bf16[4,264,256]{2,1,0:T(8,128)(2,1)S(1)} %collective-permute-done.2.refs_0_, ...), custom_call_target="tpu_custom_call" | custom-call | flops 1610612736 | bytes 1048576 | tf_op jit(solution)/shard_map/pallas_call | solution.py:166
  112.6 3.7 %shard_map.58.refs_0_ = bf16[256,512]{1,0:T(8,128)(2,1)S(1)} custom-call(s32[3]{0:T(128)S(1)} %pad_add_fusion.where_ref, bf16[256,512]{1,0:T(8,128)(2,1)S(1)} %copy-done, f32[256,128]{1,0:T(8,128)S(1)} %broadcast_in_dim.4.docs_ref, bf16[4,264,256]{2,1,0:T(8,128)(2,1)S(1)} %constant_dynamic-update-slice_fusion.refs_0_, ...), custom_call_target="tpu_custom_call" | custom-call | flops 1610612736 | bytes 1048576 | tf_op jit(solution)/shard_map/pallas_call | solution.py:166
  116.3 2.5 %collective-permute-start.8 = (bf16[256,512]{1,0:T(8,128)(2,1)S(1)}, bf16[256,512]{1,0:T(8,128)(2,1)S(1)}, u32[]{:S(2)}, u32[]{:S(2)}) collective-permute-start(bf16[256,512]{1,0:T(8,128)(2,1)S(1)} %shard_map.58.refs_0_), channel_id=1, source_target_pairs={{0,1},{1,2},{2,3},{3,4},{4,5},{5,6},{6,7},{7,0},{8,9},{9,10},{10,1... | collective-permute-start | bytes 786440 | tf_op jit(solution)/shard_map/ppermute | solution.py:182
  118.9 3.3 %collective-permute-start.9 = (bf16[256,512]{1,0:T(8,128)(2,1)S(1)}, bf16[256,512]{1,0:T(8,128)(2,1)S(1)}, u32[]{:S(2)}, u32[]{:S(2)}) collective-permute-start(bf16[256,512]{1,0:T(8,128)(2,1)S(1)} %shard_map.58.refs_0_), channel_id=1, source_target_pairs={{0,7},{1,0},{2,1},{3,2},{4,3},{5,4},{6,5},{7,6},{8,15},{9,8},{10,9... | collective-permute-start | bytes 786440 | tf_op jit(solution)/shard_map/ppermute | solution.py:182
  122.2 4.9 %collective-permute-done.8.refs_1_ = bf16[256,512]{1,0:T(8,128)(2,1)S(1)} collective-permute-done((bf16[256,512]{1,0:T(8,128)(2,1)S(1)}, bf16[256,512]{1,0:T(8,128)(2,1)S(1)}, u32[]{:S(2)}, u32[]{:S(2)}) %collective-permute-start.8) | collective-permute-done | bytes 262176 | tf_op jit(solution)/shard_map/ppermute | solution.py:182
  127.1 2.5 %collective-permute-start.10 = (bf16[256,512]{1,0:T(8,128)(2,1)S(1)}, bf16[256,512]{1,0:T(8,128)(2,1)S(1)}, u32[]{:S(2)}, u32[]{:S(2)}) collective-permute-start(bf16[256,512]{1,0:T(8,128)(2,1)S(1)} %collective-permute-done.8.refs_1_), channel_id=1, source_target_pairs={{0,1},{1,2},{2,3},{3,4},{4,5},{5,6},{6,7},{7,0},{8,9},{9,10},{10,1... | collective-permute-start | bytes 786440 | tf_op jit(solution)/shard_map/ppermute | solution.py:182
  129.9 3.7 %collective-permute-start.11 = (bf16[256,512]{1,0:T(8,128)(2,1)S(1)}, bf16[256,512]{1,0:T(8,128)(2,1)S(1)}, u32[]{:S(2)}, u32[]{:S(2)}) collective-permute-start(bf16[256,512]{1,0:T(8,128)(2,1)S(1)} %collective-permute-done.9.refs_2_), channel_id=1, source_target_pairs={{0,7},{1,0},{2,1},{3,2},{4,3},{5,4},{6,5},{7,6},{8,15},{9,8},{10,9... | collective-permute-start | bytes 786440 | tf_op jit(solution)/shard_map/ppermute | solution.py:182
  133.7 5.0 %collective-permute-done.10.refs_3_ = bf16[256,512]{1,0:T(8,128)(2,1)S(1)} collective-permute-done((bf16[256,512]{1,0:T(8,128)(2,1)S(1)}, bf16[256,512]{1,0:T(8,128)(2,1)S(1)}, u32[]{:S(2)}, u32[]{:S(2)}) %collective-permute-start.10) | collective-permute-done | bytes 262176 | tf_op jit(solution)/shard_map/ppermute | solution.py:182
  141.6 3.9 %collective-permute-start.13 = (bf16[256,512]{1,0:T(8,128)(2,1)S(1)}, bf16[256,512]{1,0:T(8,128)(2,1)S(1)}, u32[]{:S(2)}, u32[]{:S(2)}) collective-permute-start(bf16[256,512]{1,0:T(8,128)(2,1)S(1)} %collective-permute-done.11.refs_4_), channel_id=1, source_target_pairs={{0,7},{1,0},{2,1},{3,2},{4,3},{5,4},{6,5},{7,6},{8,15},{9,8},{10,9... | collective-permute-start | bytes 786440 | tf_op jit(solution)/shard_map/ppermute | solution.py:182
  145.5 5.5 %collective-permute-start.14 = (bf16[128,512]{1,0:T(8,128)(2,1)S(1)}, bf16[128,512]{1,0:T(8,128)(2,1)S(1)}, u32[]{:S(2)}, u32[]{:S(2)}) collective-permute-start(bf16[128,512]{1,0:T(8,128)(2,1)S(1)} %slice.18), channel_id=1, source_target_pairs={{0,2},{1,3},{2,4},{3,5},{4,6},{5,7},{6,0},{7,1},{8,10},{9,11},{10,... | collective-permute-start | bytes 393224 | tf_op jit(solution)/shard_map/ppermute | solution.py:182
  151.0 2.7 %collective-permute-start.15 = (bf16[128,512]{1,0:T(8,128)(2,1)S(1)}, bf16[128,512]{1,0:T(8,128)(2,1)S(1)}, u32[]{:S(2)}, u32[]{:S(2)}) collective-permute-start(bf16[128,512]{1,0:T(8,128)(2,1)S(1)} %slice.19), channel_id=1, source_target_pairs={{0,6},{1,7},{2,0},{3,1},{4,2},{5,3},{6,4},{7,5},{8,14},{9,15},{10,... | collective-permute-start | bytes 393224 | tf_op jit(solution)/shard_map/ppermute | solution.py:182
  153.7 2.4 %collective-permute-done.14.refs_7_ = bf16[128,512]{1,0:T(8,128)(2,1)S(1)} collective-permute-done((bf16[128,512]{1,0:T(8,128)(2,1)S(1)}, bf16[128,512]{1,0:T(8,128)(2,1)S(1)}, u32[]{:S(2)}, u32[]{:S(2)}) %collective-permute-start.14) | collective-permute-done | bytes 131104 | tf_op jit(solution)/shard_map/ppermute | solution.py:182
  156.1 2.7 %collective-permute-done.15.refs_8_ = bf16[128,512]{1,0:T(8,128)(2,1)S(1)} collective-permute-done((bf16[128,512]{1,0:T(8,128)(2,1)S(1)}, bf16[128,512]{1,0:T(8,128)(2,1)S(1)}, u32[]{:S(2)}, u32[]{:S(2)}) %collective-permute-start.15) | collective-permute-done | bytes 131104 | tf_op jit(solution)/shard_map/ppermute | solution.py:182
  158.9 7.1 %shard_map.59 = bf16[16,16,1024]{2,1,0:T(8,128)(2,1)S(1)} custom-call(s32[1]{0:T(128)} %bitcast.y_ref, bf16[256,512]{1,0:T(8,128)(2,1)S(1)} %shard_map.58.refs_0_, bf16[256,512]{1,0:T(8,128)(2,1)S(1)} %collective-permute-done.8.refs_1_, bf16[256,512]{1,0:T(8,128)(2,1)S(1)} %collective-permute-done.9.refs_2_, ...), custom_call_target="tpu_custom_call" | custom-call | flops 2147483648 | bytes 10485760 | tf_op jit(solution)/shard_map/pallas_call | solution.py:243
  166.0 30.7 %all_to_all.5.came_ref = bf16[16,16,1024]{2,1,0:T(8,128)(2,1)} all-to-all(bf16[16,16,1024]{2,1,0:T(8,128)(2,1)S(1)} %shard_map.59), channel_id=1, replica_groups=mesh['zl'=4,'x'=4,'core'=2,'zh'=2,'y'=8] {'zh','y'}, dimensions={0} | all-to-all | bytes 1048576 | tf_op jit(solution)/shard_map/all_to_all | solution.py:321
  (37 shorter events, 21.5 us)
Async XLA Ops:
  6.5 152.3 %all-gather.4.cloned.1.call-start = ((), (), s32[]{:S(2)}) async-start(), calls=%async_computation.1 | async-start | bytes 8650752 | tf_op jit(solution)/shard_map/all_gather | solution.py:291
  6.5 7.9 %collective-permute-start.16 = (bf16[512,256]{1,0:T(8,128)(2,1)}, bf16[512,256]{1,0:T(8,128)(2,1)S(1)}, u32[]{:S(2)}, u32[]{:S(2)}) collective-permute-start(bf16[512,256]{1,0:T(8,128)(2,1)} %param.9), channel_id=1, source_target_pairs={{0,0},{1,16},{2,32},{3,48},{4,64},{5,80},{6,96},{7,112},{16,1},{17... | collective-permute-start | bytes 786440 | tf_op jit(solution)/shard_map/ppermute | solution.py:290
  14.4 0.7 copy-start.1
  31.9 41.2 %collective-permute-start = (bf16[4,264,256]{2,1,0:T(8,128)(2,1)S(1)}, bf16[4,264,256]{2,1,0:T(8,128)(2,1)S(1)}, u32[]{:S(2)}, u32[]{:S(2)}) collective-permute-start(bf16[4,264,256]{2,1,0:T(8,128)(2,1)S(1)} %bitcast.6), channel_id=1, source_target_pairs={{0,32},{32,64},{64,96},{96,0},{1,33},{33,65},{65,97},{97,1},{2,34}... | collective-permute-start | bytes 1622024 | tf_op jit(solution)/shard_map/ppermute | solution.py:182
  50.4 29.0 %collective-permute-start.2 = (bf16[4,264,256]{2,1,0:T(8,128)(2,1)S(1)}, bf16[4,264,256]{2,1,0:T(8,128)(2,1)S(1)}, u32[]{:S(2)}, u32[]{:S(2)}) collective-permute-start(bf16[4,264,256]{2,1,0:T(8,128)(2,1)S(1)} %bitcast.7), channel_id=1, source_target_pairs={{0,96},{32,0},{64,32},{96,64},{1,97},{33,1},{65,33},{97,65},{2,98}... | collective-permute-start | bytes 1622024 | tf_op jit(solution)/shard_map/ppermute | solution.py:182
  73.1 15.9 %collective-permute-start.1 = (bf16[2,264,256]{2,1,0:T(8,128)(2,1)S(1)}, bf16[2,264,256]{2,1,0:T(8,128)(2,1)S(1)}, u32[]{:S(2)}, u32[]{:S(2)}) collective-permute-start(bf16[2,264,256]{2,1,0:T(8,128)(2,1)S(1)} %slice.16), channel_id=1, source_target_pairs={{0,32},{32,64},{64,96},{96,0},{1,33},{33,65},{65,97},{97,1},{2,34}... | collective-permute-start | bytes 811016 | tf_op jit(solution)/shard_map/ppermute | solution.py:182
  77.5 21.6 %collective-permute-start.7 = (bf16[4,264,256]{2,1,0:T(8,128)(2,1)S(1)}, bf16[4,264,256]{2,1,0:T(8,128)(2,1)S(1)}, u32[]{:S(2)}, u32[]{:S(2)}) collective-permute-start(bf16[4,264,256]{2,1,0:T(8,128)(2,1)S(1)} %bitcast.8), channel_id=1, source_target_pairs={{0,16},{16,0},{1,17},{17,1},{2,18},{18,2},{3,19},{19,3},{4,20},{20... | collective-permute-start | bytes 1622024 | tf_op jit(solution)/shard_map/ppermute | solution.py:182
  80.2 16.9 %collective-permute-start.3 = (bf16[2,264,256]{2,1,0:T(8,128)(2,1)}, bf16[2,264,256]{2,1,0:T(8,128)(2,1)S(1)}, u32[]{:S(2)}, u32[]{:S(2)}) collective-permute-start(bf16[2,264,256]{2,1,0:T(8,128)(2,1)} %slice.17), channel_id=1, source_target_pairs={{0,96},{32,0},{64,32},{96,64},{1,97},{33,1},{65,33},{97,65},{2,98}... | collective-permute-start | bytes 811016 | tf_op jit(solution)/shard_map/ppermute | solution.py:182
  84.6 20.4 %collective-permute-start.6 = (bf16[4,264,256]{2,1,0:T(8,128)(2,1)S(1)}, bf16[4,264,256]{2,1,0:T(8,128)(2,1)S(1)}, u32[]{:S(2)}, u32[]{:S(2)}) collective-permute-start(bf16[4,264,256]{2,1,0:T(8,128)(2,1)S(1)} %collective-permute-done.refs_0_), channel_id=1, source_target_pairs={{0,16},{16,0},{1,17},{17,1},{2,18},{18,2},{3,19},{19,3},{4,20},{20... | collective-permute-start | bytes 1622024 | tf_op jit(solution)/shard_map/ppermute | solution.py:182
  86.6 22.2 %collective-permute-start.5 = (bf16[4,264,256]{2,1,0:T(8,128)(2,1)S(1)}, bf16[4,264,256]{2,1,0:T(8,128)(2,1)S(1)}, u32[]{:S(2)}, u32[]{:S(2)}) collective-permute-start(bf16[4,264,256]{2,1,0:T(8,128)(2,1)S(1)} %collective-permute-done.2.refs_0_), channel_id=1, source_target_pairs={{0,16},{16,0},{1,17},{17,1},{2,18},{18,2},{3,19},{19,3},{4,20},{20... | collective-permute-start | bytes 1622024 | tf_op jit(solution)/shard_map/ppermute | solution.py:182
  97.0 15.6 %collective-permute-start.4 = (bf16[4,264,256]{2,1,0:T(8,128)(2,1)S(1)}, bf16[4,264,256]{2,1,0:T(8,128)(2,1)S(1)}, u32[]{:S(2)}, u32[]{:S(2)}) collective-permute-start(bf16[4,264,256]{2,1,0:T(8,128)(2,1)S(1)} %constant_dynamic-update-slice_fusion.refs_0_), channel_id=1, source_target_pairs={{0,16},{16,0},{1,17},{17,1},{2,18},{18,2},{3,19},{19,3},{4,20},{20... | collective-permute-start | bytes 1622024 | tf_op jit(solution)/shard_map/ppermute | solution.py:182
  99.2 1.0 copy-start
  116.3 10.7 %collective-permute-start.8 = (bf16[256,512]{1,0:T(8,128)(2,1)S(1)}, bf16[256,512]{1,0:T(8,128)(2,1)S(1)}, u32[]{:S(2)}, u32[]{:S(2)}) collective-permute-start(bf16[256,512]{1,0:T(8,128)(2,1)S(1)} %shard_map.58.refs_0_), channel_id=1, source_target_pairs={{0,1},{1,2},{2,3},{3,4},{4,5},{5,6},{6,7},{7,0},{8,9},{9,10},{10,1... | collective-permute-start | bytes 786440 | tf_op jit(solution)/shard_map/ppermute | solution.py:182
  118.9 11.1 %collective-permute-start.9 = (bf16[256,512]{1,0:T(8,128)(2,1)S(1)}, bf16[256,512]{1,0:T(8,128)(2,1)S(1)}, u32[]{:S(2)}, u32[]{:S(2)}) collective-permute-start(bf16[256,512]{1,0:T(8,128)(2,1)S(1)} %shard_map.58.refs_0_), channel_id=1, source_target_pairs={{0,7},{1,0},{2,1},{3,2},{4,3},{5,4},{6,5},{7,6},{8,15},{9,8},{10,9... | collective-permute-start | bytes 786440 | tf_op jit(solution)/shard_map/ppermute | solution.py:182
  127.1 11.6 %collective-permute-start.10 = (bf16[256,512]{1,0:T(8,128)(2,1)S(1)}, bf16[256,512]{1,0:T(8,128)(2,1)S(1)}, u32[]{:S(2)}, u32[]{:S(2)}) collective-permute-start(bf16[256,512]{1,0:T(8,128)(2,1)S(1)} %collective-permute-done.8.refs_1_), channel_id=1, source_target_pairs={{0,1},{1,2},{2,3},{3,4},{4,5},{5,6},{6,7},{7,0},{8,9},{9,10},{10,1... | collective-permute-start | bytes 786440 | tf_op jit(solution)/shard_map/ppermute | solution.py:182
  129.9 11.6 %collective-permute-start.11 = (bf16[256,512]{1,0:T(8,128)(2,1)S(1)}, bf16[256,512]{1,0:T(8,128)(2,1)S(1)}, u32[]{:S(2)}, u32[]{:S(2)}) collective-permute-start(bf16[256,512]{1,0:T(8,128)(2,1)S(1)} %collective-permute-done.9.refs_2_), channel_id=1, source_target_pairs={{0,7},{1,0},{2,1},{3,2},{4,3},{5,4},{6,5},{7,6},{8,15},{9,8},{10,9... | collective-permute-start | bytes 786440 | tf_op jit(solution)/shard_map/ppermute | solution.py:182
  138.7 20.2 %collective-permute-start.12 = (bf16[256,512]{1,0:T(8,128)(2,1)S(1)}, bf16[256,512]{1,0:T(8,128)(2,1)S(1)}, u32[]{:S(2)}, u32[]{:S(2)}) collective-permute-start(bf16[256,512]{1,0:T(8,128)(2,1)S(1)} %collective-permute-done.10.refs_3_), channel_id=1, source_target_pairs={{0,1},{1,2},{2,3},{3,4},{4,5},{5,6},{6,7},{7,0},{8,9},{9,10},{10,1... | collective-permute-start | bytes 786440 | tf_op jit(solution)/shard_map/ppermute | solution.py:182
  141.6 17.3 %collective-permute-start.13 = (bf16[256,512]{1,0:T(8,128)(2,1)S(1)}, bf16[256,512]{1,0:T(8,128)(2,1)S(1)}, u32[]{:S(2)}, u32[]{:S(2)}) collective-permute-start(bf16[256,512]{1,0:T(8,128)(2,1)S(1)} %collective-permute-done.11.refs_4_), channel_id=1, source_target_pairs={{0,7},{1,0},{2,1},{3,2},{4,3},{5,4},{6,5},{7,6},{8,15},{9,8},{10,9... | collective-permute-start | bytes 786440 | tf_op jit(solution)/shard_map/ppermute | solution.py:182
  145.5 10.6 %collective-permute-start.14 = (bf16[128,512]{1,0:T(8,128)(2,1)S(1)}, bf16[128,512]{1,0:T(8,128)(2,1)S(1)}, u32[]{:S(2)}, u32[]{:S(2)}) collective-permute-start(bf16[128,512]{1,0:T(8,128)(2,1)S(1)} %slice.18), channel_id=1, source_target_pairs={{0,2},{1,3},{2,4},{3,5},{4,6},{5,7},{6,0},{7,1},{8,10},{9,11},{10,... | collective-permute-start | bytes 393224 | tf_op jit(solution)/shard_map/ppermute | solution.py:182
  151.0 7.9 %collective-permute-start.15 = (bf16[128,512]{1,0:T(8,128)(2,1)S(1)}, bf16[128,512]{1,0:T(8,128)(2,1)S(1)}, u32[]{:S(2)}, u32[]{:S(2)}) collective-permute-start(bf16[128,512]{1,0:T(8,128)(2,1)S(1)} %slice.19), channel_id=1, source_target_pairs={{0,6},{1,7},{2,0},{3,1},{4,2},{5,3},{6,4},{7,5},{8,14},{9,15},{10,... | collective-permute-start | bytes 393224 | tf_op jit(solution)/shard_map/ppermute | solution.py:182
Sparse Core Ops, SparseCore 0:
  15.3 100.2 all-gather.3

commit v4 on v3

--- a/solution.py
+++ b/solution.py
@@ -58,7 +58,7 @@
     ]
     for at, offset in enumerate(sources):
         own, other = pieces[2 * at], pieces[2 * at + 1]
-        their_x = lax.rem(my_x + offset, X)
+        their_x = lax.rem(my_x + (1 - 2 * lax.rem(my_x, 2)) * offset + X, X)
         firsts = [low for low, _ in extents[at]]
         lasts = [high for _, high in extents[at]]
 
@@ -182,16 +182,20 @@
     return lax.ppermute(value, axis, [(i, (i + step) % size) for i in range(size)])
 
 
+def pairs(value, axis, size, second):
+    step = -1 if second else 1
+    moves = [(i, (i + (step if i % 2 == 0 else -step)) % size) for i in range(size)]
+    return lax.ppermute(value, axis, moves)
+
+
 def ring_over_y(attended):
     half = attended.shape[0] // 2
     pieces = [(0, attended)]
-    left = right = attended
+    one = two = attended
     for step in range(1, Y // 2):
-        if step == Y // 2 - 1:
-            far = (around(left[:half], "y", Y, 2), around(right[half:], "y", Y, -2))
-        left = around(left, "y", Y, 1)
-        right = around(right, "y", Y, -1)
-        pieces += [(-step, left), (step, right)]
+        one, two = (pairs(two, "y", Y, False), pairs(one, "y", Y, True))
+        pieces += [(step, one), (-step, two)]
+    far = (pairs(two[:half], "y", Y, False), pairs(one[half:], "y", Y, True))
     return pieces + [(Y // 2, far)]
 
 
@@ -202,7 +206,8 @@
     part = out_ref.shape[1]
 
     def copy(at, z):
-        their_y = lax.rem(y_ref[0] + (offsets[at] + Y), Y)
+        sign = 1 - 2 * lax.rem(y_ref[0], 2)
+        their_y = lax.rem(y_ref[0] + sign * offsets[at] + Y, Y)
         return pltpu.make_async_copy(
             weight_ref.at[z, their_y], held_ref.at[at, z], sems.at[at, z]
         )
@@ -301,19 +306,19 @@
     docs = jnp.broadcast_to(documents.astype(jnp.float32)[:, None], (rows, HD))
 
     mine = lax.all_gather(packed, "zl", axis=0)
-    left = around(mine, "x", X, 1)
-    right = around(mine, "x", X, -1)
+    one = pairs(mine, "x", X, False)
+    two = pairs(mine, "x", X, True)
     mine_other = around(mine, "core", CORE, 1)
-    far_a = around(left[: ZL // 2], "x", X, 1)
-    far_b = around(right[ZL // 2 :], "x", X, -1)
-    left_other = around(left, "core", CORE, 1)
-    right_other = around(right, "core", CORE, 1)
-    far = jnp.concatenate([far_a, far_b], axis=0)
+    far_two = pairs(one[ZL // 2 :], "x", X, True)
+    one_other = around(one, "core", CORE, 1)
+    far_one = pairs(two[: ZL // 2], "x", X, False)
+    two_other = around(two, "core", CORE, 1)
+    far = jnp.concatenate([far_one, far_two], axis=0)
     far_other = around(far, "core", CORE, 1)
 
     state = attend(where, queries, docs, [mine, mine_other], (0,), None, False)
-    state = attend(where, queries, docs, [left, left_other], (X - 1,), state, False)
-    state = attend(where, queries, docs, [right, right_other], (1,), state, False)
+    state = attend(where, queries, docs, [one, one_other], (1,), state, False)
+    state = attend(where, queries, docs, [two, two_other], (-1,), state, False)
     attended = attend(where, queries, docs, [far, far_other], (2,), state, True)
     pieces = ring_over_y(attended)
     y = lax.axis_index("y").astype(jnp.int32).reshape(1)

time: 206 us -> 201 us (0.976)
  the two profiles are of different devices: /device:TPU:200 before, /device:TPU:192 now
where the time goes in v4:
time: 201 us; the launch traced here: 200 us
  starting transfers between devices  72.3 us (36%)
  blocking collectives  45.4 us (23%)
  waiting for transfers between devices  39.6 us (20%)
  Pallas kernels  25.1 us (12%)
  between operations  13.7 us (7%)
  local copies, waits for them, and re-layouts  3.44 us (2%)
    ppermute x12, starting transfers between devices, pairs(): return lax.ppermute(value, axis, moves)  62.5 us
    ppermute x12, waiting for transfers between devices, pairs(): return lax.ppermute(value, axis, moves)  39.6 us
    all_to_all x1, blocking collectives, compute(): came = lax.all_to_all(terms, TP, split_axis=0, concat_axis=0, tiled=True)  28.7 us
    all_gather x1, blocking collectives, compute(): mine = lax.all_gather(packed, 'zl', axis=0)  16.6 us
    pallas_call x4, Pallas kernels, attend(): pl.pallas_call(functools.partial(attend_kernel, sources, first, last), ou...  16.2 us
    ppermute x4, starting transfers between devices, around(): lax.ppermute(value, axis, [(i, (i + step) % size) for i in range(size)])  8.17 us
    pallas_call x1, Pallas kernels, project(): pl.pallas_call(functools.partial(project_kernel, offsets), out_shape=jax....  7.11 us
  transfers between devices with their start and end apart: 18, of which 9 were waited for; matrix products, arithmetic and copies ran while one was open for 1% of the time, Pallas kernels for 8%

profile of v4, /device:TPU:192, one launch (start us, length us, event | category | flops | bytes accessed | tf_op | source)
XLA Modules:
  0.0 200.3 jit_solution(4545390154899007099)
XLA Ops:
  10.6 16.6 %all-gather = bf16[1056,256]{1,0:T(8,128)(2,1)S(1)} all-gather(bf16[264,256]{1,0:T(8,128)(2,1)S(1)} %pad_maximum_fusion), channel_id=2, replica_groups=mesh['zl'=4,'x'=4,'core'=2,'zh'=2,'y'=8] {'zl'}, dimensions={0}, use_global_device_ids=true | all-gather | bytes 675840 | tf_op jit(solution)/shard_map/all_gather | solution.py:308
  27.2 26.6 %collective-permute-start = (bf16[4,264,256]{2,1,0:T(8,128)(2,1)S(1)}, bf16[4,264,256]{2,1,0:T(8,128)(2,1)S(1)}, u32[]{:S(2)}, u32[]{:S(2)}) collective-permute-start(bf16[4,264,256]{2,1,0:T(8,128)(2,1)S(1)} %bitcast.6), channel_id=1, source_target_pairs={{0,96},{32,64},{64,32},{96,0},{1,97},{33,65},{65,33},{97,1},{2,98}... | collective-permute-start | bytes 1622024 | tf_op jit(solution)/shard_map/ppermute | solution.py:188
  55.7 10.6 %collective-permute-done.refs_0_ = bf16[4,264,256]{2,1,0:T(8,128)(2,1)S(1)} collective-permute-done((bf16[4,264,256]{2,1,0:T(8,128)(2,1)S(1)}, bf16[4,264,256]{2,1,0:T(8,128)(2,1)S(1)}, u32[]{:S(2)}, u32[]{:S(2)}) %collective-permute-start) | collective-permute-done | bytes 540704 | tf_op jit(solution)/shard_map/ppermute | solution.py:188
  66.3 8.4 %collective-permute-start.1 = (bf16[2,264,256]{2,1,0:T(8,128)(2,1)S(1)}, bf16[2,264,256]{2,1,0:T(8,128)(2,1)S(1)}, u32[]{:S(2)}, u32[]{:S(2)}) collective-permute-start(bf16[2,264,256]{2,1,0:T(8,128)(2,1)S(1)} %slice.16), channel_id=1, source_target_pairs={{0,32},{32,0},{64,96},{96,64},{1,33},{33,1},{65,97},{97,65},{2,34}... | collective-permute-start | bytes 811016 | tf_op jit(solution)/shard_map/ppermute | solution.py:188
  74.7 1.9 collective-permute-start.7
  76.6 5.5 %collective-permute-done.2.refs_0_ = bf16[4,264,256]{2,1,0:T(8,128)(2,1)S(1)} collective-permute-done((bf16[4,264,256]{2,1,0:T(8,128)(2,1)S(1)}, bf16[4,264,256]{2,1,0:T(8,128)(2,1)S(1)}, u32[]{:S(2)}, u32[]{:S(2)}) %collective-permute-start.2) | collective-permute-done | bytes 540704 | tf_op jit(solution)/shard_map/ppermute | solution.py:188
  82.8 2.1 %collective-permute-start.3 = (bf16[2,264,256]{2,1,0:T(8,128)(2,1)}, bf16[2,264,256]{2,1,0:T(8,128)(2,1)S(1)}, u32[]{:S(2)}, u32[]{:S(2)}) collective-permute-start(bf16[2,264,256]{2,1,0:T(8,128)(2,1)} %slice.17), channel_id=1, source_target_pairs={{0,96},{32,64},{64,32},{96,0},{1,97},{33,65},{65,33},{97,1},{2,98}... | collective-permute-start | bytes 811016 | tf_op jit(solution)/shard_map/ppermute | solution.py:188
  86.9 2.4 %collective-permute-start.5 = (bf16[4,264,256]{2,1,0:T(8,128)(2,1)S(1)}, bf16[4,264,256]{2,1,0:T(8,128)(2,1)S(1)}, u32[]{:S(2)}, u32[]{:S(2)}) collective-permute-start(bf16[4,264,256]{2,1,0:T(8,128)(2,1)S(1)} %collective-permute-done.refs_0_), channel_id=1, source_target_pairs={{0,16},{16,0},{1,17},{17,1},{2,18},{18,2},{3,19},{19,3},{4,20},{20... | collective-permute-start | bytes 1622024 | tf_op jit(solution)/shard_map/ppermute | solution.py:182
  89.3 3.9 %collective-permute-done.1 = bf16[2,264,256]{2,1,0:T(8,128)(2,1)S(1)} collective-permute-done((bf16[2,264,256]{2,1,0:T(8,128)(2,1)S(1)}, bf16[2,264,256]{2,1,0:T(8,128)(2,1)S(1)}, u32[]{:S(2)}, u32[]{:S(2)}) %collective-permute-start.1) | collective-permute-done | bytes 270368 | tf_op jit(solution)/shard_map/ppermute | solution.py:188
  96.4 4.9 %shard_map.55 = (f32[1024,128]{1,0:T(8,128)S(1)}, f32[1024,256]{1,0:T(8,128)S(1)}) custom-call(s32[3]{0:T(128)S(1)} %pad_add_fusion.where_ref, bf16[256,512]{1,0:T(8,128)(2,1)S(1)} %copy-done, f32[256,128]{1,0:T(8,128)S(1)} %broadcast_in_dim.4.docs_ref, bf16[4,264,256]{2,1,0:T(8,128)(2,1)S(1)} %bitcast.9, bf16[4,264,256]{2,1,0:T(8,128)(2,1)S(1)} %collective-permute-done.7.refs_1_), custom_call_target="tpu_custom_call" | custom-call | flops 1610612736 | bytes 1048576 | tf_op jit(solution)/shard_map/pallas_call | solution.py:166
  101.4 3.7 %shard_map.56 = (f32[1024,128]{1,0:T(8,128)S(1)}, f32[1024,256]{1,0:T(8,128)S(1)}) custom-call(s32[3]{0:T(128)S(1)} %pad_add_fusion.where_ref, bf16[256,512]{1,0:T(8,128)(2,1)S(1)} %copy-done, f32[256,128]{1,0:T(8,128)S(1)} %broadcast_in_dim.4.docs_ref, bf16[4,264,256]{2,1,0:T(8,128)(2,1)S(1)} %collective-permute-done.2.refs_0_, ...), custom_call_target="tpu_custom_call" | custom-call | flops 1610612736 | bytes 1048576 | tf_op jit(solution)/shard_map/pallas_call | solution.py:166
  105.1 3.8 %shard_map.57 = (f32[1024,128]{1,0:T(8,128)S(1)}, f32[1024,256]{1,0:T(8,128)S(1)}) custom-call(s32[3]{0:T(128)S(1)} %pad_add_fusion.where_ref, bf16[256,512]{1,0:T(8,128)(2,1)S(1)} %copy-done, f32[256,128]{1,0:T(8,128)S(1)} %broadcast_in_dim.4.docs_ref, bf16[4,264,256]{2,1,0:T(8,128)(2,1)S(1)} %collective-permute-done.refs_0_, ...), custom_call_target="tpu_custom_call" | custom-call | flops 1610612736 | bytes 1048576 | tf_op jit(solution)/shard_map/pallas_call | solution.py:166
  108.9 3.7 %shard_map.58.refs_0_ = bf16[256,512]{1,0:T(8,128)(2,1)S(1)} custom-call(s32[3]{0:T(128)S(1)} %pad_add_fusion.where_ref, bf16[256,512]{1,0:T(8,128)(2,1)S(1)} %copy-done, f32[256,128]{1,0:T(8,128)S(1)} %broadcast_in_dim.4.docs_ref, bf16[4,264,256]{2,1,0:T(8,128)(2,1)S(1)} %constant_dynamic-update-slice_fusion.refs_0_, ...), custom_call_target="tpu_custom_call" | custom-call | flops 1610612736 | bytes 1048576 | tf_op jit(solution)/shard_map/pallas_call | solution.py:166
  114.5 3.2 %collective-permute-start.8 = (bf16[256,512]{1,0:T(8,128)(2,1)S(1)}, bf16[256,512]{1,0:T(8,128)(2,1)S(1)}, u32[]{:S(2)}, u32[]{:S(2)}) collective-permute-start(bf16[256,512]{1,0:T(8,128)(2,1)S(1)} %shard_map.58.refs_0_), channel_id=1, source_target_pairs={{0,1},{1,0},{2,3},{3,2},{4,5},{5,4},{6,7},{7,6},{8,9},{9,8},{10,11... | collective-permute-start | bytes 786440 | tf_op jit(solution)/shard_map/ppermute | solution.py:188
  117.7 6.8 %collective-permute-done.9.refs_2_ = bf16[256,512]{1,0:T(8,128)(2,1)S(1)} collective-permute-done((bf16[256,512]{1,0:T(8,128)(2,1)S(1)}, bf16[256,512]{1,0:T(8,128)(2,1)S(1)}, u32[]{:S(2)}, u32[]{:S(2)}) %collective-permute-start.9) | collective-permute-done | bytes 262176 | tf_op jit(solution)/shard_map/ppermute | solution.py:188
  126.5 4.6 %collective-permute-start.11 = (bf16[256,512]{1,0:T(8,128)(2,1)S(1)}, bf16[256,512]{1,0:T(8,128)(2,1)S(1)}, u32[]{:S(2)}, u32[]{:S(2)}) collective-permute-start(bf16[256,512]{1,0:T(8,128)(2,1)S(1)} %collective-permute-done.8.refs_1_), channel_id=1, source_target_pairs={{0,7},{1,2},{2,1},{3,4},{4,3},{5,6},{6,5},{7,0},{8,15},{9,10},{10,... | collective-permute-start | bytes 786440 | tf_op jit(solution)/shard_map/ppermute | solution.py:188
  131.0 3.8 %collective-permute-done.10.refs_3_ = bf16[256,512]{1,0:T(8,128)(2,1)S(1)} collective-permute-done((bf16[256,512]{1,0:T(8,128)(2,1)S(1)}, bf16[256,512]{1,0:T(8,128)(2,1)S(1)}, u32[]{:S(2)}, u32[]{:S(2)}) %collective-permute-start.10) | collective-permute-done | bytes 262176 | tf_op jit(solution)/shard_map/ppermute | solution.py:188
  134.8 3.1 %collective-permute-start.13 = (bf16[256,512]{1,0:T(8,128)(2,1)S(1)}, bf16[256,512]{1,0:T(8,128)(2,1)S(1)}, u32[]{:S(2)}, u32[]{:S(2)}) collective-permute-start(bf16[256,512]{1,0:T(8,128)(2,1)S(1)} %collective-permute-done.10.refs_3_), channel_id=1, source_target_pairs={{0,7},{1,2},{2,1},{3,4},{4,3},{5,6},{6,5},{7,0},{8,15},{9,10},{10,... | collective-permute-start | bytes 786440 | tf_op jit(solution)/shard_map/ppermute | solution.py:188
  138.0 2.4 %collective-permute-start.12 = (bf16[256,512]{1,0:T(8,128)(2,1)S(1)}, bf16[256,512]{1,0:T(8,128)(2,1)S(1)}, u32[]{:S(2)}, u32[]{:S(2)}) collective-permute-start(bf16[256,512]{1,0:T(8,128)(2,1)S(1)} %collective-permute-done.11.refs_4_), channel_id=1, source_target_pairs={{0,1},{1,0},{2,3},{3,2},{4,5},{5,4},{6,7},{7,6},{8,9},{9,8},{10,11... | collective-permute-start | bytes 786440 | tf_op jit(solution)/shard_map/ppermute | solution.py:188
  140.4 5.0 %collective-permute-done.13.refs_6_ = bf16[256,512]{1,0:T(8,128)(2,1)S(1)} collective-permute-done((bf16[256,512]{1,0:T(8,128)(2,1)S(1)}, bf16[256,512]{1,0:T(8,128)(2,1)S(1)}, u32[]{:S(2)}, u32[]{:S(2)}) %collective-permute-start.13) | collective-permute-done | bytes 262176 | tf_op jit(solution)/shard_map/ppermute | solution.py:188
  147.7 4.5 %collective-permute-start.15 = (bf16[128,512]{1,0:T(8,128)(2,1)S(1)}, bf16[128,512]{1,0:T(8,128)(2,1)S(1)}, u32[]{:S(2)}, u32[]{:S(2)}) collective-permute-start(bf16[128,512]{1,0:T(8,128)(2,1)S(1)} %slice.19), channel_id=1, source_target_pairs={{0,7},{1,2},{2,1},{3,4},{4,3},{5,6},{6,5},{7,0},{8,15},{9,10},{10,... | collective-permute-start | bytes 393224 | tf_op jit(solution)/shard_map/ppermute | solution.py:188
  152.3 3.5 %collective-permute-done.15.refs_8_ = bf16[128,512]{1,0:T(8,128)(2,1)S(1)} collective-permute-done((bf16[128,512]{1,0:T(8,128)(2,1)S(1)}, bf16[128,512]{1,0:T(8,128)(2,1)S(1)}, u32[]{:S(2)}, u32[]{:S(2)}) %collective-permute-start.15) | collective-permute-done | bytes 131104 | tf_op jit(solution)/shard_map/ppermute | solution.py:188
  155.8 7.1 %shard_map.59 = bf16[16,16,1024]{2,1,0:T(8,128)(2,1)S(1)} custom-call(s32[1]{0:T(128)} %bitcast.y_ref, bf16[256,512]{1,0:T(8,128)(2,1)S(1)} %shard_map.58.refs_0_, bf16[256,512]{1,0:T(8,128)(2,1)S(1)} %collective-permute-done.8.refs_1_, bf16[256,512]{1,0:T(8,128)(2,1)S(1)} %collective-permute-done.9.refs_2_, ...), custom_call_target="tpu_custom_call" | custom-call | flops 2147483648 | bytes 10485760 | tf_op jit(solution)/shard_map/pallas_call | solution.py:248
  162.9 28.7 %all_to_all.5.came_ref = bf16[16,16,1024]{2,1,0:T(8,128)(2,1)} all-to-all(bf16[16,16,1024]{2,1,0:T(8,128)(2,1)S(1)} %shard_map.59), channel_id=1, replica_groups=mesh['zl'=4,'x'=4,'core'=2,'zh'=2,'y'=8] {'zh','y'}, dimensions={0} | all-to-all | bytes 1048576 | tf_op jit(solution)/shard_map/all_to_all | solution.py:326
  (37 shorter events, 19.7 us)
Async XLA Ops:
  6.5 149.3 %all-gather.4.cloned.1.call-start = ((), (), s32[]{:S(2)}) async-start(), calls=%async_computation.1 | async-start | bytes 8650752 | tf_op jit(solution)/shard_map/all_gather | solution.py:296
  6.5 1.6 collective-permute-start.16
  8.1 0.7 copy-start.1
  27.2 39.1 %collective-permute-start = (bf16[4,264,256]{2,1,0:T(8,128)(2,1)S(1)}, bf16[4,264,256]{2,1,0:T(8,128)(2,1)S(1)}, u32[]{:S(2)}, u32[]{:S(2)}) collective-permute-start(bf16[4,264,256]{2,1,0:T(8,128)(2,1)S(1)} %bitcast.6), channel_id=1, source_target_pairs={{0,96},{32,64},{64,32},{96,0},{1,97},{33,65},{65,33},{97,1},{2,98}... | collective-permute-start | bytes 1622024 | tf_op jit(solution)/shard_map/ppermute | solution.py:188
  53.8 28.3 %collective-permute-start.2 = (bf16[4,264,256]{2,1,0:T(8,128)(2,1)S(1)}, bf16[4,264,256]{2,1,0:T(8,128)(2,1)S(1)}, u32[]{:S(2)}, u32[]{:S(2)}) collective-permute-start(bf16[4,264,256]{2,1,0:T(8,128)(2,1)S(1)} %bitcast.7), channel_id=1, source_target_pairs={{0,32},{32,0},{64,96},{96,64},{1,33},{33,1},{65,97},{97,65},{2,34}... | collective-permute-start | bytes 1622024 | tf_op jit(solution)/shard_map/ppermute | solution.py:188
  66.3 26.9 %collective-permute-start.1 = (bf16[2,264,256]{2,1,0:T(8,128)(2,1)S(1)}, bf16[2,264,256]{2,1,0:T(8,128)(2,1)S(1)}, u32[]{:S(2)}, u32[]{:S(2)}) collective-permute-start(bf16[2,264,256]{2,1,0:T(8,128)(2,1)S(1)} %slice.16), channel_id=1, source_target_pairs={{0,32},{32,0},{64,96},{96,64},{1,33},{33,1},{65,97},{97,65},{2,34}... | collective-permute-start | bytes 811016 | tf_op jit(solution)/shard_map/ppermute | solution.py:188
  74.7 20.7 %collective-permute-start.7 = (bf16[4,264,256]{2,1,0:T(8,128)(2,1)S(1)}, bf16[4,264,256]{2,1,0:T(8,128)(2,1)S(1)}, u32[]{:S(2)}, u32[]{:S(2)}) collective-permute-start(bf16[4,264,256]{2,1,0:T(8,128)(2,1)S(1)} %bitcast.8), channel_id=1, source_target_pairs={{0,16},{16,0},{1,17},{17,1},{2,18},{18,2},{3,19},{19,3},{4,20},{20... | collective-permute-start | bytes 1622024 | tf_op jit(solution)/shard_map/ppermute | solution.py:182
  82.8 10.5 %collective-permute-start.3 = (bf16[2,264,256]{2,1,0:T(8,128)(2,1)}, bf16[2,264,256]{2,1,0:T(8,128)(2,1)S(1)}, u32[]{:S(2)}, u32[]{:S(2)}) collective-permute-start(bf16[2,264,256]{2,1,0:T(8,128)(2,1)} %slice.17), channel_id=1, source_target_pairs={{0,96},{32,64},{64,32},{96,0},{1,97},{33,65},{65,33},{97,1},{2,98}... | collective-permute-start | bytes 811016 | tf_op jit(solution)/shard_map/ppermute | solution.py:188
  85.0 16.4 %collective-permute-start.6 = (bf16[4,264,256]{2,1,0:T(8,128)(2,1)S(1)}, bf16[4,264,256]{2,1,0:T(8,128)(2,1)S(1)}, u32[]{:S(2)}, u32[]{:S(2)}) collective-permute-start(bf16[4,264,256]{2,1,0:T(8,128)(2,1)S(1)} %collective-permute-done.2.refs_0_), channel_id=1, source_target_pairs={{0,16},{16,0},{1,17},{17,1},{2,18},{18,2},{3,19},{19,3},{4,20},{20... | collective-permute-start | bytes 1622024 | tf_op jit(solution)/shard_map/ppermute | solution.py:182
  86.9 18.2 %collective-permute-start.5 = (bf16[4,264,256]{2,1,0:T(8,128)(2,1)S(1)}, bf16[4,264,256]{2,1,0:T(8,128)(2,1)S(1)}, u32[]{:S(2)}, u32[]{:S(2)}) collective-permute-start(bf16[4,264,256]{2,1,0:T(8,128)(2,1)S(1)} %collective-permute-done.refs_0_), channel_id=1, source_target_pairs={{0,16},{16,0},{1,17},{17,1},{2,18},{18,2},{3,19},{19,3},{4,20},{20... | collective-permute-start | bytes 1622024 | tf_op jit(solution)/shard_map/ppermute | solution.py:182
  93.3 15.6 %collective-permute-start.4 = (bf16[4,264,256]{2,1,0:T(8,128)(2,1)S(1)}, bf16[4,264,256]{2,1,0:T(8,128)(2,1)S(1)}, u32[]{:S(2)}, u32[]{:S(2)}) collective-permute-start(bf16[4,264,256]{2,1,0:T(8,128)(2,1)S(1)} %constant_dynamic-update-slice_fusion.refs_0_), channel_id=1, source_target_pairs={{0,16},{16,0},{1,17},{17,1},{2,18},{18,2},{3,19},{19,3},{4,20},{20... | collective-permute-start | bytes 1622024 | tf_op jit(solution)/shard_map/ppermute | solution.py:182
  95.4 1.0 copy-start
  112.6 11.9 %collective-permute-start.9 = (bf16[256,512]{1,0:T(8,128)(2,1)S(1)}, bf16[256,512]{1,0:T(8,128)(2,1)S(1)}, u32[]{:S(2)}, u32[]{:S(2)}) collective-permute-start(bf16[256,512]{1,0:T(8,128)(2,1)S(1)} %shard_map.58.refs_0_), channel_id=1, source_target_pairs={{0,7},{1,2},{2,1},{3,4},{4,3},{5,6},{6,5},{7,0},{8,15},{9,10},{10,... | collective-permute-start | bytes 786440 | tf_op jit(solution)/shard_map/ppermute | solution.py:188
  114.5 11.9 %collective-permute-start.8 = (bf16[256,512]{1,0:T(8,128)(2,1)S(1)}, bf16[256,512]{1,0:T(8,128)(2,1)S(1)}, u32[]{:S(2)}, u32[]{:S(2)}) collective-permute-start(bf16[256,512]{1,0:T(8,128)(2,1)S(1)} %shard_map.58.refs_0_), channel_id=1, source_target_pairs={{0,1},{1,0},{2,3},{3,2},{4,5},{5,4},{6,7},{7,6},{8,9},{9,8},{10,11... | collective-permute-start | bytes 786440 | tf_op jit(solution)/shard_map/ppermute | solution.py:188
  124.5 10.3 %collective-permute-start.10 = (bf16[256,512]{1,0:T(8,128)(2,1)S(1)}, bf16[256,512]{1,0:T(8,128)(2,1)S(1)}, u32[]{:S(2)}, u32[]{:S(2)}) collective-permute-start(bf16[256,512]{1,0:T(8,128)(2,1)S(1)} %collective-permute-done.9.refs_2_), channel_id=1, source_target_pairs={{0,1},{1,0},{2,3},{3,2},{4,5},{5,4},{6,7},{7,6},{8,9},{9,8},{10,11... | collective-permute-start | bytes 786440 | tf_op jit(solution)/shard_map/ppermute | solution.py:188
  126.5 11.5 %collective-permute-start.11 = (bf16[256,512]{1,0:T(8,128)(2,1)S(1)}, bf16[256,512]{1,0:T(8,128)(2,1)S(1)}, u32[]{:S(2)}, u32[]{:S(2)}) collective-permute-start(bf16[256,512]{1,0:T(8,128)(2,1)S(1)} %collective-permute-done.8.refs_1_), channel_id=1, source_target_pairs={{0,7},{1,2},{2,1},{3,4},{4,3},{5,6},{6,5},{7,0},{8,15},{9,10},{10,... | collective-permute-start | bytes 786440 | tf_op jit(solution)/shard_map/ppermute | solution.py:188
  134.8 10.6 %collective-permute-start.13 = (bf16[256,512]{1,0:T(8,128)(2,1)S(1)}, bf16[256,512]{1,0:T(8,128)(2,1)S(1)}, u32[]{:S(2)}, u32[]{:S(2)}) collective-permute-start(bf16[256,512]{1,0:T(8,128)(2,1)S(1)} %collective-permute-done.10.refs_3_), channel_id=1, source_target_pairs={{0,7},{1,2},{2,1},{3,4},{4,3},{5,6},{6,5},{7,0},{8,15},{9,10},{10,... | collective-permute-start | bytes 786440 | tf_op jit(solution)/shard_map/ppermute | solution.py:188
  138.0 9.7 %collective-permute-start.12 = (bf16[256,512]{1,0:T(8,128)(2,1)S(1)}, bf16[256,512]{1,0:T(8,128)(2,1)S(1)}, u32[]{:S(2)}, u32[]{:S(2)}) collective-permute-start(bf16[256,512]{1,0:T(8,128)(2,1)S(1)} %collective-permute-done.11.refs_4_), channel_id=1, source_target_pairs={{0,1},{1,0},{2,3},{3,2},{4,5},{5,4},{6,7},{7,6},{8,9},{9,8},{10,11... | collective-permute-start | bytes 786440 | tf_op jit(solution)/shard_map/ppermute | solution.py:188
  145.5 6.9 %collective-permute-start.14 = (bf16[128,512]{1,0:T(8,128)(2,1)S(1)}, bf16[128,512]{1,0:T(8,128)(2,1)S(1)}, u32[]{:S(2)}, u32[]{:S(2)}) collective-permute-start(bf16[128,512]{1,0:T(8,128)(2,1)S(1)} %slice.18), channel_id=1, source_target_pairs={{0,1},{1,0},{2,3},{3,2},{4,5},{5,4},{6,7},{7,6},{8,9},{9,8},{10,11... | collective-permute-start | bytes 393224 | tf_op jit(solution)/shard_map/ppermute | solution.py:188
  147.7 8.1 %collective-permute-start.15 = (bf16[128,512]{1,0:T(8,128)(2,1)S(1)}, bf16[128,512]{1,0:T(8,128)(2,1)S(1)}, u32[]{:S(2)}, u32[]{:S(2)}) collective-permute-start(bf16[128,512]{1,0:T(8,128)(2,1)S(1)} %slice.19), channel_id=1, source_target_pairs={{0,7},{1,2},{2,1},{3,4},{4,3},{5,6},{6,5},{7,0},{8,15},{9,10},{10,... | collective-permute-start | bytes 393224 | tf_op jit(solution)/shard_map/ppermute | solution.py:188
Sparse Core Ops, SparseCore 0:
  9.5 107.4 all-gather.3

commit v5 on v4

--- a/solution.py
+++ b/solution.py
@@ -16,6 +16,7 @@
 CTX = ("zl", "x", "core")
 TP = ("zh", "y")
 PAD = 8
+EARLY = 7
 NEG = -1e30
 SCALE2 = math.log2(math.e) / math.sqrt(HD)
 
@@ -199,71 +200,83 @@
     return pieces + [(Y // 2, far)]
 
 
-def project_kernel(offsets, y_ref, *refs):
-    pieces, (weight_ref, out_ref, held_ref, acc_ref, sems) = refs[: Y + 1], refs[Y + 1 :]
+def project_kernel(offsets, first, y_ref, *refs):
+    count = len(offsets)
+    if first:
+        blocks, (weight_ref, acc_ref, held_ref, sems) = refs[:count], refs[count:]
+    else:
+        blocks, (weight_ref, acc_ref, out_ref, held_ref, sems) = refs[: count + 1], refs[count + 1 :]
     half = acc_ref.shape[1] // 2
     width = acc_ref.shape[2]
-    part = out_ref.shape[1]
+    sign = 1 - 2 * lax.rem(y_ref[0], 2)
 
     def copy(at, z):
-        sign = 1 - 2 * lax.rem(y_ref[0], 2)
         their_y = lax.rem(y_ref[0] + sign * offsets[at] + Y, Y)
         return pltpu.make_async_copy(
             weight_ref.at[z, their_y], held_ref.at[at, z], sems.at[at, z]
         )
 
-    for at in range(Y):
+    def term(block, at, z):
+        return jnp.dot(block, held_ref[at, z], preferred_element_type=jnp.float32)
+
+    for at in range(count):
         for z in range(ZL):
             copy(at, z).start()
-    for at in range(Y):
+    if first:
+        for at in range(count):
+            for z in range(ZL):
+                copy(at, z).wait()
+                new = term(blocks[at][...], at, z)
+                acc_ref[z] = new if at == 0 else acc_ref[z] + new
+        return
+    part = out_ref.shape[1]
+    for at in range(count):
         for z in range(ZL):
             copy(at, z).wait()
-            if at < Y - 1:
-                term = jnp.dot(
-                    pieces[at][...], held_ref[at, z], preferred_element_type=jnp.float32
-                )
-                acc_ref[z] = term if at == 0 else acc_ref[z] + term
-                continue
-            for side in range(2):
-                rows = slice(side * half, (side + 1) * half)
-                term = jnp.dot(
-                    pieces[at + side][...], held_ref[at, z], preferred_element_type=jnp.float32
-                )
-                done = (acc_ref[z, rows] + term).astype(jnp.bfloat16)
-                out_ref[
-                    side * half // part : (side + 1) * half // part,
-                    :,
-                    z * width : (z + 1) * width,
-                ] = done.reshape(half // part, part, width)
-
-
-def project(y, pieces, weight):
-    rows, depth = pieces[0][1].shape
-    width = weight.shape[2]
+    for z in range(ZL):
+        for side in range(2):
+            rows = slice(side * half, (side + 1) * half)
+            total = acc_ref[z, rows]
+            for at in range(count - 1):
+                total = total + term(blocks[at][rows, :], at, z)
+            total = total + term(blocks[count - 1 + side][...], count - 1, z)
+            out_ref[
+                side * half // part : (side + 1) * half // part, :, z * width : (z + 1) * width
+            ] = total.astype(jnp.bfloat16).reshape(half // part, part, width)
+
+
+def project(y, pieces, weight, total):
+    first = total is None
+    rows = pieces[0][1].shape[0] if first else total.shape[1]
+    depth, width = weight.shape[1:]
+    count = len(pieces)
     weight = weight.reshape(ZL, X * CORE, depth, width)
     offsets = tuple(offset for offset, _ in pieces)
-    blocks = [block for _, block in pieces[:-1]] + list(pieces[-1][1])
+    blocks = [block for _, block in pieces]
+    if not first:
+        blocks = blocks[:-1] + list(blocks[-1])
     whole = pl.BlockSpec(memory_space=pltpu.VMEM)
-    out = (ZH * Y, rows // (ZH * Y), ZL * width)
+    sums = jax.ShapeDtypeStruct((ZL, rows, width), jnp.float32)
+    out = jax.ShapeDtypeStruct((ZH * Y, rows // (ZH * Y), ZL * width), jnp.bfloat16)
     return pl.pallas_call(
-        functools.partial(project_kernel, offsets),
-        out_shape=jax.ShapeDtypeStruct(out, jnp.bfloat16),
+        functools.partial(project_kernel, offsets, first),
+        out_shape=sums if first else out,
         in_specs=[pl.BlockSpec(memory_space=pltpu.SMEM)]
         + [whole] * len(blocks)
-        + [pl.BlockSpec(memory_space=pltpu.HBM)],
+        + [pl.BlockSpec(memory_space=pltpu.HBM)]
+        + [whole] * (0 if first else 1),
         out_specs=whole,
         scratch_shapes=[
-            pltpu.VMEM((Y, ZL, depth, width), jnp.bfloat16),
-            pltpu.VMEM((ZL, rows, width), jnp.float32),
-            pltpu.SemaphoreType.DMA((Y, ZL)),
+            pltpu.VMEM((count, ZL, depth, width), jnp.bfloat16),
+            pltpu.SemaphoreType.DMA((count, ZL)),
         ],
         compiler_params=pltpu.CompilerParams(vmem_limit_bytes=51 << 20),
         cost_estimate=pl.CostEstimate(
-            flops=2 * Y * rows * depth * ZL * width,
-            bytes_accessed=2 * (Y * depth * ZL * width + Y * rows * depth),
+            flops=2 * count * rows * depth * ZL * width,
+            bytes_accessed=2 * (count * depth * ZL * width + count * rows * depth),
             transcendentals=0,
         ),
-    )(y, *blocks, weight)
+    )(y, *blocks, weight, *(() if first else (total,)))
 
 
 def collect_kernel(came_ref, out_ref):
@@ -322,7 +335,8 @@
     attended = attend(where, queries, docs, [far, far_other], (2,), state, True)
     pieces = ring_over_y(attended)
     y = lax.axis_index("y").astype(jnp.int32).reshape(1)
-    terms = project(y, pieces, weight)
+    total = project(y, pieces[:EARLY], weight, None)
+    terms = project(y, pieces[EARLY:], weight, total)
     came = lax.all_to_all(terms, TP, split_axis=0, concat_axis=0, tiled=True)
     return collect(came)
 

time: 201 us -> 199 us (0.990)
  waiting for transfers between devices: 39.6 us -> 36 us
    ppermute x12, waiting for transfers between devices: 39.6 us -> 36 us  [pairs(): return lax.ppermute(value, axis, moves)]
    pallas_call x1 -> x2, Pallas kernels: 7.11 us -> 8.1 us  [project(): pl.pallas_call(functools.partial(project_kernel, offsets, first), out_sha...]
  transfers between devices with their start and end apart: 18 -> 18, of which waited for: 9 -> 7; matrix products, arithmetic and copies ran while one was open for 1% -> 1% of each run, Pallas kernels for 8% -> 11%
where the time goes in v5:
time: 199 us; the launch traced here: 198 us
  starting transfers between devices  72.3 us (36%)
  blocking collectives  45.9 us (23%)
  waiting for transfers between devices  36 us (18%)
  Pallas kernels  26.1 us (13%)
  between operations  13.7 us (7%)
  local copies, waits for them, and re-layouts  3.44 us (2%)
    ppermute x12, starting transfers between devices, pairs(): return lax.ppermute(value, axis, moves)  62.5 us
    ppermute x12, waiting for transfers between devices, pairs(): return lax.ppermute(value, axis, moves)  36 us
    all_to_all x1, blocking collectives, compute(): came = lax.all_to_all(terms, TP, split_axis=0, concat_axis=0, tiled=True)  29.2 us
    all_gather x1, blocking collectives, compute(): mine = lax.all_gather(packed, 'zl', axis=0)  16.6 us
    pallas_call x4, Pallas kernels, attend(): pl.pallas_call(functools.partial(attend_kernel, sources, first, last), ou...  16.2 us
    ppermute x4, starting transfers between devices, around(): lax.ppermute(value, axis, [(i, (i + step) % size) for i in range(size)])  8.17 us
    pallas_call x2, Pallas kernels, project(): pl.pallas_call(functools.partial(project_kernel, offsets, first), out_sha...  8.1 us
  transfers between devices with their start and end apart: 18, of which 7 were waited for; matrix products, arithmetic and copies ran while one was open for 1% of the time, Pallas kernels for 11%

profile of v5, /device:TPU:192, one launch (start us, length us, event | category | flops | bytes accessed | tf_op | source)
XLA Modules:
  0.0 198.2 jit_solution(3355546070737203855)
XLA Ops:
  10.6 16.6 %all-gather = bf16[1056,256]{1,0:T(8,128)(2,1)S(1)} all-gather(bf16[264,256]{1,0:T(8,128)(2,1)S(1)} %pad_maximum_fusion), channel_id=2, replica_groups=mesh['zl'=4,'x'=4,'core'=2,'zh'=2,'y'=8] {'zl'}, dimensions={0}, use_global_device_ids=true | all-gather | bytes 675840 | tf_op jit(solution)/shard_map/all_gather | solution.py:321
  27.2 26.6 %collective-permute-start = (bf16[4,264,256]{2,1,0:T(8,128)(2,1)S(1)}, bf16[4,264,256]{2,1,0:T(8,128)(2,1)S(1)}, u32[]{:S(2)}, u32[]{:S(2)}) collective-permute-start(bf16[4,264,256]{2,1,0:T(8,128)(2,1)S(1)} %bitcast.6), channel_id=1, source_target_pairs={{0,96},{32,64},{64,32},{96,0},{1,97},{33,65},{65,33},{97,1},{2,98}... | collective-permute-start | bytes 1622024 | tf_op jit(solution)/shard_map/ppermute | solution.py:189
  53.8 1.9 collective-permute-start.2
  55.7 10.6 %collective-permute-done.refs_0_ = bf16[4,264,256]{2,1,0:T(8,128)(2,1)S(1)} collective-permute-done((bf16[4,264,256]{2,1,0:T(8,128)(2,1)S(1)}, bf16[4,264,256]{2,1,0:T(8,128)(2,1)S(1)}, u32[]{:S(2)}, u32[]{:S(2)}) %collective-permute-start) | collective-permute-done | bytes 540704 | tf_op jit(solution)/shard_map/ppermute | solution.py:189
  66.3 8.4 %collective-permute-start.1 = (bf16[2,264,256]{2,1,0:T(8,128)(2,1)S(1)}, bf16[2,264,256]{2,1,0:T(8,128)(2,1)S(1)}, u32[]{:S(2)}, u32[]{:S(2)}) collective-permute-start(bf16[2,264,256]{2,1,0:T(8,128)(2,1)S(1)} %slice.16), channel_id=1, source_target_pairs={{0,32},{32,0},{64,96},{96,64},{1,33},{33,1},{65,97},{97,65},{2,34}... | collective-permute-start | bytes 811016 | tf_op jit(solution)/shard_map/ppermute | solution.py:189
  74.7 1.9 collective-permute-start.7
  76.6 5.5 %collective-permute-done.2.refs_0_ = bf16[4,264,256]{2,1,0:T(8,128)(2,1)S(1)} collective-permute-done((bf16[4,264,256]{2,1,0:T(8,128)(2,1)S(1)}, bf16[4,264,256]{2,1,0:T(8,128)(2,1)S(1)}, u32[]{:S(2)}, u32[]{:S(2)}) %collective-permute-start.2) | collective-permute-done | bytes 540704 | tf_op jit(solution)/shard_map/ppermute | solution.py:189
  82.8 2.1 %collective-permute-start.3 = (bf16[2,264,256]{2,1,0:T(8,128)(2,1)}, bf16[2,264,256]{2,1,0:T(8,128)(2,1)S(1)}, u32[]{:S(2)}, u32[]{:S(2)}) collective-permute-start(bf16[2,264,256]{2,1,0:T(8,128)(2,1)} %slice.17), channel_id=1, source_target_pairs={{0,96},{32,64},{64,32},{96,0},{1,97},{33,65},{65,33},{97,1},{2,98}... | collective-permute-start | bytes 811016 | tf_op jit(solution)/shard_map/ppermute | solution.py:189
  86.9 2.4 %collective-permute-start.5 = (bf16[4,264,256]{2,1,0:T(8,128)(2,1)S(1)}, bf16[4,264,256]{2,1,0:T(8,128)(2,1)S(1)}, u32[]{:S(2)}, u32[]{:S(2)}) collective-permute-start(bf16[4,264,256]{2,1,0:T(8,128)(2,1)S(1)} %collective-permute-done.refs_0_), channel_id=1, source_target_pairs={{0,16},{16,0},{1,17},{17,1},{2,18},{18,2},{3,19},{19,3},{4,20},{20... | collective-permute-start | bytes 1622024 | tf_op jit(solution)/shard_map/ppermute | solution.py:183
  89.3 3.9 %collective-permute-done.1 = bf16[2,264,256]{2,1,0:T(8,128)(2,1)S(1)} collective-permute-done((bf16[2,264,256]{2,1,0:T(8,128)(2,1)S(1)}, bf16[2,264,256]{2,1,0:T(8,128)(2,1)S(1)}, u32[]{:S(2)}, u32[]{:S(2)}) %collective-permute-start.1) | collective-permute-done | bytes 270368 | tf_op jit(solution)/shard_map/ppermute | solution.py:189
  96.4 4.9 %shard_map.55 = (f32[1024,128]{1,0:T(8,128)S(1)}, f32[1024,256]{1,0:T(8,128)S(1)}) custom-call(s32[3]{0:T(128)S(1)} %pad_add_fusion.where_ref, bf16[256,512]{1,0:T(8,128)(2,1)S(1)} %copy-done, f32[256,128]{1,0:T(8,128)S(1)} %broadcast_in_dim.4.docs_ref, bf16[4,264,256]{2,1,0:T(8,128)(2,1)S(1)} %bitcast.9, bf16[4,264,256]{2,1,0:T(8,128)(2,1)S(1)} %collective-permute-done.7.refs_1_), custom_call_target="tpu_custom_call" | custom-call | flops 1610612736 | bytes 1048576 | tf_op jit(solution)/shard_map/pallas_call | solution.py:167
  101.4 3.7 %shard_map.56 = (f32[1024,128]{1,0:T(8,128)S(1)}, f32[1024,256]{1,0:T(8,128)S(1)}) custom-call(s32[3]{0:T(128)S(1)} %pad_add_fusion.where_ref, bf16[256,512]{1,0:T(8,128)(2,1)S(1)} %copy-done, f32[256,128]{1,0:T(8,128)S(1)} %broadcast_in_dim.4.docs_ref, bf16[4,264,256]{2,1,0:T(8,128)(2,1)S(1)} %collective-permute-done.2.refs_0_, ...), custom_call_target="tpu_custom_call" | custom-call | flops 1610612736 | bytes 1048576 | tf_op jit(solution)/shard_map/pallas_call | solution.py:167
  105.1 3.8 %shard_map.57 = (f32[1024,128]{1,0:T(8,128)S(1)}, f32[1024,256]{1,0:T(8,128)S(1)}) custom-call(s32[3]{0:T(128)S(1)} %pad_add_fusion.where_ref, bf16[256,512]{1,0:T(8,128)(2,1)S(1)} %copy-done, f32[256,128]{1,0:T(8,128)S(1)} %broadcast_in_dim.4.docs_ref, bf16[4,264,256]{2,1,0:T(8,128)(2,1)S(1)} %collective-permute-done.refs_0_, ...), custom_call_target="tpu_custom_call" | custom-call | flops 1610612736 | bytes 1048576 | tf_op jit(solution)/shard_map/pallas_call | solution.py:167
  108.9 3.7 %shard_map.58.refs_0_ = bf16[256,512]{1,0:T(8,128)(2,1)S(1)} custom-call(s32[3]{0:T(128)S(1)} %pad_add_fusion.where_ref, bf16[256,512]{1,0:T(8,128)(2,1)S(1)} %copy-done, f32[256,128]{1,0:T(8,128)S(1)} %broadcast_in_dim.4.docs_ref, bf16[4,264,256]{2,1,0:T(8,128)(2,1)S(1)} %constant_dynamic-update-slice_fusion.refs_0_, ...), custom_call_target="tpu_custom_call" | custom-call | flops 1610612736 | bytes 1048576 | tf_op jit(solution)/shard_map/pallas_call | solution.py:167
  114.5 3.2 %collective-permute-start.12 = (bf16[256,512]{1,0:T(8,128)(2,1)S(1)}, bf16[256,512]{1,0:T(8,128)(2,1)S(1)}, u32[]{:S(2)}, u32[]{:S(2)}) collective-permute-start(bf16[256,512]{1,0:T(8,128)(2,1)S(1)} %shard_map.58.refs_0_), channel_id=1, source_target_pairs={{0,1},{1,0},{2,3},{3,2},{4,5},{5,4},{6,7},{7,6},{8,9},{9,8},{10,11... | collective-permute-start | bytes 786440 | tf_op jit(solution)/shard_map/ppermute | solution.py:189
  117.7 6.8 %collective-permute-done.8.refs_2_ = bf16[256,512]{1,0:T(8,128)(2,1)S(1)} collective-permute-done((bf16[256,512]{1,0:T(8,128)(2,1)S(1)}, bf16[256,512]{1,0:T(8,128)(2,1)S(1)}, u32[]{:S(2)}, u32[]{:S(2)}) %collective-permute-start.8) | collective-permute-done | bytes 262176 | tf_op jit(solution)/shard_map/ppermute | solution.py:189
  126.5 4.6 %collective-permute-start.13 = (bf16[256,512]{1,0:T(8,128)(2,1)S(1)}, bf16[256,512]{1,0:T(8,128)(2,1)S(1)}, u32[]{:S(2)}, u32[]{:S(2)}) collective-permute-start(bf16[256,512]{1,0:T(8,128)(2,1)S(1)} %collective-permute-done.12.refs_1_), channel_id=1, source_target_pairs={{0,7},{1,2},{2,1},{3,4},{4,3},{5,6},{6,5},{7,0},{8,15},{9,10},{10,... | collective-permute-start | bytes 786440 | tf_op jit(solution)/shard_map/ppermute | solution.py:189
  131.0 3.8 %collective-permute-done.9.refs_3_ = bf16[256,512]{1,0:T(8,128)(2,1)S(1)} collective-permute-done((bf16[256,512]{1,0:T(8,128)(2,1)S(1)}, bf16[256,512]{1,0:T(8,128)(2,1)S(1)}, u32[]{:S(2)}, u32[]{:S(2)}) %collective-permute-start.9) | collective-permute-done | bytes 262176 | tf_op jit(solution)/shard_map/ppermute | solution.py:189
  134.8 3.1 %collective-permute-start.10 = (bf16[256,512]{1,0:T(8,128)(2,1)S(1)}, bf16[256,512]{1,0:T(8,128)(2,1)S(1)}, u32[]{:S(2)}, u32[]{:S(2)}) collective-permute-start(bf16[256,512]{1,0:T(8,128)(2,1)S(1)} %collective-permute-done.9.refs_3_), channel_id=1, source_target_pairs={{0,7},{1,2},{2,1},{3,4},{4,3},{5,6},{6,5},{7,0},{8,15},{9,10},{10,... | collective-permute-start | bytes 786440 | tf_op jit(solution)/shard_map/ppermute | solution.py:189
  138.0 2.4 %collective-permute-start.14 = (bf16[256,512]{1,0:T(8,128)(2,1)S(1)}, bf16[256,512]{1,0:T(8,128)(2,1)S(1)}, u32[]{:S(2)}, u32[]{:S(2)}) collective-permute-start(bf16[256,512]{1,0:T(8,128)(2,1)S(1)} %collective-permute-done.13.refs_4_), channel_id=1, source_target_pairs={{0,1},{1,0},{2,3},{3,2},{4,5},{5,4},{6,7},{7,6},{8,9},{9,8},{10,11... | collective-permute-start | bytes 786440 | tf_op jit(solution)/shard_map/ppermute | solution.py:189
  140.4 5.0 %collective-permute-done.10.refs_6_ = bf16[256,512]{1,0:T(8,128)(2,1)S(1)} collective-permute-done((bf16[256,512]{1,0:T(8,128)(2,1)S(1)}, bf16[256,512]{1,0:T(8,128)(2,1)S(1)}, u32[]{:S(2)}, u32[]{:S(2)}) %collective-permute-start.10) | collective-permute-done | bytes 262176 | tf_op jit(solution)/shard_map/ppermute | solution.py:189
  147.7 4.5 %collective-permute-start.15 = (bf16[128,512]{1,0:T(8,128)(2,1)S(1)}, bf16[128,512]{1,0:T(8,128)(2,1)S(1)}, u32[]{:S(2)}, u32[]{:S(2)}) collective-permute-start(bf16[128,512]{1,0:T(8,128)(2,1)S(1)} %slice.19), channel_id=1, source_target_pairs={{0,7},{1,2},{2,1},{3,4},{4,3},{5,6},{6,5},{7,0},{8,15},{9,10},{10,... | collective-permute-start | bytes 393224 | tf_op jit(solution)/shard_map/ppermute | solution.py:189
  152.2 6.4 %shard_map.59.refs_3_ = f32[4,256,256]{2,1,0:T(8,128)S(1)} custom-call(s32[1]{0:T(128)} %bitcast.y_ref, bf16[256,512]{1,0:T(8,128)(2,1)S(1)} %shard_map.58.refs_0_, bf16[256,512]{1,0:T(8,128)(2,1)S(1)} %collective-permute-done.12.refs_1_, bf16[256,512]{1,0:T(8,128)(2,1)S(1)} %collective-permute-done.8.refs_2_, ...), custom_call_target="tpu_custom_call" | custom-call | flops 1879048192 | bytes 9175040 | tf_op jit(solution)/shard_map/pallas_call | solution.py:261
  160.4 29.2 %all_to_all.5.came_ref = bf16[16,16,1024]{2,1,0:T(8,128)(2,1)} all-to-all(bf16[16,16,1024]{2,1,0:T(8,128)(2,1)S(1)} %shard_map.60), channel_id=1, replica_groups=mesh['zl'=4,'x'=4,'core'=2,'zh'=2,'y'=8] {'zh','y'}, dimensions={0} | all-to-all | bytes 1048576 | tf_op jit(solution)/shard_map/all_to_all | solution.py:340
  (38 shorter events, 19.4 us)
Async XLA Ops:
  6.5 145.7 %all-gather.4.cloned.1.call-start = ((), (), s32[]{:S(2)}) async-start(), calls=%async_computation.1 | async-start | bytes 8650752 | tf_op jit(solution)/shard_map/all_gather | solution.py:309
  6.5 1.6 collective-permute-start.16
  8.1 0.7 copy-start.1
  27.2 39.1 %collective-permute-start = (bf16[4,264,256]{2,1,0:T(8,128)(2,1)S(1)}, bf16[4,264,256]{2,1,0:T(8,128)(2,1)S(1)}, u32[]{:S(2)}, u32[]{:S(2)}) collective-permute-start(bf16[4,264,256]{2,1,0:T(8,128)(2,1)S(1)} %bitcast.6), channel_id=1, source_target_pairs={{0,96},{32,64},{64,32},{96,0},{1,97},{33,65},{65,33},{97,1},{2,98}... | collective-permute-start | bytes 1622024 | tf_op jit(solution)/shard_map/ppermute | solution.py:189
  53.8 28.3 %collective-permute-start.2 = (bf16[4,264,256]{2,1,0:T(8,128)(2,1)S(1)}, bf16[4,264,256]{2,1,0:T(8,128)(2,1)S(1)}, u32[]{:S(2)}, u32[]{:S(2)}) collective-permute-start(bf16[4,264,256]{2,1,0:T(8,128)(2,1)S(1)} %bitcast.7), channel_id=1, source_target_pairs={{0,32},{32,0},{64,96},{96,64},{1,33},{33,1},{65,97},{97,65},{2,34}... | collective-permute-start | bytes 1622024 | tf_op jit(solution)/shard_map/ppermute | solution.py:189
  66.3 26.9 %collective-permute-start.1 = (bf16[2,264,256]{2,1,0:T(8,128)(2,1)S(1)}, bf16[2,264,256]{2,1,0:T(8,128)(2,1)S(1)}, u32[]{:S(2)}, u32[]{:S(2)}) collective-permute-start(bf16[2,264,256]{2,1,0:T(8,128)(2,1)S(1)} %slice.16), channel_id=1, source_target_pairs={{0,32},{32,0},{64,96},{96,64},{1,33},{33,1},{65,97},{97,65},{2,34}... | collective-permute-start | bytes 811016 | tf_op jit(solution)/shard_map/ppermute | solution.py:189
  74.7 20.7 %collective-permute-start.7 = (bf16[4,264,256]{2,1,0:T(8,128)(2,1)S(1)}, bf16[4,264,256]{2,1,0:T(8,128)(2,1)S(1)}, u32[]{:S(2)}, u32[]{:S(2)}) collective-permute-start(bf16[4,264,256]{2,1,0:T(8,128)(2,1)S(1)} %bitcast.8), channel_id=1, source_target_pairs={{0,16},{16,0},{1,17},{17,1},{2,18},{18,2},{3,19},{19,3},{4,20},{20... | collective-permute-start | bytes 1622024 | tf_op jit(solution)/shard_map/ppermute | solution.py:183
  82.8 10.5 %collective-permute-start.3 = (bf16[2,264,256]{2,1,0:T(8,128)(2,1)}, bf16[2,264,256]{2,1,0:T(8,128)(2,1)S(1)}, u32[]{:S(2)}, u32[]{:S(2)}) collective-permute-start(bf16[2,264,256]{2,1,0:T(8,128)(2,1)} %slice.17), channel_id=1, source_target_pairs={{0,96},{32,64},{64,32},{96,0},{1,97},{33,65},{65,33},{97,1},{2,98}... | collective-permute-start | bytes 811016 | tf_op jit(solution)/shard_map/ppermute | solution.py:189
  85.0 16.4 %collective-permute-start.6 = (bf16[4,264,256]{2,1,0:T(8,128)(2,1)S(1)}, bf16[4,264,256]{2,1,0:T(8,128)(2,1)S(1)}, u32[]{:S(2)}, u32[]{:S(2)}) collective-permute-start(bf16[4,264,256]{2,1,0:T(8,128)(2,1)S(1)} %collective-permute-done.2.refs_0_), channel_id=1, source_target_pairs={{0,16},{16,0},{1,17},{17,1},{2,18},{18,2},{3,19},{19,3},{4,20},{20... | collective-permute-start | bytes 1622024 | tf_op jit(solution)/shard_map/ppermute | solution.py:183
  86.9 18.2 %collective-permute-start.5 = (bf16[4,264,256]{2,1,0:T(8,128)(2,1)S(1)}, bf16[4,264,256]{2,1,0:T(8,128)(2,1)S(1)}, u32[]{:S(2)}, u32[]{:S(2)}) collective-permute-start(bf16[4,264,256]{2,1,0:T(8,128)(2,1)S(1)} %collective-permute-done.refs_0_), channel_id=1, source_target_pairs={{0,16},{16,0},{1,17},{17,1},{2,18},{18,2},{3,19},{19,3},{4,20},{20... | collective-permute-start | bytes 1622024 | tf_op jit(solution)/shard_map/ppermute | solution.py:183
  93.3 15.6 %collective-permute-start.4 = (bf16[4,264,256]{2,1,0:T(8,128)(2,1)S(1)}, bf16[4,264,256]{2,1,0:T(8,128)(2,1)S(1)}, u32[]{:S(2)}, u32[]{:S(2)}) collective-permute-start(bf16[4,264,256]{2,1,0:T(8,128)(2,1)S(1)} %constant_dynamic-update-slice_fusion.refs_0_), channel_id=1, source_target_pairs={{0,16},{16,0},{1,17},{17,1},{2,18},{18,2},{3,19},{19,3},{4,20},{20... | collective-permute-start | bytes 1622024 | tf_op jit(solution)/shard_map/ppermute | solution.py:183
  95.4 1.0 copy-start
  112.6 11.9 %collective-permute-start.8 = (bf16[256,512]{1,0:T(8,128)(2,1)S(1)}, bf16[256,512]{1,0:T(8,128)(2,1)S(1)}, u32[]{:S(2)}, u32[]{:S(2)}) collective-permute-start(bf16[256,512]{1,0:T(8,128)(2,1)S(1)} %shard_map.58.refs_0_), channel_id=1, source_target_pairs={{0,7},{1,2},{2,1},{3,4},{4,3},{5,6},{6,5},{7,0},{8,15},{9,10},{10,... | collective-permute-start | bytes 786440 | tf_op jit(solution)/shard_map/ppermute | solution.py:189
  114.5 11.9 %collective-permute-start.12 = (bf16[256,512]{1,0:T(8,128)(2,1)S(1)}, bf16[256,512]{1,0:T(8,128)(2,1)S(1)}, u32[]{:S(2)}, u32[]{:S(2)}) collective-permute-start(bf16[256,512]{1,0:T(8,128)(2,1)S(1)} %shard_map.58.refs_0_), channel_id=1, source_target_pairs={{0,1},{1,0},{2,3},{3,2},{4,5},{5,4},{6,7},{7,6},{8,9},{9,8},{10,11... | collective-permute-start | bytes 786440 | tf_op jit(solution)/shard_map/ppermute | solution.py:189
  124.5 10.3 %collective-permute-start.9 = (bf16[256,512]{1,0:T(8,128)(2,1)S(1)}, bf16[256,512]{1,0:T(8,128)(2,1)S(1)}, u32[]{:S(2)}, u32[]{:S(2)}) collective-permute-start(bf16[256,512]{1,0:T(8,128)(2,1)S(1)} %collective-permute-done.8.refs_2_), channel_id=1, source_target_pairs={{0,1},{1,0},{2,3},{3,2},{4,5},{5,4},{6,7},{7,6},{8,9},{9,8},{10,11... | collective-permute-start | bytes 786440 | tf_op jit(solution)/shard_map/ppermute | solution.py:189
  126.5 11.5 %collective-permute-start.13 = (bf16[256,512]{1,0:T(8,128)(2,1)S(1)}, bf16[256,512]{1,0:T(8,128)(2,1)S(1)}, u32[]{:S(2)}, u32[]{:S(2)}) collective-permute-start(bf16[256,512]{1,0:T(8,128)(2,1)S(1)} %collective-permute-done.12.refs_1_), channel_id=1, source_target_pairs={{0,7},{1,2},{2,1},{3,4},{4,3},{5,6},{6,5},{7,0},{8,15},{9,10},{10,... | collective-permute-start | bytes 786440 | tf_op jit(solution)/shard_map/ppermute | solution.py:189
  134.8 10.6 %collective-permute-start.10 = (bf16[256,512]{1,0:T(8,128)(2,1)S(1)}, bf16[256,512]{1,0:T(8,128)(2,1)S(1)}, u32[]{:S(2)}, u32[]{:S(2)}) collective-permute-start(bf16[256,512]{1,0:T(8,128)(2,1)S(1)} %collective-permute-done.9.refs_3_), channel_id=1, source_target_pairs={{0,7},{1,2},{2,1},{3,4},{4,3},{5,6},{6,5},{7,0},{8,15},{9,10},{10,... | collective-permute-start | bytes 786440 | tf_op jit(solution)/shard_map/ppermute | solution.py:189
  138.0 9.7 %collective-permute-start.14 = (bf16[256,512]{1,0:T(8,128)(2,1)S(1)}, bf16[256,512]{1,0:T(8,128)(2,1)S(1)}, u32[]{:S(2)}, u32[]{:S(2)}) collective-permute-start(bf16[256,512]{1,0:T(8,128)(2,1)S(1)} %collective-permute-done.13.refs_4_), channel_id=1, source_target_pairs={{0,1},{1,0},{2,3},{3,2},{4,5},{5,4},{6,7},{7,6},{8,9},{9,8},{10,11... | collective-permute-start | bytes 786440 | tf_op jit(solution)/shard_map/ppermute | solution.py:189
  145.5 13.2 %collective-permute-start.11 = (bf16[128,512]{1,0:T(8,128)(2,1)S(1)}, bf16[128,512]{1,0:T(8,128)(2,1)S(1)}, u32[]{:S(2)}, u32[]{:S(2)}) collective-permute-start(bf16[128,512]{1,0:T(8,128)(2,1)S(1)} %slice.18), channel_id=1, source_target_pairs={{0,1},{1,0},{2,3},{3,2},{4,5},{5,4},{6,7},{7,6},{8,9},{9,8},{10,11... | collective-permute-start | bytes 393224 | tf_op jit(solution)/shard_map/ppermute | solution.py:189
  147.7 10.9 %collective-permute-start.15 = (bf16[128,512]{1,0:T(8,128)(2,1)S(1)}, bf16[128,512]{1,0:T(8,128)(2,1)S(1)}, u32[]{:S(2)}, u32[]{:S(2)}) collective-permute-start(bf16[128,512]{1,0:T(8,128)(2,1)S(1)} %slice.19), channel_id=1, source_target_pairs={{0,7},{1,2},{2,1},{3,4},{4,3},{5,6},{6,5},{7,0},{8,15},{9,10},{10,... | collective-permute-start | bytes 393224 | tf_op jit(solution)/shard_map/ppermute | solution.py:189
Sparse Core Ops, SparseCore 0:
  9.5 107.4 all-gather.3

commit v6 on v5

--- a/solution.py
+++ b/solution.py
@@ -59,7 +59,7 @@
     ]
     for at, offset in enumerate(sources):
         own, other = pieces[2 * at], pieces[2 * at + 1]
-        their_x = lax.rem(my_x + (1 - 2 * lax.rem(my_x, 2)) * offset + X, X)
+        their_x = lax.rem(my_x + offset, X)
         firsts = [low for low, _ in extents[at]]
         lasts = [high for _, high in extents[at]]
 
@@ -319,19 +319,19 @@
     docs = jnp.broadcast_to(documents.astype(jnp.float32)[:, None], (rows, HD))
 
     mine = lax.all_gather(packed, "zl", axis=0)
-    one = pairs(mine, "x", X, False)
-    two = pairs(mine, "x", X, True)
+    left = around(mine, "x", X, 1)
+    right = around(mine, "x", X, -1)
     mine_other = around(mine, "core", CORE, 1)
-    far_two = pairs(one[ZL // 2 :], "x", X, True)
-    one_other = around(one, "core", CORE, 1)
-    far_one = pairs(two[: ZL // 2], "x", X, False)
-    two_other = around(two, "core", CORE, 1)
-    far = jnp.concatenate([far_one, far_two], axis=0)
+    far_a = around(left[: ZL // 2], "x", X, 1)
+    left_other = around(left, "core", CORE, 1)
+    far_b = around(right[ZL // 2 :], "x", X, -1)
+    right_other = around(right, "core", CORE, 1)
+    far = jnp.concatenate([far_a, far_b], axis=0)
     far_other = around(far, "core", CORE, 1)
 
     state = attend(where, queries, docs, [mine, mine_other], (0,), None, False)
-    state = attend(where, queries, docs, [one, one_other], (1,), state, False)
-    state = attend(where, queries, docs, [two, two_other], (-1,), state, False)
+    sides = [left, left_other, right, right_other]
+    state = attend(where, queries, docs, sides, (X - 1, 1), state, False)
     attended = attend(where, queries, docs, [far, far_other], (2,), state, True)
     pieces = ring_over_y(attended)
     y = lax.axis_index("y").astype(jnp.int32).reshape(1)

time: 199 us -> 205 us (1.030)
  starting transfers between devices: 72.3 us -> 76.5 us
    ppermute x4 -> x8, starting transfers between devices: 8.17 us -> 51.1 us  [around(): lax.ppermute(value, axis, [(i, (i + step) % size) for i in range(size)])]
    ppermute x12 -> x8, starting transfers between devices: 62.5 us -> 23.8 us  [pairs(): return lax.ppermute(value, axis, moves)]
    ppermute x4 -> x8, waiting for transfers between devices: 0.01 us -> 21.4 us  [around(): lax.ppermute(value, axis, [(i, (i + step) % size) for i in range(size)])]
    ppermute x12 -> x8, waiting for transfers between devices: 36 us -> 16.5 us  [pairs(): return lax.ppermute(value, axis, moves)]
    pallas_call x4 -> x3, Pallas kernels: 16.2 us -> 15.5 us  [attend(): pl.pallas_call(functools.partial(attend_kernel, sources, first, last), ou...]
  transfers between devices with their start and end apart: 18 -> 18, of which waited for: 7 -> 9; matrix products, arithmetic and copies ran while one was open for 1% -> 2% of each run, Pallas kernels for 11% -> 11%
where the time goes in v6:
time: 205 us; the launch traced here: 204 us
  starting transfers between devices  76.5 us (37%)
  blocking collectives  44.3 us (22%)
  waiting for transfers between devices  38 us (19%)
  Pallas kernels  25.5 us (12%)
  between operations  13.7 us (7%)
  local copies, waits for them, and re-layouts  5.15 us (3%)
    ppermute x8, starting transfers between devices, around(): lax.ppermute(value, axis, [(i, (i + step) % size) for i in range(size)])  51.1 us
    all_to_all x1, blocking collectives, compute(): came = lax.all_to_all(terms, TP, split_axis=0, concat_axis=0, tiled=True)  27.7 us
    ppermute x8, starting transfers between devices, pairs(): return lax.ppermute(value, axis, moves)  23.8 us
    ppermute x8, waiting for transfers between devices, around(): lax.ppermute(value, axis, [(i, (i + step) % size) for i in range(size)])  21.4 us
    all_gather x1, blocking collectives, compute(): mine = lax.all_gather(packed, 'zl', axis=0)  16.6 us
    ppermute x8, waiting for transfers between devices, pairs(): return lax.ppermute(value, axis, moves)  16.5 us
    pallas_call x3, Pallas kernels, attend(): pl.pallas_call(functools.partial(attend_kernel, sources, first, last), ou...  15.5 us
    pallas_call x2, Pallas kernels, project(): pl.pallas_call(functools.partial(project_kernel, offsets, first), out_sha...  8.1 us
  transfers between devices with their start and end apart: 18, of which 9 were waited for; matrix products, arithmetic and copies ran while one was open for 2% of the time, Pallas kernels for 11%

profile of v6, /device:TPU:192, one launch (start us, length us, event | category | flops | bytes accessed | tf_op | source)
XLA Modules:
  0.0 203.9 jit_solution(3393225019852886844)
XLA Ops:
  10.6 16.6 %all-gather = bf16[1056,256]{1,0:T(8,128)(2,1)S(1)} all-gather(bf16[264,256]{1,0:T(8,128)(2,1)S(1)} %pad_maximum_fusion), channel_id=2, replica_groups=mesh['zl'=4,'x'=4,'core'=2,'zh'=2,'y'=8] {'zl'}, dimensions={0}, use_global_device_ids=true | all-gather | bytes 675840 | tf_op jit(solution)/shard_map/all_gather | solution.py:321
  27.2 24.7 %collective-permute-start = (bf16[4,264,256]{2,1,0:T(8,128)(2,1)S(1)}, bf16[4,264,256]{2,1,0:T(8,128)(2,1)S(1)}, u32[]{:S(2)}, u32[]{:S(2)}) collective-permute-start(bf16[4,264,256]{2,1,0:T(8,128)(2,1)S(1)} %bitcast.6), channel_id=1, source_target_pairs={{0,32},{32,64},{64,96},{96,0},{1,33},{33,65},{65,97},{97,1},{2,34}... | collective-permute-start | bytes 1622024 | tf_op jit(solution)/shard_map/ppermute | solution.py:183
  51.9 3.7 %collective-permute-start.2 = (bf16[4,264,256]{2,1,0:T(8,128)(2,1)S(1)}, bf16[4,264,256]{2,1,0:T(8,128)(2,1)S(1)}, u32[]{:S(2)}, u32[]{:S(2)}) collective-permute-start(bf16[4,264,256]{2,1,0:T(8,128)(2,1)S(1)} %bitcast.7), channel_id=1, source_target_pairs={{0,96},{32,0},{64,32},{96,64},{1,97},{33,1},{65,33},{97,65},{2,98}... | collective-permute-start | bytes 1622024 | tf_op jit(solution)/shard_map/ppermute | solution.py:183
  55.7 12.8 %collective-permute-done.refs_0_ = bf16[4,264,256]{2,1,0:T(8,128)(2,1)S(1)} collective-permute-done((bf16[4,264,256]{2,1,0:T(8,128)(2,1)S(1)}, bf16[4,264,256]{2,1,0:T(8,128)(2,1)S(1)}, u32[]{:S(2)}, u32[]{:S(2)}) %collective-permute-start) | collective-permute-done | bytes 540704 | tf_op jit(solution)/shard_map/ppermute | solution.py:183
  69.2 4.5 %collective-permute-start.1 = (bf16[2,264,256]{2,1,0:T(8,128)(2,1)}, bf16[2,264,256]{2,1,0:T(8,128)(2,1)S(1)}, u32[]{:S(2)}, u32[]{:S(2)}) collective-permute-start(bf16[2,264,256]{2,1,0:T(8,128)(2,1)} %slice.16), channel_id=1, source_target_pairs={{0,32},{32,64},{64,96},{96,0},{1,33},{33,65},{65,97},{97,1},{2,34}... | collective-permute-start | bytes 811016 | tf_op jit(solution)/shard_map/ppermute | solution.py:183
  77.2 9.8 %collective-permute-start.3 = (bf16[2,264,256]{2,1,0:T(8,128)(2,1)}, bf16[2,264,256]{2,1,0:T(8,128)(2,1)}, u32[]{:S(2)}, u32[]{:S(2)}) collective-permute-start(bf16[2,264,256]{2,1,0:T(8,128)(2,1)} %slice.17), channel_id=1, source_target_pairs={{0,96},{32,0},{64,32},{96,64},{1,97},{33,1},{65,33},{97,65},{2,98}... | collective-permute-start | bytes 811016 | tf_op jit(solution)/shard_map/ppermute | solution.py:183
  87.0 2.1 %collective-permute-start.5 = (bf16[4,264,256]{2,1,0:T(8,128)(2,1)S(1)}, bf16[4,264,256]{2,1,0:T(8,128)(2,1)S(1)}, u32[]{:S(2)}, u32[]{:S(2)}) collective-permute-start(bf16[4,264,256]{2,1,0:T(8,128)(2,1)S(1)} %collective-permute-done.refs_0_), channel_id=1, source_target_pairs={{0,16},{16,0},{1,17},{17,1},{2,18},{18,2},{3,19},{19,3},{4,20},{20... | collective-permute-start | bytes 1622024 | tf_op jit(solution)/shard_map/ppermute | solution.py:183
  89.2 2.2 %collective-permute-start.6 = (bf16[4,264,256]{2,1,0:T(8,128)(2,1)S(1)}, bf16[4,264,256]{2,1,0:T(8,128)(2,1)S(1)}, u32[]{:S(2)}, u32[]{:S(2)}) collective-permute-start(bf16[4,264,256]{2,1,0:T(8,128)(2,1)S(1)} %collective-permute-done.2.refs_2_), channel_id=1, source_target_pairs={{0,16},{16,0},{1,17},{17,1},{2,18},{18,2},{3,19},{19,3},{4,20},{20... | collective-permute-start | bytes 1622024 | tf_op jit(solution)/shard_map/ppermute | solution.py:183
  91.4 7.9 %collective-permute-done.3 = bf16[2,264,256]{2,1,0:T(8,128)(2,1)} collective-permute-done((bf16[2,264,256]{2,1,0:T(8,128)(2,1)}, bf16[2,264,256]{2,1,0:T(8,128)(2,1)}, u32[]{:S(2)}, u32[]{:S(2)}) %collective-permute-start.3) | collective-permute-done | bytes 270368 | tf_op jit(solution)/shard_map/ppermute | solution.py:183
  100.3 2.0 collective-permute-start.4
  103.4 5.0 %shard_map.55 = (f32[1024,128]{1,0:T(8,128)S(1)}, f32[1024,256]{1,0:T(8,128)S(1)}) custom-call(s32[3]{0:T(128)S(1)} %pad_add_fusion.where_ref, bf16[256,512]{1,0:T(8,128)(2,1)S(1)} %copy-done, f32[256,128]{1,0:T(8,128)S(1)} %broadcast_in_dim.4.docs_ref, bf16[4,264,256]{2,1,0:T(8,128)(2,1)S(1)} %bitcast.9, bf16[4,264,256]{2,1,0:T(8,128)(2,1)S(1)} %collective-permute-done.7.refs_1_), custom_call_target="tpu_custom_call" | custom-call | flops 1610612736 | bytes 1048576 | tf_op jit(solution)/shard_map/pallas_call | solution.py:167
  108.4 6.8 %shard_map.56 = (f32[1024,128]{1,0:T(8,128)S(1)}, f32[1024,256]{1,0:T(8,128)S(1)}) custom-call(s32[3]{0:T(128)S(1)} %pad_add_fusion.where_ref, bf16[256,512]{1,0:T(8,128)(2,1)S(1)} %copy-done, f32[256,128]{1,0:T(8,128)S(1)} %broadcast_in_dim.4.docs_ref, bf16[4,264,256]{2,1,0:T(8,128)(2,1)S(1)} %collective-permute-done.refs_0_, ...), custom_call_target="tpu_custom_call" | custom-call | flops 3221225472 | bytes 2097152 | tf_op jit(solution)/shard_map/pallas_call | solution.py:167
  115.3 3.7 %shard_map.57.refs_0_ = bf16[256,512]{1,0:T(8,128)(2,1)S(1)} custom-call(s32[3]{0:T(128)S(1)} %pad_add_fusion.where_ref, bf16[256,512]{1,0:T(8,128)(2,1)S(1)} %copy-done, f32[256,128]{1,0:T(8,128)S(1)} %broadcast_in_dim.4.docs_ref, bf16[4,264,256]{2,1,0:T(8,128)(2,1)S(1)} %constant_dynamic-update-slice_fusion.refs_0_, ...), custom_call_target="tpu_custom_call" | custom-call | flops 1610612736 | bytes 1048576 | tf_op jit(solution)/shard_map/pallas_call | solution.py:167
  119.0 5.4 %collective-permute-start.8 = (bf16[256,512]{1,0:T(8,128)(2,1)S(1)}, bf16[256,512]{1,0:T(8,128)(2,1)S(1)}, u32[]{:S(2)}, u32[]{:S(2)}) collective-permute-start(bf16[256,512]{1,0:T(8,128)(2,1)S(1)} %shard_map.57.refs_0_), channel_id=1, source_target_pairs={{0,7},{1,2},{2,1},{3,4},{4,3},{5,6},{6,5},{7,0},{8,15},{9,10},{10,... | collective-permute-start | bytes 786440 | tf_op jit(solution)/shard_map/ppermute | solution.py:189
  126.3 4.6 %collective-permute-done.8.refs_2_ = bf16[256,512]{1,0:T(8,128)(2,1)S(1)} collective-permute-done((bf16[256,512]{1,0:T(8,128)(2,1)S(1)}, bf16[256,512]{1,0:T(8,128)(2,1)S(1)}, u32[]{:S(2)}, u32[]{:S(2)}) %collective-permute-start.8) | collective-permute-done | bytes 262176 | tf_op jit(solution)/shard_map/ppermute | solution.py:189
  132.8 2.6 %collective-permute-done.12.refs_1_ = bf16[256,512]{1,0:T(8,128)(2,1)S(1)} collective-permute-done((bf16[256,512]{1,0:T(8,128)(2,1)S(1)}, bf16[256,512]{1,0:T(8,128)(2,1)S(1)}, u32[]{:S(2)}, u32[]{:S(2)}) %collective-permute-start.12) | collective-permute-done | bytes 262176 | tf_op jit(solution)/shard_map/ppermute | solution.py:189
  135.4 2.9 %collective-permute-start.13 = (bf16[256,512]{1,0:T(8,128)(2,1)S(1)}, bf16[256,512]{1,0:T(8,128)(2,1)S(1)}, u32[]{:S(2)}, u32[]{:S(2)}) collective-permute-start(bf16[256,512]{1,0:T(8,128)(2,1)S(1)} %collective-permute-done.12.refs_1_), channel_id=1, source_target_pairs={{0,7},{1,2},{2,1},{3,4},{4,3},{5,6},{6,5},{7,0},{8,15},{9,10},{10,... | collective-permute-start | bytes 786440 | tf_op jit(solution)/shard_map/ppermute | solution.py:189
  138.2 3.2 %collective-permute-done.9.refs_3_ = bf16[256,512]{1,0:T(8,128)(2,1)S(1)} collective-permute-done((bf16[256,512]{1,0:T(8,128)(2,1)S(1)}, bf16[256,512]{1,0:T(8,128)(2,1)S(1)}, u32[]{:S(2)}, u32[]{:S(2)}) %collective-permute-start.9) | collective-permute-done | bytes 262176 | tf_op jit(solution)/shard_map/ppermute | solution.py:189
  141.5 5.1 %collective-permute-start.10 = (bf16[256,512]{1,0:T(8,128)(2,1)S(1)}, bf16[256,512]{1,0:T(8,128)(2,1)S(1)}, u32[]{:S(2)}, u32[]{:S(2)}) collective-permute-start(bf16[256,512]{1,0:T(8,128)(2,1)S(1)} %collective-permute-done.9.refs_3_), channel_id=1, source_target_pairs={{0,7},{1,2},{2,1},{3,4},{4,3},{5,6},{6,5},{7,0},{8,15},{9,10},{10,... | collective-permute-start | bytes 786440 | tf_op jit(solution)/shard_map/ppermute | solution.py:189
  148.7 3.7 %collective-permute-done.10.refs_6_ = bf16[256,512]{1,0:T(8,128)(2,1)S(1)} collective-permute-done((bf16[256,512]{1,0:T(8,128)(2,1)S(1)}, bf16[256,512]{1,0:T(8,128)(2,1)S(1)}, u32[]{:S(2)}, u32[]{:S(2)}) %collective-permute-start.10) | collective-permute-done | bytes 262176 | tf_op jit(solution)/shard_map/ppermute | solution.py:189
  154.4 2.2 %collective-permute-done.14.refs_5_ = bf16[256,512]{1,0:T(8,128)(2,1)S(1)} collective-permute-done((bf16[256,512]{1,0:T(8,128)(2,1)S(1)}, bf16[256,512]{1,0:T(8,128)(2,1)S(1)}, u32[]{:S(2)}, u32[]{:S(2)}) %collective-permute-start.14) | collective-permute-done | bytes 262176 | tf_op jit(solution)/shard_map/ppermute | solution.py:189
  156.6 2.8 %collective-permute-start.15 = (bf16[128,512]{1,0:T(8,128)(2,1)S(1)}, bf16[128,512]{1,0:T(8,128)(2,1)S(1)}, u32[]{:S(2)}, u32[]{:S(2)}) collective-permute-start(bf16[128,512]{1,0:T(8,128)(2,1)S(1)} %slice.19), channel_id=1, source_target_pairs={{0,7},{1,2},{2,1},{3,4},{4,3},{5,6},{6,5},{7,0},{8,15},{9,10},{10,... | collective-permute-start | bytes 393224 | tf_op jit(solution)/shard_map/ppermute | solution.py:189
  159.4 6.4 %shard_map.58.refs_3_ = f32[4,256,256]{2,1,0:T(8,128)S(1)} custom-call(s32[1]{0:T(128)} %bitcast.y_ref, bf16[256,512]{1,0:T(8,128)(2,1)S(1)} %shard_map.57.refs_0_, bf16[256,512]{1,0:T(8,128)(2,1)S(1)} %collective-permute-done.12.refs_1_, bf16[256,512]{1,0:T(8,128)(2,1)S(1)} %collective-permute-done.8.refs_2_, ...), custom_call_target="tpu_custom_call" | custom-call | flops 1879048192 | bytes 9175040 | tf_op jit(solution)/shard_map/pallas_call | solution.py:261
  167.6 27.7 %all_to_all.5.came_ref = bf16[16,16,1024]{2,1,0:T(8,128)(2,1)} all-to-all(bf16[16,16,1024]{2,1,0:T(8,128)(2,1)S(1)} %shard_map.59), channel_id=1, replica_groups=mesh['zl'=4,'x'=4,'core'=2,'zh'=2,'y'=8] {'zh','y'}, dimensions={0} | all-to-all | bytes 1048576 | tf_op jit(solution)/shard_map/all_to_all | solution.py:340
  (37 shorter events, 21.7 us)
Async XLA Ops:
  6.5 152.9 %all-gather.4.cloned.1.call-start = ((), (), s32[]{:S(2)}) async-start(), calls=%async_computation.1 | async-start | bytes 8650752 | tf_op jit(solution)/shard_map/all_gather | solution.py:309
  6.5 1.6 collective-permute-start.16
  8.1 0.7 copy-start.1
  27.2 41.3 %collective-permute-start = (bf16[4,264,256]{2,1,0:T(8,128)(2,1)S(1)}, bf16[4,264,256]{2,1,0:T(8,128)(2,1)S(1)}, u32[]{:S(2)}, u32[]{:S(2)}) collective-permute-start(bf16[4,264,256]{2,1,0:T(8,128)(2,1)S(1)} %bitcast.6), channel_id=1, source_target_pairs={{0,32},{32,64},{64,96},{96,0},{1,33},{33,65},{65,97},{97,1},{2,34}... | collective-permute-start | bytes 1622024 | tf_op jit(solution)/shard_map/ppermute | solution.py:183
  51.9 24.5 %collective-permute-start.2 = (bf16[4,264,256]{2,1,0:T(8,128)(2,1)S(1)}, bf16[4,264,256]{2,1,0:T(8,128)(2,1)S(1)}, u32[]{:S(2)}, u32[]{:S(2)}) collective-permute-start(bf16[4,264,256]{2,1,0:T(8,128)(2,1)S(1)} %bitcast.7), channel_id=1, source_target_pairs={{0,96},{32,0},{64,32},{96,64},{1,97},{33,1},{65,33},{97,65},{2,98}... | collective-permute-start | bytes 1622024 | tf_op jit(solution)/shard_map/ppermute | solution.py:183
  69.2 22.2 %collective-permute-start.1 = (bf16[2,264,256]{2,1,0:T(8,128)(2,1)}, bf16[2,264,256]{2,1,0:T(8,128)(2,1)S(1)}, u32[]{:S(2)}, u32[]{:S(2)}) collective-permute-start(bf16[2,264,256]{2,1,0:T(8,128)(2,1)} %slice.16), channel_id=1, source_target_pairs={{0,32},{32,64},{64,96},{96,0},{1,33},{33,65},{65,97},{97,1},{2,34}... | collective-permute-start | bytes 811016 | tf_op jit(solution)/shard_map/ppermute | solution.py:183
  73.8 28.6 %collective-permute-start.7 = (bf16[4,264,256]{2,1,0:T(8,128)(2,1)S(1)}, bf16[4,264,256]{2,1,0:T(8,128)(2,1)S(1)}, u32[]{:S(2)}, u32[]{:S(2)}) collective-permute-start(bf16[4,264,256]{2,1,0:T(8,128)(2,1)S(1)} %bitcast.8), channel_id=1, source_target_pairs={{0,16},{16,0},{1,17},{17,1},{2,18},{18,2},{3,19},{19,3},{4,20},{20... | collective-permute-start | bytes 1622024 | tf_op jit(solution)/shard_map/ppermute | solution.py:183
  77.2 22.1 %collective-permute-start.3 = (bf16[2,264,256]{2,1,0:T(8,128)(2,1)}, bf16[2,264,256]{2,1,0:T(8,128)(2,1)}, u32[]{:S(2)}, u32[]{:S(2)}) collective-permute-start(bf16[2,264,256]{2,1,0:T(8,128)(2,1)} %slice.17), channel_id=1, source_target_pairs={{0,96},{32,0},{64,32},{96,64},{1,97},{33,1},{65,33},{97,65},{2,98}... | collective-permute-start | bytes 811016 | tf_op jit(solution)/shard_map/ppermute | solution.py:183
  87.0 21.3 %collective-permute-start.5 = (bf16[4,264,256]{2,1,0:T(8,128)(2,1)S(1)}, bf16[4,264,256]{2,1,0:T(8,128)(2,1)S(1)}, u32[]{:S(2)}, u32[]{:S(2)}) collective-permute-start(bf16[4,264,256]{2,1,0:T(8,128)(2,1)S(1)} %collective-permute-done.refs_0_), channel_id=1, source_target_pairs={{0,16},{16,0},{1,17},{17,1},{2,18},{18,2},{3,19},{19,3},{4,20},{20... | collective-permute-start | bytes 1622024 | tf_op jit(solution)/shard_map/ppermute | solution.py:183
  89.2 19.2 %collective-permute-start.6 = (bf16[4,264,256]{2,1,0:T(8,128)(2,1)S(1)}, bf16[4,264,256]{2,1,0:T(8,128)(2,1)S(1)}, u32[]{:S(2)}, u32[]{:S(2)}) collective-permute-start(bf16[4,264,256]{2,1,0:T(8,128)(2,1)S(1)} %collective-permute-done.2.refs_2_), channel_id=1, source_target_pairs={{0,16},{16,0},{1,17},{17,1},{2,18},{18,2},{3,19},{19,3},{4,20},{20... | collective-permute-start | bytes 1622024 | tf_op jit(solution)/shard_map/ppermute | solution.py:183
  100.3 15.0 %collective-permute-start.4 = (bf16[4,264,256]{2,1,0:T(8,128)(2,1)S(1)}, bf16[4,264,256]{2,1,0:T(8,128)(2,1)S(1)}, u32[]{:S(2)}, u32[]{:S(2)}) collective-permute-start(bf16[4,264,256]{2,1,0:T(8,128)(2,1)S(1)} %constant_dynamic-update-slice_fusion.refs_0_), channel_id=1, source_target_pairs={{0,16},{16,0},{1,17},{17,1},{2,18},{18,2},{3,19},{19,3},{4,20},{20... | collective-permute-start | bytes 1622024 | tf_op jit(solution)/shard_map/ppermute | solution.py:183
  102.4 1.0 copy-start
  119.0 11.9 %collective-permute-start.8 = (bf16[256,512]{1,0:T(8,128)(2,1)S(1)}, bf16[256,512]{1,0:T(8,128)(2,1)S(1)}, u32[]{:S(2)}, u32[]{:S(2)}) collective-permute-start(bf16[256,512]{1,0:T(8,128)(2,1)S(1)} %shard_map.57.refs_0_), channel_id=1, source_target_pairs={{0,7},{1,2},{2,1},{3,4},{4,3},{5,6},{6,5},{7,0},{8,15},{9,10},{10,... | collective-permute-start | bytes 786440 | tf_op jit(solution)/shard_map/ppermute | solution.py:189
  124.4 11.0 %collective-permute-start.12 = (bf16[256,512]{1,0:T(8,128)(2,1)S(1)}, bf16[256,512]{1,0:T(8,128)(2,1)S(1)}, u32[]{:S(2)}, u32[]{:S(2)}) collective-permute-start(bf16[256,512]{1,0:T(8,128)(2,1)S(1)} %shard_map.57.refs_0_), channel_id=1, source_target_pairs={{0,1},{1,0},{2,3},{3,2},{4,5},{5,4},{6,7},{7,6},{8,9},{9,8},{10,11... | collective-permute-start | bytes 786440 | tf_op jit(solution)/shard_map/ppermute | solution.py:189
  130.9 10.6 %collective-permute-start.9 = (bf16[256,512]{1,0:T(8,128)(2,1)S(1)}, bf16[256,512]{1,0:T(8,128)(2,1)S(1)}, u32[]{:S(2)}, u32[]{:S(2)}) collective-permute-start(bf16[256,512]{1,0:T(8,128)(2,1)S(1)} %collective-permute-done.8.refs_2_), channel_id=1, source_target_pairs={{0,1},{1,0},{2,3},{3,2},{4,5},{5,4},{6,7},{7,6},{8,9},{9,8},{10,11... | collective-permute-start | bytes 786440 | tf_op jit(solution)/shard_map/ppermute | solution.py:189
  135.4 11.4 %collective-permute-start.13 = (bf16[256,512]{1,0:T(8,128)(2,1)S(1)}, bf16[256,512]{1,0:T(8,128)(2,1)S(1)}, u32[]{:S(2)}, u32[]{:S(2)}) collective-permute-start(bf16[256,512]{1,0:T(8,128)(2,1)S(1)} %collective-permute-done.12.refs_1_), channel_id=1, source_target_pairs={{0,7},{1,2},{2,1},{3,4},{4,3},{5,6},{6,5},{7,0},{8,15},{9,10},{10,... | collective-permute-start | bytes 786440 | tf_op jit(solution)/shard_map/ppermute | solution.py:189
  141.5 10.9 %collective-permute-start.10 = (bf16[256,512]{1,0:T(8,128)(2,1)S(1)}, bf16[256,512]{1,0:T(8,128)(2,1)S(1)}, u32[]{:S(2)}, u32[]{:S(2)}) collective-permute-start(bf16[256,512]{1,0:T(8,128)(2,1)S(1)} %collective-permute-done.9.refs_3_), channel_id=1, source_target_pairs={{0,7},{1,2},{2,1},{3,4},{4,3},{5,6},{6,5},{7,0},{8,15},{9,10},{10,... | collective-permute-start | bytes 786440 | tf_op jit(solution)/shard_map/ppermute | solution.py:189
  146.8 9.8 %collective-permute-start.14 = (bf16[256,512]{1,0:T(8,128)(2,1)S(1)}, bf16[256,512]{1,0:T(8,128)(2,1)S(1)}, u32[]{:S(2)}, u32[]{:S(2)}) collective-permute-start(bf16[256,512]{1,0:T(8,128)(2,1)S(1)} %collective-permute-done.13.refs_4_), channel_id=1, source_target_pairs={{0,1},{1,0},{2,3},{3,2},{4,5},{5,4},{6,7},{7,6},{8,9},{9,8},{10,11... | collective-permute-start | bytes 786440 | tf_op jit(solution)/shard_map/ppermute | solution.py:189
  152.4 13.4 %collective-permute-start.11 = (bf16[128,512]{1,0:T(8,128)(2,1)S(1)}, bf16[128,512]{1,0:T(8,128)(2,1)S(1)}, u32[]{:S(2)}, u32[]{:S(2)}) collective-permute-start(bf16[128,512]{1,0:T(8,128)(2,1)S(1)} %slice.18), channel_id=1, source_target_pairs={{0,1},{1,0},{2,3},{3,2},{4,5},{5,4},{6,7},{7,6},{8,9},{9,8},{10,11... | collective-permute-start | bytes 393224 | tf_op jit(solution)/shard_map/ppermute | solution.py:189
  156.6 9.3 %collective-permute-start.15 = (bf16[128,512]{1,0:T(8,128)(2,1)S(1)}, bf16[128,512]{1,0:T(8,128)(2,1)S(1)}, u32[]{:S(2)}, u32[]{:S(2)}) collective-permute-start(bf16[128,512]{1,0:T(8,128)(2,1)S(1)} %slice.19), channel_id=1, source_target_pairs={{0,7},{1,2},{2,1},{3,4},{4,3},{5,6},{6,5},{7,0},{8,15},{9,10},{10,... | collective-permute-start | bytes 393224 | tf_op jit(solution)/shard_map/ppermute | solution.py:189
Sparse Core Ops, SparseCore 0:
  9.5 106.4 all-gather.3
